TPU v7x, 32 devices: a whole 2x2x4 slice. The times are simulated.
32 devices in a mesh: groups: 1, seq: 32 (over z, y, x, core).
Axes of the slice: x: 2, y: 2, z: 4, core: 2. Of those that a mesh axis runs over, the one named last changes fastest.
Arguments:
- projected: bfloat16 [4096, 8192], P(('groups', 'seq')), may hold values from -6 to 6
- conv_weight: bfloat16 [4, 8192], replicated, may hold values from -3 to 3
- decay_log: float32 [32, 4096], P(None, ('groups', 'seq')), may hold values from -1 to 0, as said below
- write_strength: float32 [32, 4096], P(None, ('groups', 'seq')), may hold values from 0 to 1
- starts: int32 [4096], P(('groups', 'seq')), may hold values from 0 to 1, as said below
Outputs:
- mixer_out: bfloat16 [4096, 4096], P(('groups', 'seq'))
Inputs may be any that keep to these rules, and one draw needn't show every extreme that they name: `starts`: 1 marks the first token of an episode; the first token of the stream is always 1. `decay_log`: never positive.
All inputs are finite; a program needn't handle non-finite values.
Results may differ from a plain program's by a relative error of at most 0.009.
Values may be sent and summed in bfloat16 or wider, within the bound.
No kernel may reach another device: no remote copies, remote signals or barrier semaphores. Data moves between devices by JAX's collectives and lax.ppermute only.
A program may use at most 1 GiB of HBM per device.

v0:
```python
import functools

import jax
import jax.numpy as jnp
from jax import lax
from jax.experimental import pallas as pl
from jax.experimental.pallas import tpu as pltpu
from jax.sharding import PartitionSpec as P


HK = 16
DK = 128
HV = 32
DV = 128
KW = 4
TOK = 128
NORM_EPS = 1e-06
GROUP = 4
LOG2E = 1.4426950408889634
HIDDEN = -1e30
ROWS = GROUP * DK + 16
F32 = jnp.float32
BF16 = jnp.bfloat16


def dot(a, b):
    return jnp.dot(a, b, preferred_element_type=F32)


def halves(a):
    high = a.astype(BF16)
    return high, (a - high.astype(F32)).astype(BF16)


def params(**kw):
    return pltpu.CompilerParams(vmem_limit_bytes=20 << 20, **kw)


def whole_spec():
    return pl.BlockSpec(memory_space=pltpu.VMEM)


def smem_spec():
    return pl.BlockSpec(memory_space=pltpu.SMEM)


def in_hbm(x):
    return pltpu.with_memory_space_constraint(x, pltpu.HBM)


def prologue_kernel(decay_ref, beta_ref, starts_ref, x_ref, out_ref, tail_ref):
    rows = x_ref.shape[0]
    flags = starts_ref[...].astype(F32)
    last = 1.0 - flags[:, TOK - 1 : TOK]
    keep = [last * (1.0 - flags[:, TOK - 2 : TOK - 1]), last, jnp.ones((1, 1), F32)]
    for r in range(KW - 1):
        row = x_ref[rows - KW + 1 + r : rows - KW + 2 + r, :].astype(F32)
        tail_ref[r : r + 1, :] = (row * keep[r]).astype(BF16)
    src = lax.broadcasted_iota(jnp.int32, (TOK, TOK), 0)
    dst = lax.broadcasted_iota(jnp.int32, (TOK, TOK), 1)
    upto = (src <= dst).astype(F32)
    cum = LOG2E * jnp.dot(
        decay_ref[...], upto, precision=lax.Precision.HIGHEST, preferred_element_type=F32
    )
    flags = jnp.broadcast_to(flags, (8, TOK)).astype(BF16)
    episode = [dot(flags, (src + j <= dst).astype(BF16))[0:1] for j in range(KW)]
    usable = [(episode[0] == episode[j]).astype(F32) for j in range(1, KW)]
    living = (episode[0] == 0.0).astype(F32)
    zero = jnp.zeros((1, TOK), F32)
    shared = jnp.concatenate(usable + [episode[0], living, zero, zero, zero], axis=0)
    for pair in range(HV // GROUP):
        out_ref[pair, 0:4, :] = cum[GROUP * pair : GROUP * (pair + 1)]
        out_ref[pair, 4:8, :] = beta_ref[GROUP * pair : GROUP * (pair + 1), :]
        out_ref[pair, 8:16, :] = shared


def prologue(decay_log, write_strength, starts, projected):
    channels = projected.shape[1]
    last = projected.shape[0] // 16 - 1
    return pl.pallas_call(
        prologue_kernel,
        grid=(1,),
        in_specs=[
            pl.BlockSpec((HV, TOK), lambda i: (0, 0)),
            pl.BlockSpec((HV, TOK), lambda i: (0, 0)),
            pl.BlockSpec((1, TOK), lambda i: (0, 0)),
            pl.BlockSpec((16, channels), lambda i: (last, 0)),
        ],
        out_specs=[
            pl.BlockSpec((HV // GROUP, 16, TOK), lambda i: (0, 0, 0)),
            pl.BlockSpec((KW - 1, channels), lambda i: (0, 0)),
        ],
        out_shape=[
            jax.ShapeDtypeStruct((HV // GROUP, 16, TOK), F32),
            jax.ShapeDtypeStruct((KW - 1, channels), BF16),
        ],
        compiler_params=params(),
        cost_estimate=pl.CostEstimate(flops=10**7, bytes_accessed=10**6, transcendentals=0),
        name="prologue",
    )(
        in_hbm(decay_log),
        in_hbm(write_strength),
        in_hbm(starts.reshape(1, TOK)),
        in_hbm(projected),
    )


def place_window(x, halo, xs, first):
    cols = slice(first, first + x.shape[1])
    xs[8 : 8 + TOK, cols] = x.astype(F32)
    xs[8 - KW + 1 : 8, cols] = halo.astype(F32)


def convolve_piece(xs, first, taps, usable):
    here = slice(first, first + 128)
    total = xs[8 : 8 + TOK, here] * taps[3:4]
    for j in range(1, KW):
        total = total + (xs[8 - j : 8 - j + TOK, here] * usable[j - 1]) * taps[3 - j : 4 - j]
    return (total / (1.0 + jnp.exp2(total * -LOG2E))).astype(BF16)


def column(cols, lane):
    return jnp.broadcast_to(cols[:, lane : lane + 1], (TOK, 128))


def positions():
    i = lax.broadcasted_iota(jnp.int32, (TOK, TOK), 0)
    j = lax.broadcasted_iota(jnp.int32, (TOK, TOK), 1)
    return i, j


def hidden_where(rows, cols):
    i, j = positions()
    seen = (column(cols, 11) == rows[11:12, :]) & (i >= j)
    return jnp.where(seen, 0.0, HIDDEN)


def decay_within(rows, clock, head, hidden):
    return jnp.exp2((clock - rows[head : head + 1, :]) + hidden)


def unit(x, scale=1.0):
    return lax.rsqrt(jnp.sum(x * x, axis=-1, keepdims=True) + NORM_EPS) * scale


def split_rows(x):
    pieces, rest = [], list(x)
    for _ in range(3):
        highs = [c.astype(BF16).astype(F32) for c in rest]
        pieces += highs
        rest = [c - high for c, high in zip(rest, highs)]
    pieces.append(jnp.zeros((4, 256), F32))
    return jnp.concatenate(pieces, axis=0).astype(BF16)


LEVELS = 7
HEADS = 8


def odd_rows(get, size):
    return jnp.concatenate([get(r, r + size) for r in range(size, TOK, 2 * size)], axis=0)


def stage_kernel(tab_ref, x_hbm, w_hbm, x_out, w_out, masks, shared, sems):
    copies = [
        pltpu.make_async_copy(x_hbm, x_out, sems.at[0]),
        pltpu.make_async_copy(w_hbm, w_out, sems.at[1]),
    ]
    for copy in copies:
        copy.start()
    rows = tab_ref[0]
    cols = jnp.transpose(rows)
    for j in range(KW - 1):
        shared[j] = column(cols, 8 + j)
    shared[3] = column(cols, 12)
    shared[4] = hidden_where(rows, cols)
    i, j = positions()
    apart = i ^ j
    for level in range(LEVELS):
        masks[level] = (((apart >> level) == 1) & (i > j)).astype(F32).astype(BF16)
    shared[5] = (i > j).astype(F32)
    masks[LEVELS] = (i == j).astype(F32).astype(BF16)
    for copy in copies:
        copy.wait()


def stage(tables, projected, conv_weight):
    return pl.pallas_call(
        stage_kernel,
        in_specs=[whole_spec()] + [pl.BlockSpec(memory_space=pl.ANY)] * 2,
        out_specs=[whole_spec()] * 4,
        out_shape=[
            jax.ShapeDtypeStruct(projected.shape, BF16),
            jax.ShapeDtypeStruct(conv_weight.shape, BF16),
            jax.ShapeDtypeStruct((LEVELS + 1, TOK, TOK), BF16),
            jax.ShapeDtypeStruct((6, TOK, 128), F32),
        ],
        scratch_shapes=[pltpu.SemaphoreType.DMA((2,))],
        compiler_params=params(),
        cost_estimate=pl.CostEstimate(flops=10**6, bytes_accessed=4 * 2**20, transcendentals=0),
        name="stage",
    )(tables, in_hbm(projected), in_hbm(conv_weight))


def preparing(pair, ins, xs, sys, right, keys):
    x_ref, halo_ref, w_ref, tab_ref, _, shared = ins
    k_at = pl.multiple_of(HK * DK + pair * 256, 512)
    v_at = pl.multiple_of(2 * HK * DK + pair * 512, 1024)
    kt_ref, kt_at = keys

    def usable():
        return [shared[j] for j in range(KW - 1)]

    def place():
        place_window(x_ref[:, pl.ds(k_at, 512)], halo_ref[:, pl.ds(k_at, 512)], xs, 0)
        place_window(x_ref[:, pl.ds(v_at, 1024)], halo_ref[:, pl.ds(v_at, 1024)], xs, 512)

    def key(n):
        p, a = n // 2, n % 2
        rows = tab_ref[pair + p]
        cols = jnp.transpose(rows)
        at = n * DK
        taps = w_ref[:, pl.ds(k_at + at, DK)].astype(F32)
        k = convolve_piece(xs, at, taps, usable()).astype(F32)
        k = k * unit(k)
        kb = k.astype(BF16)
        ktb = jnp.transpose(kb.astype(F32)).astype(BF16)
        kt_ref[kt_at + p, a * DK : (a + 1) * DK, :] = ktb
        inner = dot(kb, ktb) * shared[5]
        for b in range(2):
            lane = 2 * a + b
            h = GROUP * p + lane
            clock = column(cols, lane)
            within = decay_within(rows, clock, lane, shared[4])
            carried = jnp.exp2(clock) * shared[3]
            high, low = halves((column(cols, 4 + lane) * within) * inner)
            sys[h, :, 0:128] = high
            sys[h, :, 128:256] = low
            right[h, :, 0:DK] = (carried * k).astype(BF16)

    def value(h):
        taps = w_ref[:, pl.ds(v_at + h * DV, DV)].astype(F32)
        right[h, :, DK : DK + DV] = convolve_piece(xs, 512 + h * DV, taps, usable())

    steps = [place]
    steps += [functools.partial(key, n) for n in range(4)]
    steps += [functools.partial(value, h) for h in range(HEADS)]
    return steps


def solving(pair, ins, sys, right, keys, inv, pay_ref, ef_ref, at, kt_copy=None):
    tab_ref, masks, shared = ins[3:]
    kt_ref, kt_at = keys
    kept = {}

    def begin():
        for h in range(HEADS):
            inv[h] = masks[LEVELS] - sys[h, :, 0:128] * masks[0]

    def first_product(level):
        size = 1 << level
        kept["steps"] = []
        for h in range(HEADS):
            if size < 16:
                left = sys[h, :, 0:128]
            else:
                left = odd_rows(lambda r, e: sys[h, r:e, 0:128], size)
            kept["steps"].append(dot(left, inv[h]).astype(BF16))

    def second_product(level):
        size = 1 << level
        steps = kept["steps"]
        if size < 16:
            steps = [dot(inv[h], steps[h]).astype(BF16) for h in range(HEADS)]
            for h in range(HEADS):
                inv[h] = inv[h] - steps[h] * masks[level]
            return
        blank = jnp.zeros((size, 128), BF16)
        found = []
        for h in range(HEADS):
            expanded = []
            for r in range(0, TOK // 2, size):
                expanded += [blank, steps[h][r : r + size]]
            left = odd_rows(lambda r, e: inv[h, r:e, :], size)
            found.append(dot(left, jnp.concatenate(expanded, axis=0)).astype(BF16))
        for h in range(HEADS):
            for n, r in enumerate(range(size, TOK, 2 * size)):
                inv[h, r : r + size, :] = inv[h, r : r + size, :] - (
                    found[h][n * size : (n + 1) * size] * masks[level, r : r + size, :]
                )

    def check():
        kept["gaps"] = []
        for h in range(HEADS):
            rough = inv[h]
            product = dot(sys[h], jnp.concatenate([rough, rough], axis=0))
            kept["gaps"].append(
                ((masks[LEVELS].astype(F32) - rough.astype(F32)) - product).astype(BF16)
            )

    def row(h, n):
        return tab_ref[pair + h // GROUP, n : n + 1, :]

    def correct():
        for h in range(HEADS):
            fixed = inv[h].astype(F32) + dot(inv[h], kept["gaps"][h])
            inv[h] = (fixed * row(h, 4 + h % GROUP)).astype(BF16)

    def apply():
        kept["ef"] = []
        for h in range(HEADS):
            ef = dot(inv[h], right[h]).astype(BF16)
            here = slice((h % GROUP) * TOK, (h % GROUP + 1) * TOK)
            ef_ref[at + h // GROUP, here, :] = ef
            kept["ef"].append(ef)

    def write():
        last = []
        for h in range(HEADS):
            g, n = h // GROUP, h % GROUP
            ktb = kt_ref[kt_at + g, (n // 2) * DK : (n // 2 + 1) * DK, :]
            if kt_copy is not None and n % 2 == 0:
                kt_copy[at + g, (n // 2) * DK : (n // 2 + 1) * DK, :] = ktb
            clock = row(h, n)
            final = jnp.broadcast_to(clock[:, TOK - 1 : TOK], (1, TOK))
            ending = jnp.exp2((final - clock) + shared[4, TOK - 1 : TOK, :])
            carried = jnp.exp2(final) * shared[3, TOK - 1 : TOK, :]
            last.append(jnp.concatenate([carried, carried], axis=1))
            weighted = (ktb.astype(F32) * ending).astype(BF16)
            pay_ref[at + g, n * DK : (n + 1) * DK, :] = dot(weighted, kept["ef"][h]).astype(BF16)
        for g in range(2):
            pay_ref[at + g, GROUP * DK : ROWS, :] = split_rows(last[GROUP * g : GROUP * (g + 1)])

    steps = [begin]
    for level in range(1, LEVELS):
        steps.append(functools.partial(first_product, level))
        steps.append(functools.partial(second_product, level))
    return steps + [check, correct, apply, write]


def interleave(main, side):
    done = 0
    for n, step in enumerate(main):
        step()
        due = ((n + 1) * len(side) + len(main) - 1) // len(main)
        while done < min(due, len(side)):
            side[done]()
            done += 1


def send_kernel(
    meta, x_ref, halo_ref, w_ref, tab_ref, masks, shared, pay_ref, kt_ref, ef_ref, sys_out,
    right_out, kt_out, xs, sys, right, inv,
):
    ins = (x_ref, halo_ref, w_ref, tab_ref, masks, shared)
    pair, after = meta[0], meta[1]
    sets = [(sys.at[n], right.at[n], (kt_ref, 2 * n)) for n in range(2)]
    third = (sys_out, right_out, (kt_out, 0))
    for step in preparing(pair, ins, xs, *sets[0]):
        step()
    for n in range(2):
        main = solving(pair + 2 * n, ins, *sets[n], inv, pay_ref, ef_ref, 2 * n)
        if n == 0:
            side = preparing(pair + 2, ins, xs, *sets[1])
        else:
            side = preparing(after, ins, xs, *third)
        interleave(main, side)


def keep_kernel(
    meta, x_ref, halo_ref, w_ref, tab_ref, masks, shared, sys_in, right_in, kt_in, pay_ref,
    kt_ref, ef_ref, xs, sys, right, inv,
):
    ins = (x_ref, halo_ref, w_ref, tab_ref, masks, shared)
    pair = meta[1]
    own = (sys, right, (kt_ref, 2))
    interleave(
        solving(pair, ins, sys_in, right_in, (kt_in, 0), inv, pay_ref, ef_ref, 0, kt_ref),
        preparing(pair + 2, ins, xs, *own),
    )
    for step in solving(pair + 2, ins, *own, inv, pay_ref, ef_ref, 2):
        step()


def map_shapes():
    return [
        jax.ShapeDtypeStruct((4, ROWS, 256), BF16),
        jax.ShapeDtypeStruct((4, 2 * DK, TOK), BF16),
        jax.ShapeDtypeStruct((4, GROUP * TOK, 256), BF16),
    ]


def ready_shapes():
    return [
        jax.ShapeDtypeStruct((HEADS, TOK, 256), BF16),
        jax.ShapeDtypeStruct((HEADS, TOK, 256), BF16),
        jax.ShapeDtypeStruct((2, 2 * DK, TOK), BF16),
    ]


def map_cost():
    return pl.CostEstimate(
        flops=16 * 20 * 2 * 128**3, bytes_accessed=5 * 2**20, transcendentals=10**6
    )


def send_maps(meta, *ins):
    return pl.pallas_call(
        send_kernel,
        in_specs=[smem_spec()] + [whole_spec()] * len(ins),
        out_specs=[whole_spec()] * 6,
        out_shape=map_shapes() + ready_shapes(),
        scratch_shapes=[
            pltpu.VMEM((8 + TOK, 1536), F32),
            pltpu.VMEM((2, HEADS, TOK, 256), BF16),
            pltpu.VMEM((2, HEADS, TOK, 256), BF16),
            pltpu.VMEM((HEADS, TOK, TOK), BF16),
        ],
        compiler_params=params(),
        cost_estimate=map_cost(),
        name="send_maps",
    )(meta, *ins)


def keep_maps(meta, *ins):
    return pl.pallas_call(
        keep_kernel,
        in_specs=[smem_spec()] + [whole_spec()] * len(ins),
        out_specs=[whole_spec()] * 3,
        out_shape=map_shapes(),
        scratch_shapes=[
            pltpu.VMEM((8 + TOK, 1536), F32),
            pltpu.VMEM((HEADS, TOK, 256), BF16),
            pltpu.VMEM((HEADS, TOK, 256), BF16),
            pltpu.VMEM((HEADS, TOK, TOK), BF16),
        ],
        compiler_params=params(),
        cost_estimate=map_cost(),
        name="keep_maps",
    )(meta, *ins)


def read_kernel(meta, xq_ref, hq_ref, wq_ref, rows_ref, kt_ref, ef_ref, left_ref, r_ref, d_ref, xs):
    first = meta[2] == 0
    tail = left_ref[0, GROUP * DK : ROWS, :]
    rows = rows_ref[0]
    cols = jnp.transpose(rows)
    usable = [column(cols, 8 + j) for j in range(KW - 1)]
    living = column(cols, 12)
    hidden = hidden_where(rows, cols)
    place_window(xq_ref[...], hq_ref[...], xs, 0)
    taps = wq_ref[...].astype(F32)
    for a in range(2):
        queries = convolve_piece(xs, a * DK, taps[:, a * DK : (a + 1) * DK], usable)
        q = queries.astype(F32)
        scale = unit(q, DK ** (-0.5))
        inner = dot(queries, kt_ref[0, a * DK : (a + 1) * DK, :])
        for b in range(2):
            h = 2 * a + b
            clock = column(cols, h)
            scores = (inner * decay_within(rows, clock, h, hidden)).astype(BF16)
            both = dot(scores, ef_ref[0, h * TOK : (h + 1) * TOK, :])
            carried = jnp.exp2(clock) * living
            mine = slice(h * TOK, (h + 1) * TOK)
            reader = (carried * q - both[:, :DK]) * scale
            direct = both[:, DK:] * scale
            moved = dot(reader.astype(BF16), left_ref[0, h * DK : (h + 1) * DK, :])
            c = factor(tail, h)[:, :DK]
            r_ref[0, mine, :] = jnp.where(first, reader, c * reader - moved[:, :DK]).astype(BF16)
            d_ref[0, mine, :] = jnp.where(first, direct, direct + moved[:, DK:])


def make_reads(meta, slot, projected, halo, conv_weight, tables, keys_t, ef, left):
    def at(i, m):
        return (0, m[slot] + i)

    return pl.pallas_call(
        read_kernel,
        grid_spec=pltpu.PrefetchScalarGridSpec(
            num_scalar_prefetch=1,
            grid=(4,),
            in_specs=[
                pl.BlockSpec((TOK, 256), at),
                pl.BlockSpec((KW - 1, 256), at),
                pl.BlockSpec((KW, 256), at),
                pl.BlockSpec((1, 16, TOK), lambda i, m: (m[slot] + i, 0, 0)),
                pl.BlockSpec((1, 2 * DK, TOK), lambda i, m: (i, 0, 0)),
                pl.BlockSpec((1, GROUP * TOK, 256), lambda i, m: (i, 0, 0)),
                pl.BlockSpec((1, ROWS, 256), lambda i, m: (i, 0, 0)),
            ],
            out_specs=[
                pl.BlockSpec((1, GROUP * TOK, DK), lambda i, m: (i, 0, 0)),
                pl.BlockSpec((1, GROUP * TOK, DV), lambda i, m: (i, 0, 0)),
            ],
            scratch_shapes=[pltpu.VMEM((8 + TOK, 256), F32)],
        ),
        out_shape=[
            jax.ShapeDtypeStruct((4, GROUP * TOK, DK), BF16),
            jax.ShapeDtypeStruct((4, GROUP * TOK, DV), F32),
        ],
        compiler_params=params(),
        cost_estimate=pl.CostEstimate(
            flops=16 * 6 * 2 * 128**3, bytes_accessed=5 * 2**20, transcendentals=10**6
        ),
        name="reads",
    )(meta, projected, halo, conv_weight, tables, keys_t, ef, left)


def factor(tail, head):
    tail = tail.astype(F32)
    return (tail[head : head + 1] + tail[4 + head : 5 + head]) + tail[8 + head : 9 + head]


def compose(left, left_c, right, right_c):
    right_d = right[:, :DK]
    product = dot(right_d.astype(BF16), left.astype(BF16))
    return (
        right_c * left.astype(F32)
        + jnp.concatenate(
            [left_c[:, :DK] * right_d.astype(F32), right[:, DK:].astype(F32)], axis=1
        )
        - product
    )


def apply_map(each, c, state):
    product = dot(each[:, :DK], state)
    return c[:, :DK] * state.astype(F32) + each[:, DK:].astype(F32) - product


def pair_kernel(meta, mine_ref, other_ref, *out_refs):
    first = meta[2] == 0
    for m, out_ref in enumerate(out_refs):
        g = meta[3] ^ m
        tail_m, tail_o = mine_ref[g, GROUP * DK : ROWS, :], other_ref[g, GROUP * DK : ROWS, :]
        tail_l, tail_r = jnp.where(first, tail_m, tail_o), jnp.where(first, tail_o, tail_m)
        factors = []
        for h in range(GROUP):
            here = slice(h * DK, (h + 1) * DK)
            own, other = mine_ref[g, here, :], other_ref[g, here, :]
            left, right = jnp.where(first, own, other), jnp.where(first, other, own)
            left_c, right_c = factor(tail_l, h), factor(tail_r, h)
            out_ref[here, :] = compose(left, left_c, right, right_c).astype(BF16)
            factors.append(left_c * right_c)
        out_ref[GROUP * DK : ROWS, :] = split_rows(factors)


def pair_maps(meta, mine, other):
    return pl.pallas_call(
        pair_kernel,
        in_specs=[smem_spec(), whole_spec(), whole_spec()],
        out_specs=[whole_spec()] * 4,
        out_shape=[jax.ShapeDtypeStruct((ROWS, 256), BF16)] * 4,
        compiler_params=params(),
        cost_estimate=pl.CostEstimate(
            flops=16 * 2 * 2 * 128**3, bytes_accessed=3 * 2**20, transcendentals=0
        ),
        name="pair",
    )(meta, mine, other)


def plane_kernel(meta, x0, x1, x2, x3, prefix_ref, plane_ref, exit_ref, maps, sems):
    copies = []
    for m, x in enumerate((x0, x1, x2, x3)):
        copy = pltpu.make_async_copy(x, maps.at[meta[3] ^ m], sems.at[m])
        copy.start()
        copies.append(copy)
    prefix_ref[0, 0 : GROUP * DK, :] = jnp.zeros((GROUP * DK, 256), BF16)
    ones = jnp.ones((1, 256), F32)
    prefix_ref[0, GROUP * DK : ROWS, :] = split_rows([ones] * GROUP)
    for copy in copies:
        copy.wait()
    prefix_ref[1] = maps[0]
    run = [maps[0, h * DK : (h + 1) * DK, :].astype(F32) for h in range(GROUP)]
    run_c = [factor(maps[0, GROUP * DK : ROWS, :], h) for h in range(GROUP)]
    for a in range(1, 4):
        tail = maps[a, GROUP * DK : ROWS, :]
        for h in range(GROUP):
            here = slice(h * DK, (h + 1) * DK)
            c = factor(tail, h)
            run[h] = compose(run[h], run_c[h], maps[a, here, :], c)
            run_c[h] = run_c[h] * c
            if a < 3:
                prefix_ref[a + 1, here, :] = run[h].astype(BF16)
            else:
                plane_ref[here, :] = run[h].astype(BF16)
                exit_ref[here, :] = run[h][:, DK:].astype(BF16)
        if a < 3:
            prefix_ref[a + 1, GROUP * DK : ROWS, :] = split_rows(run_c)
    plane_ref[GROUP * DK : ROWS, :] = split_rows(run_c)


def plane_maps(meta, pieces):
    return pl.pallas_call(
        plane_kernel,
        in_specs=[smem_spec()] + [pl.BlockSpec(memory_space=pl.ANY)] * 4,
        out_specs=[whole_spec()] * 3,
        out_shape=[
            jax.ShapeDtypeStruct((4, ROWS, 256), BF16),
            jax.ShapeDtypeStruct((ROWS, 256), BF16),
            jax.ShapeDtypeStruct((GROUP * DK, DV), BF16),
        ],
        scratch_shapes=[pltpu.VMEM((4, ROWS, 256), BF16), pltpu.SemaphoreType.DMA((4,))],
        compiler_params=params(),
        cost_estimate=pl.CostEstimate(
            flops=12 * 2 * 2 * 128**3, bytes_accessed=2 * 2**20, transcendentals=0
        ),
        name="plane",
    )(meta, *pieces)


def hop_kernel(plane_ref, state_ref, out_ref):
    tail = plane_ref[GROUP * DK : ROWS, :]
    for h in range(GROUP):
        here = slice(h * DK, (h + 1) * DK)
        state = apply_map(plane_ref[here, :], factor(tail, h), state_ref[here, :])
        out_ref[here, :] = state.astype(BF16)


def hop(plane_map, state):
    return pl.pallas_call(
        hop_kernel,
        in_specs=[whole_spec()] * 2,
        out_specs=whole_spec(),
        out_shape=jax.ShapeDtypeStruct((GROUP * DK, DV), BF16),
        compiler_params=params(),
        cost_estimate=pl.CostEstimate(
            flops=4 * 2 * 128**3, bytes_accessed=2**19, transcendentals=0
        ),
        name="hop",
    )(plane_map, state)


def spread_kernel(meta, prefix_ref, before_ref, far_ref, *refs):
    out_refs = refs[-4:]
    state_refs = refs[:-4]
    before_tail = before_ref[GROUP * DK : ROWS, :]
    for h in range(GROUP):
        here = slice(h * DK, (h + 1) * DK)
        state = apply_map(before_ref[here, :], factor(before_tail, h), far_ref[here, :])
        state = state.astype(BF16)
        for ref in state_refs:
            state = state + ref[here, :]
        for m, out_ref in enumerate(out_refs):
            a = meta[3] ^ m
            c = factor(prefix_ref[a, GROUP * DK : ROWS, :], h)
            out_ref[here, :] = apply_map(prefix_ref[a, here, :], c, state).astype(BF16)


def spread(meta, prefix, before, far, states):
    return pl.pallas_call(
        spread_kernel,
        in_specs=[smem_spec()] + [whole_spec()] * (3 + len(states)),
        out_specs=[whole_spec()] * 4,
        out_shape=[jax.ShapeDtypeStruct((GROUP * DK, DV), BF16)] * 4,
        compiler_params=params(),
        cost_estimate=pl.CostEstimate(
            flops=20 * 2 * 128**3, bytes_accessed=2**21, transcendentals=0
        ),
        name="spread",
    )(meta, prefix, before, far, *states)


def entering_states(plane_map, leaving, planes):
    def ahead(block, plane, distance=1):
        members = range(8 * plane, 8 * plane + 8)
        return lax.ppermute(block, "seq", [(i, i + 8 * distance) for i in members])

    if planes == 4:
        first = ahead(leaving, 0)
        before = ahead(plane_map, 2)
        second = hop(plane_map, first)
        far = ahead(second, 1, 2)
        near = ahead(second, 1)
        return before, far, [first, near]
    states = []
    for plane in range(planes - 1):
        state = ahead(leaving, plane)
        states.append(state)
        if plane < planes - 2:
            leaving = hop(plane_map, state)
    return jnp.zeros_like(plane_map), jnp.zeros_like(leaving), states


def read_out(meta, r_ref, d_ref, e_refs, rows):
    for m, e_ref in enumerate(e_refs):
        g = meta[3] ^ m
        for h in range(GROUP):
            here = slice(h * TOK, (h + 1) * TOK)
            total = dot(r_ref[g, here, :], e_ref[here, :]) + d_ref[g, here, :]
            rows[g, :, h * DV : (h + 1) * DV] = total.astype(BF16)
        yield m, g


def half_kernel(meta, r_ref, d_ref, e0, e1, e2, e3, rows):
    for _ in read_out(meta, r_ref, d_ref, (e0, e1, e2, e3), rows):
        pass


def read_half(meta, reads, direct, states):
    return pl.pallas_call(
        half_kernel,
        in_specs=[smem_spec()] + [whole_spec()] * 6,
        out_specs=whole_spec(),
        out_shape=jax.ShapeDtypeStruct((4, TOK, GROUP * DV), BF16),
        compiler_params=params(),
        cost_estimate=pl.CostEstimate(
            flops=16 * 2 * 128**3, bytes_accessed=3 * 2**20, transcendentals=0
        ),
        name="half",
    )(meta, reads, direct, *states)


def emit_kernel(meta, kept, r_ref, d_ref, e0, e1, e2, e3, out_ref, rows, sems):
    copies = []

    def put(source, n, slot, g):
        start = pl.multiple_of((meta[slot] + g) * (GROUP * DV), GROUP * DV)
        copy = pltpu.make_async_copy(
            source.at[g], out_ref.at[:, pl.ds(start, GROUP * DV)], sems.at[n]
        )
        copy.start()
        copies.append(copy)

    for g in range(4):
        put(kept, g, 1, g)
    for m, g in read_out(meta, r_ref, d_ref, (e0, e1, e2, e3), rows):
        put(rows, 4 + m, 0, g)
    for copy in copies:
        copy.wait()


def emit(meta, kept, reads, direct, states):
    return pl.pallas_call(
        emit_kernel,
        in_specs=[smem_spec()] + [whole_spec()] * 7,
        out_specs=pl.BlockSpec(memory_space=pl.ANY),
        out_shape=jax.ShapeDtypeStruct((TOK, HV * DV), BF16),
        scratch_shapes=[
            pltpu.VMEM((4, TOK, GROUP * DV), BF16),
            pltpu.SemaphoreType.DMA((8,)),
        ],
        compiler_params=params(),
        cost_estimate=pl.CostEstimate(
            flops=16 * 2 * 128**3, bytes_accessed=3 * 2**20, transcendentals=0
        ),
        name="emit",
    )(meta, kept, reads, direct, *states)


def shards(projected, conv_weight, decay_log, write_strength, starts):
    count = lax.axis_size("seq")
    me = lax.axis_index("seq")
    core, place = me & 1, (me >> 1) & 3
    slots = lax.iota(jnp.int32, 8)
    meta = jnp.zeros((8,), jnp.int32)
    for slot, value in enumerate((4 * (1 - core), 4 * core, core, place, me >> 3)):
        meta = jnp.where(slots == slot, value, meta)

    def exchange(block, bits):
        return lax.ppermute(block, "seq", [(i, i ^ bits) for i in range(count)])

    tables, tail_rows = prologue(decay_log, write_strength, starts, projected)
    halo = lax.ppermute(tail_rows, "seq", [(i, i + 1) for i in range(count - 1)])
    projected, conv_weight, masks, shared = stage(tables, projected, conv_weight)
    ins = (projected, halo, conv_weight, tables, masks, shared)

    pay_s, kt_s, ef_s, *ready = send_maps(meta, *ins)
    other = exchange(pay_s, 1)
    mine, kt_k, ef_k = keep_maps(meta, *ins, *ready)
    x0, x1, x2, x3 = pair_maps(meta, mine, other)
    x3, x1, x2 = exchange(x3, 6), exchange(x1, 2), exchange(x2, 4)
    x0, own = lax.optimization_barrier((x0, mine))
    left = exchange(own, 1)
    r_k, d_k = make_reads(meta, 1, projected, halo, conv_weight, tables, kt_k, ef_k, other)
    r_s, d_s = make_reads(meta, 0, projected, halo, conv_weight, tables, kt_s, ef_s, left)
    x0, r_k, d_k, r_s, d_s = lax.optimization_barrier((x0, r_k, d_k, r_s, d_s))
    prefix, plane_map, leaving = plane_maps(meta, (x0, x1, x2, x3))
    before, far, arrived = entering_states(plane_map, leaving, count // 8)
    e0, e1, e2, e3 = spread(meta, prefix, before, far, arrived)
    e3, e1, e2 = exchange(e3, 6), exchange(e1, 2), exchange(e2, 4)
    states = (e0, e1, e2, e3)
    partner = [exchange(e, 1) for e in states]
    kept = read_half(meta, r_k, d_k, states)
    return emit(meta, kept, r_s, d_s, partner)


def solution(mesh):
    in_specs = (
        P(("groups", "seq"), None),
        P(),
        P(None, ("groups", "seq")),
        P(None, ("groups", "seq")),
        P(("groups", "seq")),
    )
    out_specs = P(("groups", "seq"), None)

    return jax.shard_map(shards, mesh=mesh, in_specs=in_specs, out_specs=out_specs, check_vma=False)
```

profile of v0, /device:TPU:25, one launch (start us, length us, event | category | flops | bytes accessed | tf_op | source)
XLA Modules:
  0.0 67.2 jit_solution(9248154479636117555)
XLA Ops:
  0.0 1.2 %prologue.1 = (f32[8,16,128]{2,1,0:T(8,128)S(1)}, bf16[3,8192]{1,0:T(4,128)(2,1)S(1)}) custom-call(f32[32,128]{1,0:T(8,128)} %decay_ref.1, f32[32,128]{1,0:T(8,128)} %beta_ref.1, s32[1,128]{1,0:T(1,128)} %bitcast.1, bf16[128,8192]{1,0:T(8,128)(2,1)} %x_hbm.1), custom_call_target="tpu_custom_call" | custom-call | flops 10000000 | bytes 1000000 | tf_op jit(solution)/shard_map/prologue/pallas_call | solution.py:80
  1.2 3.7 %collective-permute-start = (bf16[3,8192]{1,0:T(4,128)(2,1)S(1)}, bf16[3,8192]{1,0:T(4,128)(2,1)S(1)}, u32[]{:S(2)}, u32[]{:S(2)}) collective-permute-start(bf16[3,8192]{1,0:T(4,128)(2,1)S(1)} %get-tuple-element.44), channel_id=1, source_target_pairs={{0,1},{1,2},{2,3},{3,4},{4,5},{5,6},{6,7},{7,8},{8,9},{9,10},{10,1... | collective-permute-start | bytes 147464 | tf_op jit(solution)/shard_map/ppermute | solution.py:764
  5.0 1.6 %stage.1 = (bf16[128,8192]{1,0:T(8,128)(2,1)S(1)}, bf16[4,8192]{1,0:T(4,128)(2,1)S(1)}, bf16[8,128,128]{2,1,0:T(8,128)(2,1)S(1)}, f32[6,128,128]{2,1,0:T(8,128)S(1)}) custom-call(f32[8,16,128]{2,1,0:T(8,128)S(1)} %get-tuple-element.42.tab_ref.rows_ref, bf16[128,8192]{1,0:T(8,128)(2,1)} %x_hbm.1, bf16[4,8192]{1,0:T(4,128)(2,1)} %w_hbm.1), custom_call_target="tpu_custom_call" | custom-call | flops 1000000 | bytes 4194304 | tf_op jit(solution)/shard_map/stage/pallas_call | solution.py:188
  6.6 0.0 collective-permute-done.halo_ref.hq_ref
  6.6 7.8 %send_maps.1 = (bf16[4,528,256]{2,1,0:T(8,128)(2,1)S(1)}, bf16[4,256,128]{2,1,0:T(8,128)(2,1)S(1)}, bf16[4,512,256]{2,1,0:T(8,128)(2,1)S(1)}, bf16[8,128,256]{2,...) custom-call(s32[8]{0:T(128)S(1)} %compare_select_fusion.4.meta, ...), custom_call_target="tpu_custom_call" | custom-call | flops 1342177280 | bytes 5242880 | tf_op jit(solution)/shard_map/send_maps/pallas_call | solution.py:408
  14.4 2.8 %collective-permute-start.1 = (bf16[4,528,256]{2,1,0:T(8,128)(2,1)S(1)}, bf16[4,528,256]{2,1,0:T(8,128)(2,1)S(1)}, u32[]{:S(2)}, u32[]{:S(2)}) collective-permute-start(bf16[4,528,256]{2,1,0:T(8,128)(2,1)S(1)} %get-tuple-element.52), channel_id=1, source_target_pairs={{0,1},{1,0},{2,3},{3,2},{4,5},{5,4},{6,7},{7,6},{8,9},{9,8},{10,11... | collective-permute-start | bytes 3244040 | tf_op jit(solution)/shard_map/ppermute | solution.py:761
  17.2 6.1 %keep_maps.1 = (bf16[4,528,256]{2,1,0:T(8,128)(2,1)S(1)}, bf16[4,256,128]{2,1,0:T(8,128)(2,1)S(1)}, bf16[4,512,256]{2,1,0:T(8,128)(2,1)S(1)}) custom-call(s32[8]{0:T(128)S(1)} %compare_select_fusion.4.meta, bf16[128,8192]{1,0:T(8,128)(2,1)S(1)} %get-tuple-element.43.x_ref.xq_ref, bf16[3,8192]{1,0:T(4,128)(2,1)S(1)} %collective-permute-done.halo_ref.hq_ref, ...), custom_call_target="tpu_custom_call" | custom-call | flops 1342177280 | bytes 5242880 | tf_op jit(solution)/shard_map/keep_maps/pallas_call | solution.py:426
  23.2 0.0 collective-permute-done.1.other_ref.left_ref
  23.2 1.4 %pair.1 = (bf16[528,256]{1,0:T(8,128)(2,1)S(1)}, bf16[528,256]{1,0:T(8,128)(2,1)S(1)}, bf16[528,256]{1,0:T(8,128)(2,1)S(1)}, bf16[528,256]{1,0:T(8,128)(2,1)S(1)}) custom-call(s32[8]{0:T(128)S(1)} %compare_select_fusion.4.meta, bf16[4,528,256]{2,1,0:T(8,128)(2,1)S(1)} %get-tuple-element.61.mine_ref, ...), custom_call_target="tpu_custom_call" | custom-call | flops 134217728 | bytes 3145728 | tf_op jit(solution)/shard_map/pair/pallas_call | solution.py:549
  24.7 0.1 collective-permute-start.2
  24.8 0.1 collective-permute-start.3
  24.8 0.6 collective-permute-start.4
  25.5 2.0 %collective-permute-start.5 = (bf16[528,256]{1,0:T(8,128)(2,1)S(1)}, bf16[528,256]{1,0:T(8,128)(2,1)S(1)}, u32[]{:S(2)}, u32[]{:S(2)}) collective-permute-start(bf16[528,256]{1,0:T(8,128)(2,1)S(1)} %get-tuple-element.69), channel_id=1, source_target_pairs={{0,6},{1,7},{2,4},{3,5},{4,2},{5,3},{6,0},{7,1},{8,14},{9,15},{10,... | collective-permute-start | bytes 811016 | tf_op jit(solution)/shard_map/ppermute | solution.py:761
  27.5 4.2 %reads.2 = (bf16[4,512,128]{2,1,0:T(8,128)(2,1)S(1)}, f32[4,512,128]{2,1,0:T(8,128)S(1)}) custom-call(s32[8]{0:T(128)S(1)} %compare_select_fusion.4.meta, bf16[128,8192]{1,0:T(8,128)(2,1)S(1)} %get-tuple-element.43.x_ref.xq_ref, bf16[3,8192]{1,0:T(4,128)(2,1)S(1)} %collective-permute-done.halo_ref.hq_ref, ...), custom_call_target="tpu_custom_call" | custom-call | flops 402653184 | bytes 5242880 | tf_op jit(solution)/shard_map/reads/pallas_call | solution.py:477
  31.7 0.0 collective-permute-done.2.left_ref
  31.7 4.2 %reads.3 = (bf16[4,512,128]{2,1,0:T(8,128)(2,1)S(1)}, f32[4,512,128]{2,1,0:T(8,128)S(1)}) custom-call(s32[8]{0:T(128)S(1)} %compare_select_fusion.4.meta, bf16[128,8192]{1,0:T(8,128)(2,1)S(1)} %get-tuple-element.43.x_ref.xq_ref, bf16[3,8192]{1,0:T(4,128)(2,1)S(1)} %collective-permute-done.halo_ref.hq_ref, ...), custom_call_target="tpu_custom_call" | custom-call | flops 402653184 | bytes 5242880 | tf_op jit(solution)/shard_map/reads/pallas_call | solution.py:477
  35.9 0.0 collective-permute-done.3.x1
  36.0 0.0 collective-permute-done.4.x2
  36.0 2.3 %collective-permute-done.5.x3 = bf16[528,256]{1,0:T(8,128)(2,1)S(1)} collective-permute-done((bf16[528,256]{1,0:T(8,128)(2,1)S(1)}, bf16[528,256]{1,0:T(8,128)(2,1)S(1)}, u32[]{:S(2)}, u32[]{:S(2)}) %collective-permute-start.5) | collective-permute-done | bytes 270368 | tf_op jit(solution)/shard_map/ppermute | solution.py:761
  38.3 1.3 %plane.1 = (bf16[4,528,256]{2,1,0:T(8,128)(2,1)S(1)}, bf16[528,256]{1,0:T(8,128)(2,1)S(1)}, bf16[512,128]{1,0:T(8,128)(2,1)S(1)}) custom-call(s32[8]{0:T(128)S(1)} %compare_select_fusion.4.meta, bf16[528,256]{1,0:T(8,128)(2,1)S(1)} %get-tuple-element.66.x0, bf16[528,256]{1,0:T(8,128)(2,1)S(1)} %collective-permute-done.3.x1, ...), custom_call_target="tpu_custom_call" | custom-call | flops 100663296 | bytes 2097152 | tf_op jit(solution)/shard_map/plane/pallas_call | solution.py:594
  39.6 1.3 %collective-permute-start.6 = (bf16[528,256]{1,0:T(8,128)(2,1)S(1)}, bf16[528,256]{1,0:T(8,128)(2,1)S(1)}, u32[]{:S(2)}, u32[]{:S(2)}) collective-permute-start(bf16[528,256]{1,0:T(8,128)(2,1)S(1)} %get-tuple-element.71.plane_ref), channel_id=1, source_target_pairs={{16,24},{17,25},{18,26},{19,27},{20,28},{21,29},{22,30},{23,31}} | collective-permute-start | bytes 811016 | tf_op jit(solution)/shard_map/ppermute | solution.py:667
  40.9 0.7 collective-permute-start.7
  41.6 0.0 collective-permute-done.7.state_ref.refs_0_
  41.6 0.2 hop.1
  41.8 0.7 collective-permute-start.9
  42.4 1.3 %collective-permute-start.8 = (bf16[512,128]{1,0:T(8,128)(2,1)S(1)}, bf16[512,128]{1,0:T(8,128)(2,1)S(1)}, u32[]{:S(2)}, u32[]{:S(2)}) collective-permute-start(bf16[512,128]{1,0:T(8,128)(2,1)S(1)} %hop.1), channel_id=1, source_target_pairs={{8,24},{9,25},{10,26},{11,27},{12,28},{13,29},{14,30},{15,31}} | collective-permute-start | bytes 393224 | tf_op jit(solution)/shard_map/ppermute | solution.py:667
  43.7 0.0 collective-permute-done.9.refs_1_
  43.8 7.7 %collective-permute-done.8.far_ref = bf16[512,128]{1,0:T(8,128)(2,1)S(1)} collective-permute-done((bf16[512,128]{1,0:T(8,128)(2,1)S(1)}, bf16[512,128]{1,0:T(8,128)(2,1)S(1)}, u32[]{:S(2)}, u32[]{:S(2)}) %collective-permute-start.8) | collective-permute-done | bytes 131104 | tf_op jit(solution)/shard_map/ppermute | solution.py:667
  51.5 0.0 collective-permute-done.6.before_ref
  51.5 1.4 %spread.1 = (bf16[512,128]{1,0:T(8,128)(2,1)S(1)}, bf16[512,128]{1,0:T(8,128)(2,1)S(1)}, bf16[512,128]{1,0:T(8,128)(2,1)S(1)}, bf16[512,128]{1,0:T(8,128)(2,1)S(1)}) custom-call(s32[8]{0:T(128)S(1)} %compare_select_fusion.4.meta, bf16[4,528,256]{2,1,0:T(8,128)(2,1)S(1)} %get-tuple-element.70.prefix_ref, ...), custom_call_target="tpu_custom_call" | custom-call | flops 83886080 | bytes 2097152 | tf_op jit(solution)/shard_map/spread/pallas_call | solution.py:651
  52.9 0.2 collective-permute-start.10
  53.2 1.1 %collective-permute-start.11 = (bf16[512,128]{1,0:T(8,128)(2,1)S(1)}, bf16[512,128]{1,0:T(8,128)(2,1)S(1)}, u32[]{:S(2)}, u32[]{:S(2)}) collective-permute-start(bf16[512,128]{1,0:T(8,128)(2,1)S(1)} %get-tuple-element.75), channel_id=1, source_target_pairs={{0,4},{1,5},{2,6},{3,7},{4,0},{5,1},{6,2},{7,3},{8,12},{9,13},{10,... | collective-permute-start | bytes 393224 | tf_op jit(solution)/shard_map/ppermute | solution.py:761
  54.2 1.4 %collective-permute-start.12 = (bf16[512,128]{1,0:T(8,128)(2,1)S(1)}, bf16[512,128]{1,0:T(8,128)(2,1)S(1)}, u32[]{:S(2)}, u32[]{:S(2)}) collective-permute-start(bf16[512,128]{1,0:T(8,128)(2,1)S(1)} %get-tuple-element.76), channel_id=1, source_target_pairs={{0,6},{1,7},{2,4},{3,5},{4,2},{5,3},{6,0},{7,1},{8,14},{9,15},{10,... | collective-permute-start | bytes 393224 | tf_op jit(solution)/shard_map/ppermute | solution.py:761
  55.6 4.2 %collective-permute-start.13 = (bf16[512,128]{1,0:T(8,128)(2,1)S(1)}, bf16[512,128]{1,0:T(8,128)(2,1)S(1)}, u32[]{:S(2)}, u32[]{:S(2)}) collective-permute-start(bf16[512,128]{1,0:T(8,128)(2,1)S(1)} %get-tuple-element.73.e0), channel_id=1, source_target_pairs={{0,1},{1,0},{2,3},{3,2},{4,5},{5,4},{6,7},{7,6},{8,9},{9,8},{10,11... | collective-permute-start | bytes 393224 | tf_op jit(solution)/shard_map/ppermute | solution.py:761
  59.8 0.0 collective-permute-done.10.e1
  59.8 1.5 %collective-permute-start.14 = (bf16[512,128]{1,0:T(8,128)(2,1)S(1)}, bf16[512,128]{1,0:T(8,128)(2,1)S(1)}, u32[]{:S(2)}, u32[]{:S(2)}) collective-permute-start(bf16[512,128]{1,0:T(8,128)(2,1)S(1)} %collective-permute-done.10.e1), channel_id=1, source_target_pairs={{0,1},{1,0},{2,3},{3,2},{4,5},{5,4},{6,7},{7,6},{8,9},{9,8},{10,11... | collective-permute-start | bytes 393224 | tf_op jit(solution)/shard_map/ppermute | solution.py:761
  61.3 0.0 collective-permute-done.11.e2
  61.3 1.5 %collective-permute-start.15 = (bf16[512,128]{1,0:T(8,128)(2,1)S(1)}, bf16[512,128]{1,0:T(8,128)(2,1)S(1)}, u32[]{:S(2)}, u32[]{:S(2)}) collective-permute-start(bf16[512,128]{1,0:T(8,128)(2,1)S(1)} %collective-permute-done.11.e2), channel_id=1, source_target_pairs={{0,1},{1,0},{2,3},{3,2},{4,5},{5,4},{6,7},{7,6},{8,9},{9,8},{10,11... | collective-permute-start | bytes 393224 | tf_op jit(solution)/shard_map/ppermute | solution.py:761
  62.8 0.0 collective-permute-done.12.e3
  62.8 1.5 %collective-permute-start.16 = (bf16[512,128]{1,0:T(8,128)(2,1)S(1)}, bf16[512,128]{1,0:T(8,128)(2,1)S(1)}, u32[]{:S(2)}, u32[]{:S(2)}) collective-permute-start(bf16[512,128]{1,0:T(8,128)(2,1)S(1)} %collective-permute-done.12.e3), channel_id=1, source_target_pairs={{0,1},{1,0},{2,3},{3,2},{4,5},{5,4},{6,7},{7,6},{8,9},{9,8},{10,11... | collective-permute-start | bytes 393224 | tf_op jit(solution)/shard_map/ppermute | solution.py:761
  64.3 0.8 %half.1.kept = bf16[4,128,512]{2,1,0:T(8,128)(2,1)S(1)} custom-call(s32[8]{0:T(128)S(1)} %compare_select_fusion.4.meta, bf16[4,512,128]{2,1,0:T(8,128)(2,1)S(1)} %get-tuple-element.64.r_ref, f32[4,512,128]{2,1,0:T(8,128)S(1)} %get-tuple-element.65.d_ref, bf16[512,128]{1,0:T(8,128)(2,1)S(1)} %get-tuple-element.73.e0, ...), custom_call_target="tpu_custom_call" | custom-call | flops 67108864 | bytes 3145728 | tf_op jit(solution)/shard_map/half/pallas_call | solution.py:701
  65.1 0.0 collective-permute-done.13.e0
  65.1 0.0 collective-permute-done.14.e1
  65.2 0.0 collective-permute-done.15.e2
  65.2 0.1 collective-permute-done.16.e3
  65.3 1.7 %emit.1 = bf16[128,4096]{1,0:T(8,128)(2,1)} custom-call(s32[8]{0:T(128)S(1)} %compare_select_fusion.4.meta, bf16[4,128,512]{2,1,0:T(8,128)(2,1)S(1)} %half.1.kept, bf16[4,512,128]{2,1,0:T(8,128)(2,1)S(1)} %get-tuple-element.77.r_ref, f32[4,512,128]{2,1,0:T(8,128)S(1)} %get-tuple-element.78.d_ref, bf16[512,128]{1,0:T(8,128)(2,1)S(1)} %collective-permute-done.13.e0, ...), custom_call_target="tpu_custom_call" | custom-call | flops 67108864 | bytes 3145728 | tf_op jit(solution)/shard_map/emit/pallas_call | solution.py:734
  (1 shorter events, 0.0 us)
Async XLA Ops:
  1.2 5.3 %collective-permute-start = (bf16[3,8192]{1,0:T(4,128)(2,1)S(1)}, bf16[3,8192]{1,0:T(4,128)(2,1)S(1)}, u32[]{:S(2)}, u32[]{:S(2)}) collective-permute-start(bf16[3,8192]{1,0:T(4,128)(2,1)S(1)} %get-tuple-element.44), channel_id=1, source_target_pairs={{0,1},{1,2},{2,3},{3,4},{4,5},{5,6},{6,7},{7,8},{8,9},{9,10},{10,1... | collective-permute-start | bytes 147464 | tf_op jit(solution)/shard_map/ppermute | solution.py:764
  14.4 8.8 %collective-permute-start.1 = (bf16[4,528,256]{2,1,0:T(8,128)(2,1)S(1)}, bf16[4,528,256]{2,1,0:T(8,128)(2,1)S(1)}, u32[]{:S(2)}, u32[]{:S(2)}) collective-permute-start(bf16[4,528,256]{2,1,0:T(8,128)(2,1)S(1)} %get-tuple-element.52), channel_id=1, source_target_pairs={{0,1},{1,0},{2,3},{3,2},{4,5},{5,4},{6,7},{7,6},{8,9},{9,8},{10,11... | collective-permute-start | bytes 3244040 | tf_op jit(solution)/shard_map/ppermute | solution.py:761
  24.7 7.0 %collective-permute-start.2 = (bf16[4,528,256]{2,1,0:T(8,128)(2,1)S(1)}, bf16[4,528,256]{2,1,0:T(8,128)(2,1)S(1)}, u32[]{:S(2)}, u32[]{:S(2)}) collective-permute-start(bf16[4,528,256]{2,1,0:T(8,128)(2,1)S(1)} %get-tuple-element.61.mine_ref), channel_id=1, source_target_pairs={{0,1},{1,0},{2,3},{3,2},{4,5},{5,4},{6,7},{7,6},{8,9},{9,8},{10,11... | collective-permute-start | bytes 3244040 | tf_op jit(solution)/shard_map/ppermute | solution.py:761
  24.8 11.2 %collective-permute-start.3 = (bf16[528,256]{1,0:T(8,128)(2,1)S(1)}, bf16[528,256]{1,0:T(8,128)(2,1)S(1)}, u32[]{:S(2)}, u32[]{:S(2)}) collective-permute-start(bf16[528,256]{1,0:T(8,128)(2,1)S(1)} %get-tuple-element.67), channel_id=1, source_target_pairs={{0,2},{1,3},{2,0},{3,1},{4,6},{5,7},{6,4},{7,5},{8,10},{9,11},{10,... | collective-permute-start | bytes 811016 | tf_op jit(solution)/shard_map/ppermute | solution.py:761
  24.8 11.1 %collective-permute-start.4 = (bf16[528,256]{1,0:T(8,128)(2,1)S(1)}, bf16[528,256]{1,0:T(8,128)(2,1)S(1)}, u32[]{:S(2)}, u32[]{:S(2)}) collective-permute-start(bf16[528,256]{1,0:T(8,128)(2,1)S(1)} %get-tuple-element.68), channel_id=1, source_target_pairs={{0,4},{1,5},{2,6},{3,7},{4,0},{5,1},{6,2},{7,3},{8,12},{9,13},{10,... | collective-permute-start | bytes 811016 | tf_op jit(solution)/shard_map/ppermute | solution.py:761
  25.5 12.8 %collective-permute-start.5 = (bf16[528,256]{1,0:T(8,128)(2,1)S(1)}, bf16[528,256]{1,0:T(8,128)(2,1)S(1)}, u32[]{:S(2)}, u32[]{:S(2)}) collective-permute-start(bf16[528,256]{1,0:T(8,128)(2,1)S(1)} %get-tuple-element.69), channel_id=1, source_target_pairs={{0,6},{1,7},{2,4},{3,5},{4,2},{5,3},{6,0},{7,1},{8,14},{9,15},{10,... | collective-permute-start | bytes 811016 | tf_op jit(solution)/shard_map/ppermute | solution.py:761
  39.6 11.9 %collective-permute-start.6 = (bf16[528,256]{1,0:T(8,128)(2,1)S(1)}, bf16[528,256]{1,0:T(8,128)(2,1)S(1)}, u32[]{:S(2)}, u32[]{:S(2)}) collective-permute-start(bf16[528,256]{1,0:T(8,128)(2,1)S(1)} %get-tuple-element.71.plane_ref), channel_id=1, source_target_pairs={{16,24},{17,25},{18,26},{19,27},{20,28},{21,29},{22,30},{23,31}} | collective-permute-start | bytes 811016 | tf_op jit(solution)/shard_map/ppermute | solution.py:667
  40.9 0.7 %collective-permute-start.7 = (bf16[512,128]{1,0:T(8,128)(2,1)S(1)}, bf16[512,128]{1,0:T(8,128)(2,1)S(1)}, u32[]{:S(2)}, u32[]{:S(2)}) collective-permute-start(bf16[512,128]{1,0:T(8,128)(2,1)S(1)} %get-tuple-element.72), channel_id=1, source_target_pairs={{0,8},{1,9},{2,10},{3,11},{4,12},{5,13},{6,14},{7,15}} | collective-permute-start | bytes 393224 | tf_op jit(solution)/shard_map/ppermute | solution.py:667
  41.8 2.0 %collective-permute-start.9 = (bf16[512,128]{1,0:T(8,128)(2,1)S(1)}, bf16[512,128]{1,0:T(8,128)(2,1)S(1)}, u32[]{:S(2)}, u32[]{:S(2)}) collective-permute-start(bf16[512,128]{1,0:T(8,128)(2,1)S(1)} %hop.1), channel_id=1, source_target_pairs={{8,16},{9,17},{10,18},{11,19},{12,20},{13,21},{14,22},{15,23}} | collective-permute-start | bytes 393224 | tf_op jit(solution)/shard_map/ppermute | solution.py:667
  42.4 9.0 %collective-permute-start.8 = (bf16[512,128]{1,0:T(8,128)(2,1)S(1)}, bf16[512,128]{1,0:T(8,128)(2,1)S(1)}, u32[]{:S(2)}, u32[]{:S(2)}) collective-permute-start(bf16[512,128]{1,0:T(8,128)(2,1)S(1)} %hop.1), channel_id=1, source_target_pairs={{8,24},{9,25},{10,26},{11,27},{12,28},{13,29},{14,30},{15,31}} | collective-permute-start | bytes 393224 | tf_op jit(solution)/shard_map/ppermute | solution.py:667
  52.9 6.9 %collective-permute-start.10 = (bf16[512,128]{1,0:T(8,128)(2,1)S(1)}, bf16[512,128]{1,0:T(8,128)(2,1)S(1)}, u32[]{:S(2)}, u32[]{:S(2)}) collective-permute-start(bf16[512,128]{1,0:T(8,128)(2,1)S(1)} %get-tuple-element.74), channel_id=1, source_target_pairs={{0,2},{1,3},{2,0},{3,1},{4,6},{5,7},{6,4},{7,5},{8,10},{9,11},{10,... | collective-permute-start | bytes 393224 | tf_op jit(solution)/shard_map/ppermute | solution.py:761
  53.2 8.1 %collective-permute-start.11 = (bf16[512,128]{1,0:T(8,128)(2,1)S(1)}, bf16[512,128]{1,0:T(8,128)(2,1)S(1)}, u32[]{:S(2)}, u32[]{:S(2)}) collective-permute-start(bf16[512,128]{1,0:T(8,128)(2,1)S(1)} %get-tuple-element.75), channel_id=1, source_target_pairs={{0,4},{1,5},{2,6},{3,7},{4,0},{5,1},{6,2},{7,3},{8,12},{9,13},{10,... | collective-permute-start | bytes 393224 | tf_op jit(solution)/shard_map/ppermute | solution.py:761
  54.2 8.5 %collective-permute-start.12 = (bf16[512,128]{1,0:T(8,128)(2,1)S(1)}, bf16[512,128]{1,0:T(8,128)(2,1)S(1)}, u32[]{:S(2)}, u32[]{:S(2)}) collective-permute-start(bf16[512,128]{1,0:T(8,128)(2,1)S(1)} %get-tuple-element.76), channel_id=1, source_target_pairs={{0,6},{1,7},{2,4},{3,5},{4,2},{5,3},{6,0},{7,1},{8,14},{9,15},{10,... | collective-permute-start | bytes 393224 | tf_op jit(solution)/shard_map/ppermute | solution.py:761
  55.6 9.5 %collective-permute-start.13 = (bf16[512,128]{1,0:T(8,128)(2,1)S(1)}, bf16[512,128]{1,0:T(8,128)(2,1)S(1)}, u32[]{:S(2)}, u32[]{:S(2)}) collective-permute-start(bf16[512,128]{1,0:T(8,128)(2,1)S(1)} %get-tuple-element.73.e0), channel_id=1, source_target_pairs={{0,1},{1,0},{2,3},{3,2},{4,5},{5,4},{6,7},{7,6},{8,9},{9,8},{10,11... | collective-permute-start | bytes 393224 | tf_op jit(solution)/shard_map/ppermute | solution.py:761
  59.8 5.4 %collective-permute-start.14 = (bf16[512,128]{1,0:T(8,128)(2,1)S(1)}, bf16[512,128]{1,0:T(8,128)(2,1)S(1)}, u32[]{:S(2)}, u32[]{:S(2)}) collective-permute-start(bf16[512,128]{1,0:T(8,128)(2,1)S(1)} %collective-permute-done.10.e1), channel_id=1, source_target_pairs={{0,1},{1,0},{2,3},{3,2},{4,5},{5,4},{6,7},{7,6},{8,9},{9,8},{10,11... | collective-permute-start | bytes 393224 | tf_op jit(solution)/shard_map/ppermute | solution.py:761
  61.3 3.9 %collective-permute-start.15 = (bf16[512,128]{1,0:T(8,128)(2,1)S(1)}, bf16[512,128]{1,0:T(8,128)(2,1)S(1)}, u32[]{:S(2)}, u32[]{:S(2)}) collective-permute-start(bf16[512,128]{1,0:T(8,128)(2,1)S(1)} %collective-permute-done.11.e2), channel_id=1, source_target_pairs={{0,1},{1,0},{2,3},{3,2},{4,5},{5,4},{6,7},{7,6},{8,9},{9,8},{10,11... | collective-permute-start | bytes 393224 | tf_op jit(solution)/shard_map/ppermute | solution.py:761
  62.8 2.5 %collective-permute-start.16 = (bf16[512,128]{1,0:T(8,128)(2,1)S(1)}, bf16[512,128]{1,0:T(8,128)(2,1)S(1)}, u32[]{:S(2)}, u32[]{:S(2)}) collective-permute-start(bf16[512,128]{1,0:T(8,128)(2,1)S(1)} %collective-permute-done.12.e3), channel_id=1, source_target_pairs={{0,1},{1,0},{2,3},{3,2},{4,5},{5,4},{6,7},{7,6},{8,9},{9,8},{10,11... | collective-permute-start | bytes 393224 | tf_op jit(solution)/shard_map/ppermute | solution.py:761
where the time goes:
time: 67.4 us; the launch traced here: 67.2 us
  Pallas kernels  32.1 us (48%)
  starting transfers between devices  24.5 us (36%)
  waiting for transfers between devices  10.2 us (15%)
    ppermute x12, starting transfers between devices, exchange(): return lax.ppermute(block, 'seq', [(i, i ^ bits) for i in range(count)])  16.9 us
    pallas_call x2, Pallas kernels, make_reads(): pl.pallas_call(read_kernel, grid_spec=pltpu.PrefetchScalarGridSpec(num_sc...  8.45 us
    pallas_call x1, Pallas kernels, send_maps(): pl.pallas_call(send_kernel, in_specs=[smem_spec()] + [whole_spec()] * len...  7.78 us
    ppermute x4, waiting for transfers between devices, ahead(): return lax.ppermute(block, 'seq', [(i, i + 8 * distance) for i in members])  7.72 us
    pallas_call x1, Pallas kernels, keep_maps(): pl.pallas_call(keep_kernel, in_specs=[smem_spec()] + [whole_spec()] * len...  6.06 us
    ppermute x4, starting transfers between devices, ahead(): return lax.ppermute(block, 'seq', [(i, i + 8 * distance) for i in members])  3.92 us
    ppermute x1, starting transfers between devices, shards(): lax.ppermute(tail_rows, 'seq', [(i, i + 1) for i in range(count - 1)])  3.68 us
    ppermute x12, waiting for transfers between devices, exchange(): return lax.ppermute(block, 'seq', [(i, i ^ bits) for i in range(count)])  2.44 us
  transfers between devices with their start and end apart: 17, of which 3 were waited for; matrix products, arithmetic and copies ran while one was open for 0% of the time, Pallas kernels for 26%

commit v1 on v0

--- a/solution.py
+++ b/solution.py
@@ -27,11 +27,6 @@
     return jnp.dot(a, b, preferred_element_type=F32)
 
 
-def halves(a):
-    high = a.astype(BF16)
-    return high, (a - high.astype(F32)).astype(BF16)
-
-
 def params(**kw):
     return pltpu.CompilerParams(vmem_limit_bytes=20 << 20, **kw)
 
@@ -48,7 +43,7 @@
     return pltpu.with_memory_space_constraint(x, pltpu.HBM)
 
 
-def prologue_kernel(decay_ref, beta_ref, starts_ref, x_ref, out_ref, tail_ref):
+def tail_kernel(starts_ref, x_ref, tail_ref):
     rows = x_ref.shape[0]
     flags = starts_ref[...].astype(F32)
     last = 1.0 - flags[:, TOK - 1 : TOK]
@@ -56,13 +51,35 @@
     for r in range(KW - 1):
         row = x_ref[rows - KW + 1 + r : rows - KW + 2 + r, :].astype(F32)
         tail_ref[r : r + 1, :] = (row * keep[r]).astype(BF16)
-    src = lax.broadcasted_iota(jnp.int32, (TOK, TOK), 0)
-    dst = lax.broadcasted_iota(jnp.int32, (TOK, TOK), 1)
-    upto = (src <= dst).astype(F32)
+
+
+def tail_of(starts, projected):
+    channels = projected.shape[1]
+    last = projected.shape[0] // 16 - 1
+    return pl.pallas_call(
+        tail_kernel,
+        grid=(1,),
+        in_specs=[
+            pl.BlockSpec((1, TOK), lambda i: (0, 0)),
+            pl.BlockSpec((16, channels), lambda i: (last, 0)),
+        ],
+        out_specs=pl.BlockSpec((KW - 1, channels), lambda i: (0, 0)),
+        out_shape=jax.ShapeDtypeStruct((KW - 1, channels), BF16),
+        compiler_params=params(),
+        cost_estimate=pl.CostEstimate(flops=10**5, bytes_accessed=10**6, transcendentals=0),
+        name="tail",
+    )(in_hbm(starts), in_hbm(projected))
+
+
+def write_tables(decay_ref, beta_ref, starts_ref, out_ref):
+    src, dst = positions()
     cum = LOG2E * jnp.dot(
-        decay_ref[...], upto, precision=lax.Precision.HIGHEST, preferred_element_type=F32
+        decay_ref[...],
+        (src <= dst).astype(F32),
+        precision=lax.Precision.HIGHEST,
+        preferred_element_type=F32,
     )
-    flags = jnp.broadcast_to(flags, (8, TOK)).astype(BF16)
+    flags = jnp.broadcast_to(starts_ref[...].astype(F32), (8, TOK)).astype(BF16)
     episode = [dot(flags, (src + j <= dst).astype(BF16))[0:1] for j in range(KW)]
     usable = [(episode[0] == episode[j]).astype(F32) for j in range(1, KW)]
     living = (episode[0] == 0.0).astype(F32)
@@ -74,37 +91,6 @@
         out_ref[pair, 8:16, :] = shared
 
 
-def prologue(decay_log, write_strength, starts, projected):
-    channels = projected.shape[1]
-    last = projected.shape[0] // 16 - 1
-    return pl.pallas_call(
-        prologue_kernel,
-        grid=(1,),
-        in_specs=[
-            pl.BlockSpec((HV, TOK), lambda i: (0, 0)),
-            pl.BlockSpec((HV, TOK), lambda i: (0, 0)),
-            pl.BlockSpec((1, TOK), lambda i: (0, 0)),
-            pl.BlockSpec((16, channels), lambda i: (last, 0)),
-        ],
-        out_specs=[
-            pl.BlockSpec((HV // GROUP, 16, TOK), lambda i: (0, 0, 0)),
-            pl.BlockSpec((KW - 1, channels), lambda i: (0, 0)),
-        ],
-        out_shape=[
-            jax.ShapeDtypeStruct((HV // GROUP, 16, TOK), F32),
-            jax.ShapeDtypeStruct((KW - 1, channels), BF16),
-        ],
-        compiler_params=params(),
-        cost_estimate=pl.CostEstimate(flops=10**7, bytes_accessed=10**6, transcendentals=0),
-        name="prologue",
-    )(
-        in_hbm(decay_log),
-        in_hbm(write_strength),
-        in_hbm(starts.reshape(1, TOK)),
-        in_hbm(projected),
-    )
-
-
 def place_window(x, halo, xs, first):
     cols = slice(first, first + x.shape[1])
     xs[8 : 8 + TOK, cols] = x.astype(F32)
@@ -161,13 +147,16 @@
     return jnp.concatenate([get(r, r + size) for r in range(size, TOK, 2 * size)], axis=0)
 
 
-def stage_kernel(tab_ref, x_hbm, w_hbm, x_out, w_out, masks, shared, sems):
+def stage_kernel(
+    decay_ref, beta_ref, starts_ref, x_hbm, w_hbm, x_out, w_out, tab_ref, masks, shared, sems
+):
     copies = [
         pltpu.make_async_copy(x_hbm, x_out, sems.at[0]),
         pltpu.make_async_copy(w_hbm, w_out, sems.at[1]),
     ]
     for copy in copies:
         copy.start()
+    write_tables(decay_ref, beta_ref, starts_ref, tab_ref)
     rows = tab_ref[0]
     cols = jnp.transpose(rows)
     for j in range(KW - 1):
@@ -184,22 +173,34 @@
         copy.wait()
 
 
-def stage(tables, projected, conv_weight):
+def stage(decay_log, write_strength, starts, projected, conv_weight):
+    def whole(*shape):
+        return pl.BlockSpec(shape, lambda i: (0,) * len(shape))
+
     return pl.pallas_call(
         stage_kernel,
-        in_specs=[whole_spec()] + [pl.BlockSpec(memory_space=pl.ANY)] * 2,
-        out_specs=[whole_spec()] * 4,
+        grid=(1,),
+        in_specs=[whole(HV, TOK), whole(HV, TOK), whole(1, TOK)]
+        + [pl.BlockSpec(memory_space=pl.ANY)] * 2,
+        out_specs=[whole_spec()] * 5,
         out_shape=[
             jax.ShapeDtypeStruct(projected.shape, BF16),
             jax.ShapeDtypeStruct(conv_weight.shape, BF16),
+            jax.ShapeDtypeStruct((HV // GROUP, 16, TOK), F32),
             jax.ShapeDtypeStruct((LEVELS + 1, TOK, TOK), BF16),
             jax.ShapeDtypeStruct((6, TOK, 128), F32),
         ],
         scratch_shapes=[pltpu.SemaphoreType.DMA((2,))],
         compiler_params=params(),
-        cost_estimate=pl.CostEstimate(flops=10**6, bytes_accessed=4 * 2**20, transcendentals=0),
+        cost_estimate=pl.CostEstimate(flops=10**7, bytes_accessed=4 * 2**20, transcendentals=0),
         name="stage",
-    )(tables, in_hbm(projected), in_hbm(conv_weight))
+    )(
+        in_hbm(decay_log),
+        in_hbm(write_strength),
+        in_hbm(starts),
+        in_hbm(projected),
+        in_hbm(conv_weight),
+    )
 
 
 def preparing(pair, ins, xs, sys, right, keys):
@@ -233,9 +234,7 @@
             clock = column(cols, lane)
             within = decay_within(rows, clock, lane, shared[4])
             carried = jnp.exp2(clock) * shared[3]
-            high, low = halves((column(cols, 4 + lane) * within) * inner)
-            sys[h, :, 0:128] = high
-            sys[h, :, 128:256] = low
+            sys[h] = ((column(cols, 4 + lane) * within) * inner).astype(BF16)
             right[h, :, 0:DK] = (carried * k).astype(BF16)
 
     def value(h):
@@ -255,16 +254,16 @@
 
     def begin():
         for h in range(HEADS):
-            inv[h] = masks[LEVELS] - sys[h, :, 0:128] * masks[0]
+            inv[h] = masks[LEVELS] - sys[h] * masks[0]
 
     def first_product(level):
         size = 1 << level
         kept["steps"] = []
         for h in range(HEADS):
             if size < 16:
-                left = sys[h, :, 0:128]
+                left = sys[h]
             else:
-                left = odd_rows(lambda r, e: sys[h, r:e, 0:128], size)
+                left = odd_rows(lambda r, e: sys[h, r:e, :], size)
             kept["steps"].append(dot(left, inv[h]).astype(BF16))
 
     def second_product(level):
@@ -293,7 +292,7 @@
         kept["gaps"] = []
         for h in range(HEADS):
             rough = inv[h]
-            product = dot(sys[h], jnp.concatenate([rough, rough], axis=0))
+            product = dot(sys[h], rough)
             kept["gaps"].append(
                 ((masks[LEVELS].astype(F32) - rough.astype(F32)) - product).astype(BF16)
             )
@@ -392,7 +391,7 @@
 
 def ready_shapes():
     return [
-        jax.ShapeDtypeStruct((HEADS, TOK, 256), BF16),
+        jax.ShapeDtypeStruct((HEADS, TOK, TOK), BF16),
         jax.ShapeDtypeStruct((HEADS, TOK, 256), BF16),
         jax.ShapeDtypeStruct((2, 2 * DK, TOK), BF16),
     ]
@@ -412,7 +411,7 @@
         out_shape=map_shapes() + ready_shapes(),
         scratch_shapes=[
             pltpu.VMEM((8 + TOK, 1536), F32),
-            pltpu.VMEM((2, HEADS, TOK, 256), BF16),
+            pltpu.VMEM((2, HEADS, TOK, TOK), BF16),
             pltpu.VMEM((2, HEADS, TOK, 256), BF16),
             pltpu.VMEM((HEADS, TOK, TOK), BF16),
         ],
@@ -430,7 +429,7 @@
         out_shape=map_shapes(),
         scratch_shapes=[
             pltpu.VMEM((8 + TOK, 1536), F32),
-            pltpu.VMEM((HEADS, TOK, 256), BF16),
+            pltpu.VMEM((HEADS, TOK, TOK), BF16),
             pltpu.VMEM((HEADS, TOK, 256), BF16),
             pltpu.VMEM((HEADS, TOK, TOK), BF16),
         ],
@@ -529,20 +528,22 @@
 
 
 def pair_kernel(meta, mine_ref, other_ref, *out_refs):
-    first = meta[2] == 0
-    for m, out_ref in enumerate(out_refs):
-        g = meta[3] ^ m
-        tail_m, tail_o = mine_ref[g, GROUP * DK : ROWS, :], other_ref[g, GROUP * DK : ROWS, :]
-        tail_l, tail_r = jnp.where(first, tail_m, tail_o), jnp.where(first, tail_o, tail_m)
-        factors = []
-        for h in range(GROUP):
-            here = slice(h * DK, (h + 1) * DK)
-            own, other = mine_ref[g, here, :], other_ref[g, here, :]
-            left, right = jnp.where(first, own, other), jnp.where(first, other, own)
-            left_c, right_c = factor(tail_l, h), factor(tail_r, h)
-            out_ref[here, :] = compose(left, left_c, right, right_c).astype(BF16)
-            factors.append(left_c * right_c)
-        out_ref[GROUP * DK : ROWS, :] = split_rows(factors)
+    def combine(left_ref, right_ref):
+        for m, out_ref in enumerate(out_refs):
+            g = meta[3] ^ m
+            left_tail = left_ref[g, GROUP * DK : ROWS, :]
+            right_tail = right_ref[g, GROUP * DK : ROWS, :]
+            factors = []
+            for h in range(GROUP):
+                here = slice(h * DK, (h + 1) * DK)
+                left_c, right_c = factor(left_tail, h), factor(right_tail, h)
+                both = compose(left_ref[g, here, :], left_c, right_ref[g, here, :], right_c)
+                out_ref[here, :] = both.astype(BF16)
+                factors.append(left_c * right_c)
+            out_ref[GROUP * DK : ROWS, :] = split_rows(factors)
+
+    pl.when(meta[2] == 0)(lambda: combine(mine_ref, other_ref))
+    pl.when(meta[2] != 0)(lambda: combine(other_ref, mine_ref))
 
 
 def pair_maps(meta, mine, other):
@@ -760,9 +761,12 @@
     def exchange(block, bits):
         return lax.ppermute(block, "seq", [(i, i ^ bits) for i in range(count)])
 
-    tables, tail_rows = prologue(decay_log, write_strength, starts, projected)
+    starts = starts.reshape(1, TOK)
+    tail_rows = tail_of(starts, projected)
     halo = lax.ppermute(tail_rows, "seq", [(i, i + 1) for i in range(count - 1)])
-    projected, conv_weight, masks, shared = stage(tables, projected, conv_weight)
+    projected, conv_weight, tables, masks, shared = stage(
+        decay_log, write_strength, starts, projected, conv_weight
+    )
     ins = (projected, halo, conv_weight, tables, masks, shared)
 
     pay_s, kt_s, ef_s, *ready = send_maps(meta, *ins)

time: 67.4 us -> 66.9 us (level)
  starting transfers between devices: 24.5 us -> 23.8 us
    ppermute x12, starting transfers between devices: 16.9 us -> 16.2 us  [exchange(): return lax.ppermute(block, 'seq', [(i, i ^ bits) for i in range(count)])]
  transfers between devices with their start and end apart: 17 -> 17, of which waited for: 3 -> 3; matrix products, arithmetic and copies ran while one was open for 0% -> 0% of each run, Pallas kernels for 26% -> 27%
where the time goes in v1:
time: 66.9 us; the launch traced here: 66.6 us
  Pallas kernels  32.3 us (48%)
  starting transfers between devices  23.8 us (36%)
  waiting for transfers between devices  10.1 us (15%)
    ppermute x12, starting transfers between devices, exchange(): return lax.ppermute(block, 'seq', [(i, i ^ bits) for i in range(count)])  16.2 us
    pallas_call x2, Pallas kernels, make_reads(): pl.pallas_call(read_kernel, grid_spec=pltpu.PrefetchScalarGridSpec(num_sc...  8.45 us
    ppermute x4, waiting for transfers between devices, ahead(): return lax.ppermute(block, 'seq', [(i, i + 8 * distance) for i in members])  7.68 us
    pallas_call x1, Pallas kernels, send_maps(): pl.pallas_call(send_kernel, in_specs=[smem_spec()] + [whole_spec()] * len...  7.52 us
    pallas_call x1, Pallas kernels, keep_maps(): pl.pallas_call(keep_kernel, in_specs=[smem_spec()] + [whole_spec()] * len...  5.96 us
    ppermute x4, starting transfers between devices, ahead(): return lax.ppermute(block, 'seq', [(i, i + 8 * distance) for i in members])  3.92 us
    ppermute x1, starting transfers between devices, shards(): lax.ppermute(tail_rows, 'seq', [(i, i + 1) for i in range(count - 1)])  3.68 us
    ppermute x12, waiting for transfers between devices, exchange(): return lax.ppermute(block, 'seq', [(i, i ^ bits) for i in range(count)])  2.45 us
  transfers between devices with their start and end apart: 17, of which 3 were waited for; matrix products, arithmetic and copies ran while one was open for 0% of the time, Pallas kernels for 27%

profile of v1, /device:TPU:25, one launch (start us, length us, event | category | flops | bytes accessed | tf_op | source)
XLA Modules:
  0.0 66.6 jit_solution(3719731867052910612)
XLA Ops:
  0.0 1.1 %tail.1 = bf16[3,8192]{1,0:T(4,128)(2,1)S(1)} custom-call(s32[1,128]{1,0:T(1,128)} %bitcast.1, bf16[128,8192]{1,0:T(8,128)(2,1)} %x_ref.1), custom_call_target="tpu_custom_call" | custom-call | flops 100000 | bytes 1000000 | tf_op jit(solution)/shard_map/tail/pallas_call | solution.py:59
  1.1 3.7 %collective-permute-start = (bf16[3,8192]{1,0:T(4,128)(2,1)S(1)}, bf16[3,8192]{1,0:T(4,128)(2,1)S(1)}, u32[]{:S(2)}, u32[]{:S(2)}) collective-permute-start(bf16[3,8192]{1,0:T(4,128)(2,1)S(1)} %tail.1), channel_id=1, source_target_pairs={{0,1},{1,2},{2,3},{3,4},{4,5},{5,6},{6,7},{7,8},{8,9},{9,10},{10,1... | collective-permute-start | bytes 147464 | tf_op jit(solution)/shard_map/ppermute | solution.py:766
  4.9 2.4 %stage.1 = (bf16[128,8192]{1,0:T(8,128)(2,1)S(1)}, bf16[4,8192]{1,0:T(4,128)(2,1)S(1)}, f32[8,16,128]{2,1,0:T(8,128)S(1)}, bf16[8,128,128]{2,1,0:T(8,128)(2,1)S(1)}, f32[6,128,128]{2,1,0:T(8,128)S(1)}) custom-call(f32[32,128]{1,0:T(8,128)} %decay_ref.1, f32[32,128]{1,0:T(8,128)} %beta_ref.1, s32[1,128]{1,0:T(1,128)} %bitcast.2, bf16[128,8192]{1,0:T(8,128)(2,1)} %x_ref.1, ...), custom_call_target="tpu_custom_call" | custom-call | flops 10000000 | bytes 4194304 | tf_op jit(solution)/shard_map/stage/pallas_call | solution.py:180
  7.2 0.0 collective-permute-done.halo_ref.hq_ref
  7.2 7.5 %send_maps.1 = (bf16[4,528,256]{2,1,0:T(8,128)(2,1)S(1)}, bf16[4,256,128]{2,1,0:T(8,128)(2,1)S(1)}, bf16[4,512,256]{2,1,0:T(8,128)(2,1)S(1)}, bf16[8,128,128]{2,...) custom-call(s32[8]{0:T(128)S(1)} %compare_select_fusion.4.meta, ...), custom_call_target="tpu_custom_call" | custom-call | flops 1342177280 | bytes 5242880 | tf_op jit(solution)/shard_map/send_maps/pallas_call | solution.py:407
  14.8 2.0 %collective-permute-start.1 = (bf16[4,528,256]{2,1,0:T(8,128)(2,1)S(1)}, bf16[4,528,256]{2,1,0:T(8,128)(2,1)S(1)}, u32[]{:S(2)}, u32[]{:S(2)}) collective-permute-start(bf16[4,528,256]{2,1,0:T(8,128)(2,1)S(1)} %get-tuple-element.50), channel_id=1, source_target_pairs={{0,1},{1,0},{2,3},{3,2},{4,5},{5,4},{6,7},{7,6},{8,9},{9,8},{10,11... | collective-permute-start | bytes 3244040 | tf_op jit(solution)/shard_map/ppermute | solution.py:762
  16.8 6.0 %keep_maps.1 = (bf16[4,528,256]{2,1,0:T(8,128)(2,1)S(1)}, bf16[4,256,128]{2,1,0:T(8,128)(2,1)S(1)}, bf16[4,512,256]{2,1,0:T(8,128)(2,1)S(1)}) custom-call(s32[8]{0:T(128)S(1)} %compare_select_fusion.4.meta, bf16[128,8192]{1,0:T(8,128)(2,1)S(1)} %get-tuple-element.41.x_ref.xq_ref, bf16[3,8192]{1,0:T(4,128)(2,1)S(1)} %collective-permute-done.halo_ref.hq_ref, ...), custom_call_target="tpu_custom_call" | custom-call | flops 1342177280 | bytes 5242880 | tf_op jit(solution)/shard_map/keep_maps/pallas_call | solution.py:425
  22.8 0.0 collective-permute-done.1.other_ref.left_ref
  22.8 1.4 %pair.1 = (bf16[528,256]{1,0:T(8,128)(2,1)S(1)}, bf16[528,256]{1,0:T(8,128)(2,1)S(1)}, bf16[528,256]{1,0:T(8,128)(2,1)S(1)}, bf16[528,256]{1,0:T(8,128)(2,1)S(1)}) custom-call(s32[8]{0:T(128)S(1)} %compare_select_fusion.4.meta, bf16[4,528,256]{2,1,0:T(8,128)(2,1)S(1)} %get-tuple-element.59.mine_ref, ...), custom_call_target="tpu_custom_call" | custom-call | flops 134217728 | bytes 3145728 | tf_op jit(solution)/shard_map/pair/pallas_call | solution.py:550
  24.2 0.1 collective-permute-start.2
  24.2 0.1 collective-permute-start.3
  24.3 0.6 collective-permute-start.4
  25.0 2.0 %collective-permute-start.5 = (bf16[528,256]{1,0:T(8,128)(2,1)S(1)}, bf16[528,256]{1,0:T(8,128)(2,1)S(1)}, u32[]{:S(2)}, u32[]{:S(2)}) collective-permute-start(bf16[528,256]{1,0:T(8,128)(2,1)S(1)} %get-tuple-element.67), channel_id=1, source_target_pairs={{0,6},{1,7},{2,4},{3,5},{4,2},{5,3},{6,0},{7,1},{8,14},{9,15},{10,... | collective-permute-start | bytes 811016 | tf_op jit(solution)/shard_map/ppermute | solution.py:762
  26.9 4.2 %reads.2 = (bf16[4,512,128]{2,1,0:T(8,128)(2,1)S(1)}, f32[4,512,128]{2,1,0:T(8,128)S(1)}) custom-call(s32[8]{0:T(128)S(1)} %compare_select_fusion.4.meta, bf16[128,8192]{1,0:T(8,128)(2,1)S(1)} %get-tuple-element.41.x_ref.xq_ref, bf16[3,8192]{1,0:T(4,128)(2,1)S(1)} %collective-permute-done.halo_ref.hq_ref, ...), custom_call_target="tpu_custom_call" | custom-call | flops 402653184 | bytes 5242880 | tf_op jit(solution)/shard_map/reads/pallas_call | solution.py:476
  31.2 0.0 collective-permute-done.2.left_ref
  31.2 4.2 %reads.3 = (bf16[4,512,128]{2,1,0:T(8,128)(2,1)S(1)}, f32[4,512,128]{2,1,0:T(8,128)S(1)}) custom-call(s32[8]{0:T(128)S(1)} %compare_select_fusion.4.meta, bf16[128,8192]{1,0:T(8,128)(2,1)S(1)} %get-tuple-element.41.x_ref.xq_ref, bf16[3,8192]{1,0:T(4,128)(2,1)S(1)} %collective-permute-done.halo_ref.hq_ref, ...), custom_call_target="tpu_custom_call" | custom-call | flops 402653184 | bytes 5242880 | tf_op jit(solution)/shard_map/reads/pallas_call | solution.py:476
  35.4 0.0 collective-permute-done.3.x1
  35.4 0.0 collective-permute-done.4.x2
  35.4 2.3 %collective-permute-done.5.x3 = bf16[528,256]{1,0:T(8,128)(2,1)S(1)} collective-permute-done((bf16[528,256]{1,0:T(8,128)(2,1)S(1)}, bf16[528,256]{1,0:T(8,128)(2,1)S(1)}, u32[]{:S(2)}, u32[]{:S(2)}) %collective-permute-start.5) | collective-permute-done | bytes 270368 | tf_op jit(solution)/shard_map/ppermute | solution.py:762
  37.8 1.3 %plane.1 = (bf16[4,528,256]{2,1,0:T(8,128)(2,1)S(1)}, bf16[528,256]{1,0:T(8,128)(2,1)S(1)}, bf16[512,128]{1,0:T(8,128)(2,1)S(1)}) custom-call(s32[8]{0:T(128)S(1)} %compare_select_fusion.4.meta, bf16[528,256]{1,0:T(8,128)(2,1)S(1)} %get-tuple-element.64.x0, bf16[528,256]{1,0:T(8,128)(2,1)S(1)} %collective-permute-done.3.x1, ...), custom_call_target="tpu_custom_call" | custom-call | flops 100663296 | bytes 2097152 | tf_op jit(solution)/shard_map/plane/pallas_call | solution.py:595
  39.1 1.3 %collective-permute-start.6 = (bf16[528,256]{1,0:T(8,128)(2,1)S(1)}, bf16[528,256]{1,0:T(8,128)(2,1)S(1)}, u32[]{:S(2)}, u32[]{:S(2)}) collective-permute-start(bf16[528,256]{1,0:T(8,128)(2,1)S(1)} %get-tuple-element.69.plane_ref), channel_id=1, source_target_pairs={{16,24},{17,25},{18,26},{19,27},{20,28},{21,29},{22,30},{23,31}} | collective-permute-start | bytes 811016 | tf_op jit(solution)/shard_map/ppermute | solution.py:668
  40.4 0.7 %collective-permute-start.7 = (bf16[512,128]{1,0:T(8,128)(2,1)S(1)}, bf16[512,128]{1,0:T(8,128)(2,1)S(1)}, u32[]{:S(2)}, u32[]{:S(2)}) collective-permute-start(bf16[512,128]{1,0:T(8,128)(2,1)S(1)} %get-tuple-element.70), channel_id=1, source_target_pairs={{0,8},{1,9},{2,10},{3,11},{4,12},{5,13},{6,14},{7,15}} | collective-permute-start | bytes 393224 | tf_op jit(solution)/shard_map/ppermute | solution.py:668
  41.1 0.0 collective-permute-done.7.state_ref.refs_0_
  41.1 0.2 hop.1
  41.2 0.7 %collective-permute-start.9 = (bf16[512,128]{1,0:T(8,128)(2,1)S(1)}, bf16[512,128]{1,0:T(8,128)(2,1)S(1)}, u32[]{:S(2)}, u32[]{:S(2)}) collective-permute-start(bf16[512,128]{1,0:T(8,128)(2,1)S(1)} %hop.1), channel_id=1, source_target_pairs={{8,16},{9,17},{10,18},{11,19},{12,20},{13,21},{14,22},{15,23}} | collective-permute-start | bytes 393224 | tf_op jit(solution)/shard_map/ppermute | solution.py:668
  41.9 1.3 %collective-permute-start.8 = (bf16[512,128]{1,0:T(8,128)(2,1)S(1)}, bf16[512,128]{1,0:T(8,128)(2,1)S(1)}, u32[]{:S(2)}, u32[]{:S(2)}) collective-permute-start(bf16[512,128]{1,0:T(8,128)(2,1)S(1)} %hop.1), channel_id=1, source_target_pairs={{8,24},{9,25},{10,26},{11,27},{12,28},{13,29},{14,30},{15,31}} | collective-permute-start | bytes 393224 | tf_op jit(solution)/shard_map/ppermute | solution.py:668
  43.2 0.0 collective-permute-done.9.refs_1_
  43.2 7.7 %collective-permute-done.8.far_ref = bf16[512,128]{1,0:T(8,128)(2,1)S(1)} collective-permute-done((bf16[512,128]{1,0:T(8,128)(2,1)S(1)}, bf16[512,128]{1,0:T(8,128)(2,1)S(1)}, u32[]{:S(2)}, u32[]{:S(2)}) %collective-permute-start.8) | collective-permute-done | bytes 131104 | tf_op jit(solution)/shard_map/ppermute | solution.py:668
  50.9 0.0 collective-permute-done.6.before_ref
  50.9 1.4 %spread.1 = (bf16[512,128]{1,0:T(8,128)(2,1)S(1)}, bf16[512,128]{1,0:T(8,128)(2,1)S(1)}, bf16[512,128]{1,0:T(8,128)(2,1)S(1)}, bf16[512,128]{1,0:T(8,128)(2,1)S(1)}) custom-call(s32[8]{0:T(128)S(1)} %compare_select_fusion.4.meta, bf16[4,528,256]{2,1,0:T(8,128)(2,1)S(1)} %get-tuple-element.68.prefix_ref, ...), custom_call_target="tpu_custom_call" | custom-call | flops 83886080 | bytes 2097152 | tf_op jit(solution)/shard_map/spread/pallas_call | solution.py:652
  52.4 0.8 %collective-permute-start.10 = (bf16[512,128]{1,0:T(8,128)(2,1)S(1)}, bf16[512,128]{1,0:T(8,128)(2,1)S(1)}, u32[]{:S(2)}, u32[]{:S(2)}) collective-permute-start(bf16[512,128]{1,0:T(8,128)(2,1)S(1)} %get-tuple-element.72), channel_id=1, source_target_pairs={{0,2},{1,3},{2,0},{3,1},{4,6},{5,7},{6,4},{7,5},{8,10},{9,11},{10,... | collective-permute-start | bytes 393224 | tf_op jit(solution)/shard_map/ppermute | solution.py:762
  53.1 0.6 collective-permute-start.11
  53.7 1.4 %collective-permute-start.12 = (bf16[512,128]{1,0:T(8,128)(2,1)S(1)}, bf16[512,128]{1,0:T(8,128)(2,1)S(1)}, u32[]{:S(2)}, u32[]{:S(2)}) collective-permute-start(bf16[512,128]{1,0:T(8,128)(2,1)S(1)} %get-tuple-element.74), channel_id=1, source_target_pairs={{0,6},{1,7},{2,4},{3,5},{4,2},{5,3},{6,0},{7,1},{8,14},{9,15},{10,... | collective-permute-start | bytes 393224 | tf_op jit(solution)/shard_map/ppermute | solution.py:762
  55.1 4.2 %collective-permute-start.13 = (bf16[512,128]{1,0:T(8,128)(2,1)S(1)}, bf16[512,128]{1,0:T(8,128)(2,1)S(1)}, u32[]{:S(2)}, u32[]{:S(2)}) collective-permute-start(bf16[512,128]{1,0:T(8,128)(2,1)S(1)} %get-tuple-element.71.e0), channel_id=1, source_target_pairs={{0,1},{1,0},{2,3},{3,2},{4,5},{5,4},{6,7},{7,6},{8,9},{9,8},{10,11... | collective-permute-start | bytes 393224 | tf_op jit(solution)/shard_map/ppermute | solution.py:762
  59.3 0.0 collective-permute-done.10.e1
  59.3 1.5 %collective-permute-start.14 = (bf16[512,128]{1,0:T(8,128)(2,1)S(1)}, bf16[512,128]{1,0:T(8,128)(2,1)S(1)}, u32[]{:S(2)}, u32[]{:S(2)}) collective-permute-start(bf16[512,128]{1,0:T(8,128)(2,1)S(1)} %collective-permute-done.10.e1), channel_id=1, source_target_pairs={{0,1},{1,0},{2,3},{3,2},{4,5},{5,4},{6,7},{7,6},{8,9},{9,8},{10,11... | collective-permute-start | bytes 393224 | tf_op jit(solution)/shard_map/ppermute | solution.py:762
  60.7 0.0 collective-permute-done.11.e2
  60.7 1.5 %collective-permute-start.15 = (bf16[512,128]{1,0:T(8,128)(2,1)S(1)}, bf16[512,128]{1,0:T(8,128)(2,1)S(1)}, u32[]{:S(2)}, u32[]{:S(2)}) collective-permute-start(bf16[512,128]{1,0:T(8,128)(2,1)S(1)} %collective-permute-done.11.e2), channel_id=1, source_target_pairs={{0,1},{1,0},{2,3},{3,2},{4,5},{5,4},{6,7},{7,6},{8,9},{9,8},{10,11... | collective-permute-start | bytes 393224 | tf_op jit(solution)/shard_map/ppermute | solution.py:762
  62.2 0.0 collective-permute-done.12.e3
  62.2 1.5 %collective-permute-start.16 = (bf16[512,128]{1,0:T(8,128)(2,1)S(1)}, bf16[512,128]{1,0:T(8,128)(2,1)S(1)}, u32[]{:S(2)}, u32[]{:S(2)}) collective-permute-start(bf16[512,128]{1,0:T(8,128)(2,1)S(1)} %collective-permute-done.12.e3), channel_id=1, source_target_pairs={{0,1},{1,0},{2,3},{3,2},{4,5},{5,4},{6,7},{7,6},{8,9},{9,8},{10,11... | collective-permute-start | bytes 393224 | tf_op jit(solution)/shard_map/ppermute | solution.py:762
  63.8 0.8 %half.1.kept = bf16[4,128,512]{2,1,0:T(8,128)(2,1)S(1)} custom-call(s32[8]{0:T(128)S(1)} %compare_select_fusion.4.meta, bf16[4,512,128]{2,1,0:T(8,128)(2,1)S(1)} %get-tuple-element.62.r_ref, f32[4,512,128]{2,1,0:T(8,128)S(1)} %get-tuple-element.63.d_ref, bf16[512,128]{1,0:T(8,128)(2,1)S(1)} %get-tuple-element.71.e0, ...), custom_call_target="tpu_custom_call" | custom-call | flops 67108864 | bytes 3145728 | tf_op jit(solution)/shard_map/half/pallas_call | solution.py:702
  64.6 0.0 collective-permute-done.13.e0
  64.6 0.0 collective-permute-done.14.e1
  64.6 0.0 collective-permute-done.15.e2
  64.6 0.1 collective-permute-done.16.e3
  64.8 1.7 %emit.1 = bf16[128,4096]{1,0:T(8,128)(2,1)} custom-call(s32[8]{0:T(128)S(1)} %compare_select_fusion.4.meta, bf16[4,128,512]{2,1,0:T(8,128)(2,1)S(1)} %half.1.kept, bf16[4,512,128]{2,1,0:T(8,128)(2,1)S(1)} %get-tuple-element.75.r_ref, f32[4,512,128]{2,1,0:T(8,128)S(1)} %get-tuple-element.76.d_ref, bf16[512,128]{1,0:T(8,128)(2,1)S(1)} %collective-permute-done.13.e0, ...), custom_call_target="tpu_custom_call" | custom-call | flops 67108864 | bytes 3145728 | tf_op jit(solution)/shard_map/emit/pallas_call | solution.py:735
  (1 shorter events, 0.0 us)
Async XLA Ops:
  1.1 6.1 %collective-permute-start = (bf16[3,8192]{1,0:T(4,128)(2,1)S(1)}, bf16[3,8192]{1,0:T(4,128)(2,1)S(1)}, u32[]{:S(2)}, u32[]{:S(2)}) collective-permute-start(bf16[3,8192]{1,0:T(4,128)(2,1)S(1)} %tail.1), channel_id=1, source_target_pairs={{0,1},{1,2},{2,3},{3,4},{4,5},{5,6},{6,7},{7,8},{8,9},{9,10},{10,1... | collective-permute-start | bytes 147464 | tf_op jit(solution)/shard_map/ppermute | solution.py:766
  14.8 8.0 %collective-permute-start.1 = (bf16[4,528,256]{2,1,0:T(8,128)(2,1)S(1)}, bf16[4,528,256]{2,1,0:T(8,128)(2,1)S(1)}, u32[]{:S(2)}, u32[]{:S(2)}) collective-permute-start(bf16[4,528,256]{2,1,0:T(8,128)(2,1)S(1)} %get-tuple-element.50), channel_id=1, source_target_pairs={{0,1},{1,0},{2,3},{3,2},{4,5},{5,4},{6,7},{7,6},{8,9},{9,8},{10,11... | collective-permute-start | bytes 3244040 | tf_op jit(solution)/shard_map/ppermute | solution.py:762
  24.2 7.0 %collective-permute-start.2 = (bf16[4,528,256]{2,1,0:T(8,128)(2,1)S(1)}, bf16[4,528,256]{2,1,0:T(8,128)(2,1)S(1)}, u32[]{:S(2)}, u32[]{:S(2)}) collective-permute-start(bf16[4,528,256]{2,1,0:T(8,128)(2,1)S(1)} %get-tuple-element.59.mine_ref), channel_id=1, source_target_pairs={{0,1},{1,0},{2,3},{3,2},{4,5},{5,4},{6,7},{7,6},{8,9},{9,8},{10,11... | collective-permute-start | bytes 3244040 | tf_op jit(solution)/shard_map/ppermute | solution.py:762
  24.2 11.2 %collective-permute-start.3 = (bf16[528,256]{1,0:T(8,128)(2,1)S(1)}, bf16[528,256]{1,0:T(8,128)(2,1)S(1)}, u32[]{:S(2)}, u32[]{:S(2)}) collective-permute-start(bf16[528,256]{1,0:T(8,128)(2,1)S(1)} %get-tuple-element.65), channel_id=1, source_target_pairs={{0,2},{1,3},{2,0},{3,1},{4,6},{5,7},{6,4},{7,5},{8,10},{9,11},{10,... | collective-permute-start | bytes 811016 | tf_op jit(solution)/shard_map/ppermute | solution.py:762
  24.3 11.1 %collective-permute-start.4 = (bf16[528,256]{1,0:T(8,128)(2,1)S(1)}, bf16[528,256]{1,0:T(8,128)(2,1)S(1)}, u32[]{:S(2)}, u32[]{:S(2)}) collective-permute-start(bf16[528,256]{1,0:T(8,128)(2,1)S(1)} %get-tuple-element.66), channel_id=1, source_target_pairs={{0,4},{1,5},{2,6},{3,7},{4,0},{5,1},{6,2},{7,3},{8,12},{9,13},{10,... | collective-permute-start | bytes 811016 | tf_op jit(solution)/shard_map/ppermute | solution.py:762
  25.0 12.8 %collective-permute-start.5 = (bf16[528,256]{1,0:T(8,128)(2,1)S(1)}, bf16[528,256]{1,0:T(8,128)(2,1)S(1)}, u32[]{:S(2)}, u32[]{:S(2)}) collective-permute-start(bf16[528,256]{1,0:T(8,128)(2,1)S(1)} %get-tuple-element.67), channel_id=1, source_target_pairs={{0,6},{1,7},{2,4},{3,5},{4,2},{5,3},{6,0},{7,1},{8,14},{9,15},{10,... | collective-permute-start | bytes 811016 | tf_op jit(solution)/shard_map/ppermute | solution.py:762
  39.1 11.8 %collective-permute-start.6 = (bf16[528,256]{1,0:T(8,128)(2,1)S(1)}, bf16[528,256]{1,0:T(8,128)(2,1)S(1)}, u32[]{:S(2)}, u32[]{:S(2)}) collective-permute-start(bf16[528,256]{1,0:T(8,128)(2,1)S(1)} %get-tuple-element.69.plane_ref), channel_id=1, source_target_pairs={{16,24},{17,25},{18,26},{19,27},{20,28},{21,29},{22,30},{23,31}} | collective-permute-start | bytes 811016 | tf_op jit(solution)/shard_map/ppermute | solution.py:668
  40.4 0.7 %collective-permute-start.7 = (bf16[512,128]{1,0:T(8,128)(2,1)S(1)}, bf16[512,128]{1,0:T(8,128)(2,1)S(1)}, u32[]{:S(2)}, u32[]{:S(2)}) collective-permute-start(bf16[512,128]{1,0:T(8,128)(2,1)S(1)} %get-tuple-element.70), channel_id=1, source_target_pairs={{0,8},{1,9},{2,10},{3,11},{4,12},{5,13},{6,14},{7,15}} | collective-permute-start | bytes 393224 | tf_op jit(solution)/shard_map/ppermute | solution.py:668
  41.2 2.0 %collective-permute-start.9 = (bf16[512,128]{1,0:T(8,128)(2,1)S(1)}, bf16[512,128]{1,0:T(8,128)(2,1)S(1)}, u32[]{:S(2)}, u32[]{:S(2)}) collective-permute-start(bf16[512,128]{1,0:T(8,128)(2,1)S(1)} %hop.1), channel_id=1, source_target_pairs={{8,16},{9,17},{10,18},{11,19},{12,20},{13,21},{14,22},{15,23}} | collective-permute-start | bytes 393224 | tf_op jit(solution)/shard_map/ppermute | solution.py:668
  41.9 9.0 %collective-permute-start.8 = (bf16[512,128]{1,0:T(8,128)(2,1)S(1)}, bf16[512,128]{1,0:T(8,128)(2,1)S(1)}, u32[]{:S(2)}, u32[]{:S(2)}) collective-permute-start(bf16[512,128]{1,0:T(8,128)(2,1)S(1)} %hop.1), channel_id=1, source_target_pairs={{8,24},{9,25},{10,26},{11,27},{12,28},{13,29},{14,30},{15,31}} | collective-permute-start | bytes 393224 | tf_op jit(solution)/shard_map/ppermute | solution.py:668
  52.4 6.9 %collective-permute-start.10 = (bf16[512,128]{1,0:T(8,128)(2,1)S(1)}, bf16[512,128]{1,0:T(8,128)(2,1)S(1)}, u32[]{:S(2)}, u32[]{:S(2)}) collective-permute-start(bf16[512,128]{1,0:T(8,128)(2,1)S(1)} %get-tuple-element.72), channel_id=1, source_target_pairs={{0,2},{1,3},{2,0},{3,1},{4,6},{5,7},{6,4},{7,5},{8,10},{9,11},{10,... | collective-permute-start | bytes 393224 | tf_op jit(solution)/shard_map/ppermute | solution.py:762
  53.1 7.6 %collective-permute-start.11 = (bf16[512,128]{1,0:T(8,128)(2,1)S(1)}, bf16[512,128]{1,0:T(8,128)(2,1)S(1)}, u32[]{:S(2)}, u32[]{:S(2)}) collective-permute-start(bf16[512,128]{1,0:T(8,128)(2,1)S(1)} %get-tuple-element.73), channel_id=1, source_target_pairs={{0,4},{1,5},{2,6},{3,7},{4,0},{5,1},{6,2},{7,3},{8,12},{9,13},{10,... | collective-permute-start | bytes 393224 | tf_op jit(solution)/shard_map/ppermute | solution.py:762
  53.7 8.5 %collective-permute-start.12 = (bf16[512,128]{1,0:T(8,128)(2,1)S(1)}, bf16[512,128]{1,0:T(8,128)(2,1)S(1)}, u32[]{:S(2)}, u32[]{:S(2)}) collective-permute-start(bf16[512,128]{1,0:T(8,128)(2,1)S(1)} %get-tuple-element.74), channel_id=1, source_target_pairs={{0,6},{1,7},{2,4},{3,5},{4,2},{5,3},{6,0},{7,1},{8,14},{9,15},{10,... | collective-permute-start | bytes 393224 | tf_op jit(solution)/shard_map/ppermute | solution.py:762
  55.1 9.5 %collective-permute-start.13 = (bf16[512,128]{1,0:T(8,128)(2,1)S(1)}, bf16[512,128]{1,0:T(8,128)(2,1)S(1)}, u32[]{:S(2)}, u32[]{:S(2)}) collective-permute-start(bf16[512,128]{1,0:T(8,128)(2,1)S(1)} %get-tuple-element.71.e0), channel_id=1, source_target_pairs={{0,1},{1,0},{2,3},{3,2},{4,5},{5,4},{6,7},{7,6},{8,9},{9,8},{10,11... | collective-permute-start | bytes 393224 | tf_op jit(solution)/shard_map/ppermute | solution.py:762
  59.3 5.4 %collective-permute-start.14 = (bf16[512,128]{1,0:T(8,128)(2,1)S(1)}, bf16[512,128]{1,0:T(8,128)(2,1)S(1)}, u32[]{:S(2)}, u32[]{:S(2)}) collective-permute-start(bf16[512,128]{1,0:T(8,128)(2,1)S(1)} %collective-permute-done.10.e1), channel_id=1, source_target_pairs={{0,1},{1,0},{2,3},{3,2},{4,5},{5,4},{6,7},{7,6},{8,9},{9,8},{10,11... | collective-permute-start | bytes 393224 | tf_op jit(solution)/shard_map/ppermute | solution.py:762
  60.7 3.9 %collective-permute-start.15 = (bf16[512,128]{1,0:T(8,128)(2,1)S(1)}, bf16[512,128]{1,0:T(8,128)(2,1)S(1)}, u32[]{:S(2)}, u32[]{:S(2)}) collective-permute-start(bf16[512,128]{1,0:T(8,128)(2,1)S(1)} %collective-permute-done.11.e2), channel_id=1, source_target_pairs={{0,1},{1,0},{2,3},{3,2},{4,5},{5,4},{6,7},{7,6},{8,9},{9,8},{10,11... | collective-permute-start | bytes 393224 | tf_op jit(solution)/shard_map/ppermute | solution.py:762
  62.2 2.5 %collective-permute-start.16 = (bf16[512,128]{1,0:T(8,128)(2,1)S(1)}, bf16[512,128]{1,0:T(8,128)(2,1)S(1)}, u32[]{:S(2)}, u32[]{:S(2)}) collective-permute-start(bf16[512,128]{1,0:T(8,128)(2,1)S(1)} %collective-permute-done.12.e3), channel_id=1, source_target_pairs={{0,1},{1,0},{2,3},{3,2},{4,5},{5,4},{6,7},{7,6},{8,9},{9,8},{10,11... | collective-permute-start | bytes 393224 | tf_op jit(solution)/shard_map/ppermute | solution.py:762

commit v2 on v1

--- a/solution.py
+++ b/solution.py
@@ -148,14 +148,21 @@
 
 
 def stage_kernel(
-    decay_ref, beta_ref, starts_ref, x_hbm, w_hbm, x_out, w_out, tab_ref, masks, shared, sems
+    decay_hbm, beta_hbm, starts_hbm, x_hbm, w_hbm, x_out, w_out, tab_ref, masks, shared,
+    decay_ref, beta_ref, starts_ref, sems,
 ):
-    copies = [
-        pltpu.make_async_copy(x_hbm, x_out, sems.at[0]),
-        pltpu.make_async_copy(w_hbm, w_out, sems.at[1]),
+    moves = [
+        (decay_hbm, decay_ref),
+        (beta_hbm, beta_ref),
+        (starts_hbm, starts_ref),
+        (x_hbm, x_out),
+        (w_hbm, w_out),
     ]
+    copies = [pltpu.make_async_copy(*move, sems.at[n]) for n, move in enumerate(moves)]
     for copy in copies:
         copy.start()
+    for copy in copies[:3]:
+        copy.wait()
     write_tables(decay_ref, beta_ref, starts_ref, tab_ref)
     rows = tab_ref[0]
     cols = jnp.transpose(rows)
@@ -169,19 +176,14 @@
         masks[level] = (((apart >> level) == 1) & (i > j)).astype(F32).astype(BF16)
     shared[5] = (i > j).astype(F32)
     masks[LEVELS] = (i == j).astype(F32).astype(BF16)
-    for copy in copies:
+    for copy in copies[3:]:
         copy.wait()
 
 
 def stage(decay_log, write_strength, starts, projected, conv_weight):
-    def whole(*shape):
-        return pl.BlockSpec(shape, lambda i: (0,) * len(shape))
-
     return pl.pallas_call(
         stage_kernel,
-        grid=(1,),
-        in_specs=[whole(HV, TOK), whole(HV, TOK), whole(1, TOK)]
-        + [pl.BlockSpec(memory_space=pl.ANY)] * 2,
+        in_specs=[pl.BlockSpec(memory_space=pl.ANY)] * 5,
         out_specs=[whole_spec()] * 5,
         out_shape=[
             jax.ShapeDtypeStruct(projected.shape, BF16),
@@ -190,7 +192,12 @@
             jax.ShapeDtypeStruct((LEVELS + 1, TOK, TOK), BF16),
             jax.ShapeDtypeStruct((6, TOK, 128), F32),
         ],
-        scratch_shapes=[pltpu.SemaphoreType.DMA((2,))],
+        scratch_shapes=[
+            pltpu.VMEM((HV, TOK), F32),
+            pltpu.VMEM((HV, TOK), F32),
+            pltpu.VMEM((1, TOK), jnp.int32),
+            pltpu.SemaphoreType.DMA((5,)),
+        ],
         compiler_params=params(),
         cost_estimate=pl.CostEstimate(flops=10**7, bytes_accessed=4 * 2**20, transcendentals=0),
         name="stage",
@@ -560,48 +567,49 @@
     )(meta, mine, other)
 
 
-def plane_kernel(meta, x0, x1, x2, x3, prefix_ref, plane_ref, exit_ref, maps, sems):
-    copies = []
-    for m, x in enumerate((x0, x1, x2, x3)):
-        copy = pltpu.make_async_copy(x, maps.at[meta[3] ^ m], sems.at[m])
-        copy.start()
-        copies.append(copy)
-    prefix_ref[0, 0 : GROUP * DK, :] = jnp.zeros((GROUP * DK, 256), BF16)
-    ones = jnp.ones((1, 256), F32)
-    prefix_ref[0, GROUP * DK : ROWS, :] = split_rows([ones] * GROUP)
-    for copy in copies:
-        copy.wait()
-    prefix_ref[1] = maps[0]
-    run = [maps[0, h * DK : (h + 1) * DK, :].astype(F32) for h in range(GROUP)]
-    run_c = [factor(maps[0, GROUP * DK : ROWS, :], h) for h in range(GROUP)]
-    for a in range(1, 4):
-        tail = maps[a, GROUP * DK : ROWS, :]
-        for h in range(GROUP):
-            here = slice(h * DK, (h + 1) * DK)
-            c = factor(tail, h)
-            run[h] = compose(run[h], run_c[h], maps[a, here, :], c)
-            run_c[h] = run_c[h] * c
+def by_place(meta, body):
+    for place in range(4):
+        pl.when(meta[3] == place)(functools.partial(body, place))
+
+
+def plane_kernel(meta, x0, x1, x2, x3, prefix_ref, plane_ref, exit_ref):
+    pieces = (x0, x1, x2, x3)
+    prefix_ref[0] = jnp.zeros((ROWS, 256), BF16)
+
+    def chain(place):
+        maps = [pieces[place ^ a] for a in range(4)]
+        prefix_ref[1] = maps[0][...]
+        run = [maps[0][h * DK : (h + 1) * DK, :].astype(F32) for h in range(GROUP)]
+        run_c = [factor(maps[0][GROUP * DK : ROWS, :], h) for h in range(GROUP)]
+        for a in range(1, 4):
+            tail = maps[a][GROUP * DK : ROWS, :]
+            for h in range(GROUP):
+                here = slice(h * DK, (h + 1) * DK)
+                c = factor(tail, h)
+                run[h] = compose(run[h], run_c[h], maps[a][here, :], c)
+                run_c[h] = run_c[h] * c
+                if a < 3:
+                    prefix_ref[a + 1, here, :] = run[h].astype(BF16)
+                else:
+                    plane_ref[here, :] = run[h].astype(BF16)
+                    exit_ref[here, :] = run[h][:, DK:].astype(BF16)
             if a < 3:
-                prefix_ref[a + 1, here, :] = run[h].astype(BF16)
-            else:
-                plane_ref[here, :] = run[h].astype(BF16)
-                exit_ref[here, :] = run[h][:, DK:].astype(BF16)
-        if a < 3:
-            prefix_ref[a + 1, GROUP * DK : ROWS, :] = split_rows(run_c)
-    plane_ref[GROUP * DK : ROWS, :] = split_rows(run_c)
+                prefix_ref[a + 1, GROUP * DK : ROWS, :] = split_rows(run_c)
+        plane_ref[GROUP * DK : ROWS, :] = split_rows(run_c)
+
+    by_place(meta, chain)
 
 
 def plane_maps(meta, pieces):
     return pl.pallas_call(
         plane_kernel,
-        in_specs=[smem_spec()] + [pl.BlockSpec(memory_space=pl.ANY)] * 4,
+        in_specs=[smem_spec()] + [whole_spec()] * 4,
         out_specs=[whole_spec()] * 3,
         out_shape=[
             jax.ShapeDtypeStruct((4, ROWS, 256), BF16),
             jax.ShapeDtypeStruct((ROWS, 256), BF16),
             jax.ShapeDtypeStruct((GROUP * DK, DV), BF16),
         ],
-        scratch_shapes=[pltpu.VMEM((4, ROWS, 256), BF16), pltpu.SemaphoreType.DMA((4,))],
         compiler_params=params(),
         cost_estimate=pl.CostEstimate(
             flops=12 * 2 * 2 * 128**3, bytes_accessed=2 * 2**20, transcendentals=0
@@ -636,16 +644,21 @@
     out_refs = refs[-4:]
     state_refs = refs[:-4]
     before_tail = before_ref[GROUP * DK : ROWS, :]
-    for h in range(GROUP):
-        here = slice(h * DK, (h + 1) * DK)
-        state = apply_map(before_ref[here, :], factor(before_tail, h), far_ref[here, :])
-        state = state.astype(BF16)
-        for ref in state_refs:
-            state = state + ref[here, :]
-        for m, out_ref in enumerate(out_refs):
-            a = meta[3] ^ m
-            c = factor(prefix_ref[a, GROUP * DK : ROWS, :], h)
-            out_ref[here, :] = apply_map(prefix_ref[a, here, :], c, state).astype(BF16)
+
+    def send(place):
+        for h in range(GROUP):
+            here = slice(h * DK, (h + 1) * DK)
+            state = apply_map(before_ref[here, :], factor(before_tail, h), far_ref[here, :])
+            state = state.astype(BF16)
+            for ref in state_refs:
+                state = state + ref[here, :]
+            out_refs[place][here, :] = state
+            for a in range(1, 4):
+                c = factor(prefix_ref[a, GROUP * DK : ROWS, :], h)
+                after = apply_map(prefix_ref[a, here, :], c, state)
+                out_refs[place ^ a][here, :] = after.astype(BF16)
+
+    by_place(meta, send)
 
 
 def spread(meta, prefix, before, far, states):
@@ -683,70 +696,69 @@
     return jnp.zeros_like(plane_map), jnp.zeros_like(leaving), states
 
 
-def read_out(meta, r_ref, d_ref, e_refs, rows):
-    for m, e_ref in enumerate(e_refs):
-        g = meta[3] ^ m
+def read_group(g, parts, out):
+    for n, (r_ref, d_ref, e_ref) in enumerate(parts):
         for h in range(GROUP):
             here = slice(h * TOK, (h + 1) * TOK)
             total = dot(r_ref[g, here, :], e_ref[here, :]) + d_ref[g, here, :]
-            rows[g, :, h * DV : (h + 1) * DV] = total.astype(BF16)
-        yield m, g
-
-
-def half_kernel(meta, r_ref, d_ref, e0, e1, e2, e3, rows):
-    for _ in read_out(meta, r_ref, d_ref, (e0, e1, e2, e3), rows):
-        pass
-
-
-def read_half(meta, reads, direct, states):
-    return pl.pallas_call(
-        half_kernel,
+            out[n, :, h * DV : (h + 1) * DV] = total.astype(BF16)
+
+
+def group_kernel(m, meta, r_k, d_k, e_k, r_s, d_s, e_s, out):
+    read_group(meta[3] ^ m, ((r_k, d_k, e_k), (r_s, d_s, e_s)), out)
+
+
+def group_cost():
+    return pl.CostEstimate(flops=8 * 2 * 128**3, bytes_accessed=2**20, transcendentals=0)
+
+
+def read_out(m, meta, *parts):
+    return pl.pallas_call(
+        functools.partial(group_kernel, m),
         in_specs=[smem_spec()] + [whole_spec()] * 6,
         out_specs=whole_spec(),
-        out_shape=jax.ShapeDtypeStruct((4, TOK, GROUP * DV), BF16),
-        compiler_params=params(),
-        cost_estimate=pl.CostEstimate(
-            flops=16 * 2 * 128**3, bytes_accessed=3 * 2**20, transcendentals=0
-        ),
-        name="half",
-    )(meta, reads, direct, *states)
-
-
-def emit_kernel(meta, kept, r_ref, d_ref, e0, e1, e2, e3, out_ref, rows, sems):
+        out_shape=jax.ShapeDtypeStruct((2, TOK, GROUP * DV), BF16),
+        compiler_params=params(),
+        cost_estimate=group_cost(),
+        name="group",
+    )(meta, *parts)
+
+
+def emit_kernel(meta, g0, g1, g2, r_k, d_k, e_k, r_s, d_s, e_s, out_ref, rows, sems):
     copies = []
 
-    def put(source, n, slot, g):
-        start = pl.multiple_of((meta[slot] + g) * (GROUP * DV), GROUP * DV)
-        copy = pltpu.make_async_copy(
-            source.at[g], out_ref.at[:, pl.ds(start, GROUP * DV)], sems.at[n]
-        )
-        copy.start()
-        copies.append(copy)
-
-    for g in range(4):
-        put(kept, g, 1, g)
-    for m, g in read_out(meta, r_ref, d_ref, (e0, e1, e2, e3), rows):
-        put(rows, 4 + m, 0, g)
+    def put(source, m):
+        g = meta[3] ^ m
+        for n in range(2):
+            start = pl.multiple_of((meta[1 - n] + g) * (GROUP * DV), GROUP * DV)
+            copy = pltpu.make_async_copy(
+                source.at[n], out_ref.at[:, pl.ds(start, GROUP * DV)], sems.at[2 * m + n]
+            )
+            copy.start()
+            copies.append(copy)
+
+    for m, group in enumerate((g0, g1, g2)):
+        put(group, m)
+    read_group(meta[3] ^ 3, ((r_k, d_k, e_k), (r_s, d_s, e_s)), rows)
+    put(rows, 3)
     for copy in copies:
         copy.wait()
 
 
-def emit(meta, kept, reads, direct, states):
+def emit(meta, *parts):
     return pl.pallas_call(
         emit_kernel,
-        in_specs=[smem_spec()] + [whole_spec()] * 7,
+        in_specs=[smem_spec()] + [whole_spec()] * 9,
         out_specs=pl.BlockSpec(memory_space=pl.ANY),
         out_shape=jax.ShapeDtypeStruct((TOK, HV * DV), BF16),
         scratch_shapes=[
-            pltpu.VMEM((4, TOK, GROUP * DV), BF16),
+            pltpu.VMEM((2, TOK, GROUP * DV), BF16),
             pltpu.SemaphoreType.DMA((8,)),
         ],
         compiler_params=params(),
-        cost_estimate=pl.CostEstimate(
-            flops=16 * 2 * 128**3, bytes_accessed=3 * 2**20, transcendentals=0
-        ),
+        cost_estimate=group_cost(),
         name="emit",
-    )(meta, kept, reads, direct, *states)
+    )(meta, *parts)
 
 
 def shards(projected, conv_weight, decay_log, write_strength, starts):
@@ -782,11 +794,14 @@
     prefix, plane_map, leaving = plane_maps(meta, (x0, x1, x2, x3))
     before, far, arrived = entering_states(plane_map, leaving, count // 8)
     e0, e1, e2, e3 = spread(meta, prefix, before, far, arrived)
-    e3, e1, e2 = exchange(e3, 6), exchange(e1, 2), exchange(e2, 4)
-    states = (e0, e1, e2, e3)
+    states = [e0, e1, e2, e3]
+    for m in range(1, 4):
+        states[m] = exchange(states[m], 2 * m)
     partner = [exchange(e, 1) for e in states]
-    kept = read_half(meta, r_k, d_k, states)
-    return emit(meta, kept, r_s, d_s, partner)
+    groups = []
+    for m in range(3):
+        groups.append(read_out(m, meta, r_k, d_k, states[m], r_s, d_s, partner[m]))
+    return emit(meta, *groups, r_k, d_k, states[3], r_s, d_s, partner[3])
 
 
 def solution(mesh):

time: 66.9 us -> 68 us (1.016)
    pallas_call x4 -> x6, Pallas kernels: 6.23 us -> 6.75 us  [the longest x3 2.28 us: read_out(): pl.pallas_call(functools.partial(group_kernel, m), in_specs=[smem_spec()]...]
  transfers between devices with their start and end apart: 17 -> 17, of which waited for: 3 -> 2; matrix products, arithmetic and copies ran while one was open for 0% -> 0% of each run, Pallas kernels for 27% -> 27%
where the time goes in v2:
time: 68 us; the launch traced here: 67.7 us
  Pallas kernels  32.8 us (48%)
  starting transfers between devices  24.4 us (36%)
  waiting for transfers between devices  10 us (15%)
    ppermute x12, starting transfers between devices, exchange(): return lax.ppermute(block, 'seq', [(i, i ^ bits) for i in range(count)])  16.8 us
    pallas_call x2, Pallas kernels, make_reads(): pl.pallas_call(read_kernel, grid_spec=pltpu.PrefetchScalarGridSpec(num_sc...  8.45 us
    ppermute x4, waiting for transfers between devices, ahead(): return lax.ppermute(block, 'seq', [(i, i + 8 * distance) for i in members])  7.7 us
    pallas_call x1, Pallas kernels, send_maps(): pl.pallas_call(send_kernel, in_specs=[smem_spec()] + [whole_spec()] * len...  7.52 us
    pallas_call x1, Pallas kernels, keep_maps(): pl.pallas_call(keep_kernel, in_specs=[smem_spec()] + [whole_spec()] * len...  5.94 us
    ppermute x4, starting transfers between devices, ahead(): return lax.ppermute(block, 'seq', [(i, i + 8 * distance) for i in members])  3.92 us
    ppermute x1, starting transfers between devices, shards(): lax.ppermute(tail_rows, 'seq', [(i, i + 1) for i in range(count - 1)])  3.68 us
    ppermute x12, waiting for transfers between devices, exchange(): return lax.ppermute(block, 'seq', [(i, i ^ bits) for i in range(count)])  2.34 us
  transfers between devices with their start and end apart: 17, of which 2 were waited for; matrix products, arithmetic and copies ran while one was open for 0% of the time, Pallas kernels for 27%

profile of v2, /device:TPU:25, one launch (start us, length us, event | category | flops | bytes accessed | tf_op | source)
XLA Modules:
  0.0 67.7 jit_solution(4049130211802366560)
XLA Ops:
  0.0 1.1 %tail.1 = bf16[3,8192]{1,0:T(4,128)(2,1)S(1)} custom-call(s32[1,128]{1,0:T(1,128)} %bitcast.1, bf16[128,8192]{1,0:T(8,128)(2,1)} %x_ref.1), custom_call_target="tpu_custom_call" | custom-call | flops 100000 | bytes 1000000 | tf_op jit(solution)/shard_map/tail/pallas_call | solution.py:59
  1.1 3.7 %collective-permute-start = (bf16[3,8192]{1,0:T(4,128)(2,1)S(1)}, bf16[3,8192]{1,0:T(4,128)(2,1)S(1)}, u32[]{:S(2)}, u32[]{:S(2)}) collective-permute-start(bf16[3,8192]{1,0:T(4,128)(2,1)S(1)} %tail.1), channel_id=1, source_target_pairs={{0,1},{1,2},{2,3},{3,4},{4,5},{5,6},{6,7},{7,8},{8,9},{9,10},{10,1... | collective-permute-start | bytes 147464 | tf_op jit(solution)/shard_map/ppermute | solution.py:778
  4.9 1.7 %stage.1 = (bf16[128,8192]{1,0:T(8,128)(2,1)S(1)}, bf16[4,8192]{1,0:T(4,128)(2,1)S(1)}, f32[8,16,128]{2,1,0:T(8,128)S(1)}, bf16[8,128,128]{2,1,0:T(8,128)(2,1)S(1)}, f32[6,128,128]{2,1,0:T(8,128)S(1)}) custom-call(f32[32,128]{1,0:T(8,128)} %decay_hbm.1, f32[32,128]{1,0:T(8,128)} %beta_hbm.1, s32[1,128]{1,0:T(1,128)} %bitcast.2, bf16[128,8192]{1,0:T(8,128)(2,1)} %x_ref.1, ...), custom_call_target="tpu_custom_call" | custom-call | flops 10000000 | bytes 4194304 | tf_op jit(solution)/shard_map/stage/pallas_call | solution.py:184
  6.6 0.0 collective-permute-done.halo_ref.hq_ref
  6.6 7.5 %send_maps.1 = (bf16[4,528,256]{2,1,0:T(8,128)(2,1)S(1)}, bf16[4,256,128]{2,1,0:T(8,128)(2,1)S(1)}, bf16[4,512,256]{2,1,0:T(8,128)(2,1)S(1)}, bf16[8,128,128]{2,...) custom-call(s32[8]{0:T(128)S(1)} %compare_select_fusion.4.meta, ...), custom_call_target="tpu_custom_call" | custom-call | flops 1342177280 | bytes 5242880 | tf_op jit(solution)/shard_map/send_maps/pallas_call | solution.py:414
  14.1 2.7 %collective-permute-start.1 = (bf16[4,528,256]{2,1,0:T(8,128)(2,1)S(1)}, bf16[4,528,256]{2,1,0:T(8,128)(2,1)S(1)}, u32[]{:S(2)}, u32[]{:S(2)}) collective-permute-start(bf16[4,528,256]{2,1,0:T(8,128)(2,1)S(1)} %get-tuple-element.50), channel_id=1, source_target_pairs={{0,1},{1,0},{2,3},{3,2},{4,5},{5,4},{6,7},{7,6},{8,9},{9,8},{10,11... | collective-permute-start | bytes 3244040 | tf_op jit(solution)/shard_map/ppermute | solution.py:774
  16.8 5.9 %keep_maps.1 = (bf16[4,528,256]{2,1,0:T(8,128)(2,1)S(1)}, bf16[4,256,128]{2,1,0:T(8,128)(2,1)S(1)}, bf16[4,512,256]{2,1,0:T(8,128)(2,1)S(1)}) custom-call(s32[8]{0:T(128)S(1)} %compare_select_fusion.4.meta, bf16[128,8192]{1,0:T(8,128)(2,1)S(1)} %get-tuple-element.41.x_ref.xq_ref, bf16[3,8192]{1,0:T(4,128)(2,1)S(1)} %collective-permute-done.halo_ref.hq_ref, ...), custom_call_target="tpu_custom_call" | custom-call | flops 1342177280 | bytes 5242880 | tf_op jit(solution)/shard_map/keep_maps/pallas_call | solution.py:432
  22.7 0.0 collective-permute-done.1.other_ref.left_ref
  22.7 1.4 %pair.1 = (bf16[528,256]{1,0:T(8,128)(2,1)S(1)}, bf16[528,256]{1,0:T(8,128)(2,1)S(1)}, bf16[528,256]{1,0:T(8,128)(2,1)S(1)}, bf16[528,256]{1,0:T(8,128)(2,1)S(1)}) custom-call(s32[8]{0:T(128)S(1)} %compare_select_fusion.4.meta, bf16[4,528,256]{2,1,0:T(8,128)(2,1)S(1)} %get-tuple-element.59.mine_ref, ...), custom_call_target="tpu_custom_call" | custom-call | flops 134217728 | bytes 3145728 | tf_op jit(solution)/shard_map/pair/pallas_call | solution.py:557
  24.1 0.1 collective-permute-start.2
  24.2 0.1 collective-permute-start.3
  24.3 0.6 collective-permute-start.4
  24.9 2.0 %collective-permute-start.5 = (bf16[528,256]{1,0:T(8,128)(2,1)S(1)}, bf16[528,256]{1,0:T(8,128)(2,1)S(1)}, u32[]{:S(2)}, u32[]{:S(2)}) collective-permute-start(bf16[528,256]{1,0:T(8,128)(2,1)S(1)} %get-tuple-element.67), channel_id=1, source_target_pairs={{0,6},{1,7},{2,4},{3,5},{4,2},{5,3},{6,0},{7,1},{8,14},{9,15},{10,... | collective-permute-start | bytes 811016 | tf_op jit(solution)/shard_map/ppermute | solution.py:774
  26.9 4.2 %reads.2 = (bf16[4,512,128]{2,1,0:T(8,128)(2,1)S(1)}, f32[4,512,128]{2,1,0:T(8,128)S(1)}) custom-call(s32[8]{0:T(128)S(1)} %compare_select_fusion.4.meta, bf16[128,8192]{1,0:T(8,128)(2,1)S(1)} %get-tuple-element.41.x_ref.xq_ref, bf16[3,8192]{1,0:T(4,128)(2,1)S(1)} %collective-permute-done.halo_ref.hq_ref, ...), custom_call_target="tpu_custom_call" | custom-call | flops 402653184 | bytes 5242880 | tf_op jit(solution)/shard_map/reads/pallas_call | solution.py:483
  31.2 0.0 collective-permute-done.2.left_ref
  31.2 4.2 %reads.3 = (bf16[4,512,128]{2,1,0:T(8,128)(2,1)S(1)}, f32[4,512,128]{2,1,0:T(8,128)S(1)}) custom-call(s32[8]{0:T(128)S(1)} %compare_select_fusion.4.meta, bf16[128,8192]{1,0:T(8,128)(2,1)S(1)} %get-tuple-element.41.x_ref.xq_ref, bf16[3,8192]{1,0:T(4,128)(2,1)S(1)} %collective-permute-done.halo_ref.hq_ref, ...), custom_call_target="tpu_custom_call" | custom-call | flops 402653184 | bytes 5242880 | tf_op jit(solution)/shard_map/reads/pallas_call | solution.py:483
  35.4 0.0 collective-permute-done.3.x1
  35.4 0.0 collective-permute-done.4.x2
  35.4 2.3 %collective-permute-done.5.x3 = bf16[528,256]{1,0:T(8,128)(2,1)S(1)} collective-permute-done((bf16[528,256]{1,0:T(8,128)(2,1)S(1)}, bf16[528,256]{1,0:T(8,128)(2,1)S(1)}, u32[]{:S(2)}, u32[]{:S(2)}) %collective-permute-start.5) | collective-permute-done | bytes 270368 | tf_op jit(solution)/shard_map/ppermute | solution.py:774
  37.7 1.2 %plane.1 = (bf16[4,528,256]{2,1,0:T(8,128)(2,1)S(1)}, bf16[528,256]{1,0:T(8,128)(2,1)S(1)}, bf16[512,128]{1,0:T(8,128)(2,1)S(1)}) custom-call(s32[8]{0:T(128)S(1)} %compare_select_fusion.4.meta, bf16[528,256]{1,0:T(8,128)(2,1)S(1)} %get-tuple-element.64.x0, bf16[528,256]{1,0:T(8,128)(2,1)S(1)} %collective-permute-done.3.x1, ...), custom_call_target="tpu_custom_call" | custom-call | flops 100663296 | bytes 2097152 | tf_op jit(solution)/shard_map/plane/pallas_call | solution.py:604
  38.9 1.3 %collective-permute-start.6 = (bf16[528,256]{1,0:T(8,128)(2,1)S(1)}, bf16[528,256]{1,0:T(8,128)(2,1)S(1)}, u32[]{:S(2)}, u32[]{:S(2)}) collective-permute-start(bf16[528,256]{1,0:T(8,128)(2,1)S(1)} %get-tuple-element.69.plane_ref), channel_id=1, source_target_pairs={{16,24},{17,25},{18,26},{19,27},{20,28},{21,29},{22,30},{23,31}} | collective-permute-start | bytes 811016 | tf_op jit(solution)/shard_map/ppermute | solution.py:681
  40.2 0.7 collective-permute-start.7
  40.9 0.0 collective-permute-done.7.state_ref.refs_0_
  40.9 0.2 hop.1
  41.1 0.7 collective-permute-start.9
  41.7 1.3 %collective-permute-start.8 = (bf16[512,128]{1,0:T(8,128)(2,1)S(1)}, bf16[512,128]{1,0:T(8,128)(2,1)S(1)}, u32[]{:S(2)}, u32[]{:S(2)}) collective-permute-start(bf16[512,128]{1,0:T(8,128)(2,1)S(1)} %hop.1), channel_id=1, source_target_pairs={{8,24},{9,25},{10,26},{11,27},{12,28},{13,29},{14,30},{15,31}} | collective-permute-start | bytes 393224 | tf_op jit(solution)/shard_map/ppermute | solution.py:681
  43.0 0.0 collective-permute-done.9.refs_1_
  43.1 7.7 %collective-permute-done.8.far_ref = bf16[512,128]{1,0:T(8,128)(2,1)S(1)} collective-permute-done((bf16[512,128]{1,0:T(8,128)(2,1)S(1)}, bf16[512,128]{1,0:T(8,128)(2,1)S(1)}, u32[]{:S(2)}, u32[]{:S(2)}) %collective-permute-start.8) | collective-permute-done | bytes 131104 | tf_op jit(solution)/shard_map/ppermute | solution.py:681
  50.7 0.0 collective-permute-done.6.before_ref
  50.7 1.4 %spread.1 = (bf16[512,128]{1,0:T(8,128)(2,1)S(1)}, bf16[512,128]{1,0:T(8,128)(2,1)S(1)}, bf16[512,128]{1,0:T(8,128)(2,1)S(1)}, bf16[512,128]{1,0:T(8,128)(2,1)S(1)}) custom-call(s32[8]{0:T(128)S(1)} %compare_select_fusion.4.meta, bf16[4,528,256]{2,1,0:T(8,128)(2,1)S(1)} %get-tuple-element.68.prefix_ref, ...), custom_call_target="tpu_custom_call" | custom-call | flops 83886080 | bytes 2097152 | tf_op jit(solution)/shard_map/spread/pallas_call | solution.py:665
  52.2 0.2 collective-permute-start.11
  52.4 1.1 %collective-permute-start.13 = (bf16[512,128]{1,0:T(8,128)(2,1)S(1)}, bf16[512,128]{1,0:T(8,128)(2,1)S(1)}, u32[]{:S(2)}, u32[]{:S(2)}) collective-permute-start(bf16[512,128]{1,0:T(8,128)(2,1)S(1)} %get-tuple-element.75), channel_id=1, source_target_pairs={{0,4},{1,5},{2,6},{3,7},{4,0},{5,1},{6,2},{7,3},{8,12},{9,13},{10,... | collective-permute-start | bytes 393224 | tf_op jit(solution)/shard_map/ppermute | solution.py:774
  53.5 1.4 %collective-permute-start.15 = (bf16[512,128]{1,0:T(8,128)(2,1)S(1)}, bf16[512,128]{1,0:T(8,128)(2,1)S(1)}, u32[]{:S(2)}, u32[]{:S(2)}) collective-permute-start(bf16[512,128]{1,0:T(8,128)(2,1)S(1)} %get-tuple-element.76), channel_id=1, source_target_pairs={{0,6},{1,7},{2,4},{3,5},{4,2},{5,3},{6,0},{7,1},{8,14},{9,15},{10,... | collective-permute-start | bytes 393224 | tf_op jit(solution)/shard_map/ppermute | solution.py:774
  54.9 4.2 %collective-permute-start.10 = (bf16[512,128]{1,0:T(8,128)(2,1)S(1)}, bf16[512,128]{1,0:T(8,128)(2,1)S(1)}, u32[]{:S(2)}, u32[]{:S(2)}) collective-permute-start(bf16[512,128]{1,0:T(8,128)(2,1)S(1)} %get-tuple-element.71.e_k), channel_id=1, source_target_pairs={{0,1},{1,0},{2,3},{3,2},{4,5},{5,4},{6,7},{7,6},{8,9},{9,8},{10,11... | collective-permute-start | bytes 393224 | tf_op jit(solution)/shard_map/ppermute | solution.py:774
  59.0 0.0 collective-permute-done.11.e_k
  59.1 1.5 %collective-permute-start.12 = (bf16[512,128]{1,0:T(8,128)(2,1)S(1)}, bf16[512,128]{1,0:T(8,128)(2,1)S(1)}, u32[]{:S(2)}, u32[]{:S(2)}) collective-permute-start(bf16[512,128]{1,0:T(8,128)(2,1)S(1)} %collective-permute-done.11.e_k), channel_id=1, source_target_pairs={{0,1},{1,0},{2,3},{3,2},{4,5},{5,4},{6,7},{7,6},{8,9},{9,8},{10,11... | collective-permute-start | bytes 393224 | tf_op jit(solution)/shard_map/ppermute | solution.py:774
  60.5 0.0 collective-permute-done.13.e_k
  60.5 1.5 %collective-permute-start.14 = (bf16[512,128]{1,0:T(8,128)(2,1)S(1)}, bf16[512,128]{1,0:T(8,128)(2,1)S(1)}, u32[]{:S(2)}, u32[]{:S(2)}) collective-permute-start(bf16[512,128]{1,0:T(8,128)(2,1)S(1)} %collective-permute-done.13.e_k), channel_id=1, source_target_pairs={{0,1},{1,0},{2,3},{3,2},{4,5},{5,4},{6,7},{7,6},{8,9},{9,8},{10,11... | collective-permute-start | bytes 393224 | tf_op jit(solution)/shard_map/ppermute | solution.py:774
  62.0 0.0 collective-permute-done.15.e_k
  62.0 1.5 %collective-permute-start.16 = (bf16[512,128]{1,0:T(8,128)(2,1)S(1)}, bf16[512,128]{1,0:T(8,128)(2,1)S(1)}, u32[]{:S(2)}, u32[]{:S(2)}) collective-permute-start(bf16[512,128]{1,0:T(8,128)(2,1)S(1)} %collective-permute-done.15.e_k), channel_id=1, source_target_pairs={{0,1},{1,0},{2,3},{3,2},{4,5},{5,4},{6,7},{7,6},{8,9},{9,8},{10,11... | collective-permute-start | bytes 393224 | tf_op jit(solution)/shard_map/ppermute | solution.py:774
  63.5 0.0 collective-permute-done.10.e_s
  63.5 0.8 %group.3.g0 = bf16[2,128,512]{2,1,0:T(8,128)(2,1)S(1)} custom-call(s32[8]{0:T(128)S(1)} %compare_select_fusion.4.meta, bf16[4,512,128]{2,1,0:T(8,128)(2,1)S(1)} %get-tuple-element.62.r_k, f32[4,512,128]{2,1,0:T(8,128)S(1)} %get-tuple-element.63.d_k, bf16[512,128]{1,0:T(8,128)(2,1)S(1)} %get-tuple-element.71.e_k, ...), custom_call_target="tpu_custom_call" | custom-call | flops 33554432 | bytes 1048576 | tf_op jit(solution)/shard_map/group/pallas_call | solution.py:716
  64.3 0.0 collective-permute-done.12.e_s
  64.3 0.8 %group.4.g1 = bf16[2,128,512]{2,1,0:T(8,128)(2,1)S(1)} custom-call(s32[8]{0:T(128)S(1)} %compare_select_fusion.4.meta, bf16[4,512,128]{2,1,0:T(8,128)(2,1)S(1)} %get-tuple-element.62.r_k, f32[4,512,128]{2,1,0:T(8,128)S(1)} %get-tuple-element.63.d_k, bf16[512,128]{1,0:T(8,128)(2,1)S(1)} %collective-permute-done.11.e_k, ...), custom_call_target="tpu_custom_call" | custom-call | flops 33554432 | bytes 1048576 | tf_op jit(solution)/shard_map/group/pallas_call | solution.py:716
  65.1 0.0 collective-permute-done.14.e_s
  65.1 0.8 %group.5.g2 = bf16[2,128,512]{2,1,0:T(8,128)(2,1)S(1)} custom-call(s32[8]{0:T(128)S(1)} %compare_select_fusion.4.meta, bf16[4,512,128]{2,1,0:T(8,128)(2,1)S(1)} %get-tuple-element.62.r_k, f32[4,512,128]{2,1,0:T(8,128)S(1)} %get-tuple-element.63.d_k, bf16[512,128]{1,0:T(8,128)(2,1)S(1)} %collective-permute-done.13.e_k, ...), custom_call_target="tpu_custom_call" | custom-call | flops 33554432 | bytes 1048576 | tf_op jit(solution)/shard_map/group/pallas_call | solution.py:716
  65.9 0.0 collective-permute-done.16.e_s
  65.9 1.6 %emit.1 = bf16[128,4096]{1,0:T(8,128)(2,1)} custom-call(s32[8]{0:T(128)S(1)} %compare_select_fusion.4.meta, bf16[2,128,512]{2,1,0:T(8,128)(2,1)S(1)} %group.3.g0, bf16[2,128,512]{2,1,0:T(8,128)(2,1)S(1)} %group.4.g1, bf16[2,128,512]{2,1,0:T(8,128)(2,1)S(1)} %group.5.g2, bf16[4,512,128]{2,1,0:T(8,128)(2,1)S(1)} %get-tuple-element.62.r_k, ...), custom_call_target="tpu_custom_call" | custom-call | flops 33554432 | bytes 1048576 | tf_op jit(solution)/shard_map/emit/pallas_call | solution.py:749
  (1 shorter events, 0.0 us)
Async XLA Ops:
  1.1 5.4 %collective-permute-start = (bf16[3,8192]{1,0:T(4,128)(2,1)S(1)}, bf16[3,8192]{1,0:T(4,128)(2,1)S(1)}, u32[]{:S(2)}, u32[]{:S(2)}) collective-permute-start(bf16[3,8192]{1,0:T(4,128)(2,1)S(1)} %tail.1), channel_id=1, source_target_pairs={{0,1},{1,2},{2,3},{3,4},{4,5},{5,6},{6,7},{7,8},{8,9},{9,10},{10,1... | collective-permute-start | bytes 147464 | tf_op jit(solution)/shard_map/ppermute | solution.py:778
  14.1 8.6 %collective-permute-start.1 = (bf16[4,528,256]{2,1,0:T(8,128)(2,1)S(1)}, bf16[4,528,256]{2,1,0:T(8,128)(2,1)S(1)}, u32[]{:S(2)}, u32[]{:S(2)}) collective-permute-start(bf16[4,528,256]{2,1,0:T(8,128)(2,1)S(1)} %get-tuple-element.50), channel_id=1, source_target_pairs={{0,1},{1,0},{2,3},{3,2},{4,5},{5,4},{6,7},{7,6},{8,9},{9,8},{10,11... | collective-permute-start | bytes 3244040 | tf_op jit(solution)/shard_map/ppermute | solution.py:774
  24.1 7.0 %collective-permute-start.2 = (bf16[4,528,256]{2,1,0:T(8,128)(2,1)S(1)}, bf16[4,528,256]{2,1,0:T(8,128)(2,1)S(1)}, u32[]{:S(2)}, u32[]{:S(2)}) collective-permute-start(bf16[4,528,256]{2,1,0:T(8,128)(2,1)S(1)} %get-tuple-element.59.mine_ref), channel_id=1, source_target_pairs={{0,1},{1,0},{2,3},{3,2},{4,5},{5,4},{6,7},{7,6},{8,9},{9,8},{10,11... | collective-permute-start | bytes 3244040 | tf_op jit(solution)/shard_map/ppermute | solution.py:774
  24.2 11.2 %collective-permute-start.3 = (bf16[528,256]{1,0:T(8,128)(2,1)S(1)}, bf16[528,256]{1,0:T(8,128)(2,1)S(1)}, u32[]{:S(2)}, u32[]{:S(2)}) collective-permute-start(bf16[528,256]{1,0:T(8,128)(2,1)S(1)} %get-tuple-element.65), channel_id=1, source_target_pairs={{0,2},{1,3},{2,0},{3,1},{4,6},{5,7},{6,4},{7,5},{8,10},{9,11},{10,... | collective-permute-start | bytes 811016 | tf_op jit(solution)/shard_map/ppermute | solution.py:774
  24.3 11.1 %collective-permute-start.4 = (bf16[528,256]{1,0:T(8,128)(2,1)S(1)}, bf16[528,256]{1,0:T(8,128)(2,1)S(1)}, u32[]{:S(2)}, u32[]{:S(2)}) collective-permute-start(bf16[528,256]{1,0:T(8,128)(2,1)S(1)} %get-tuple-element.66), channel_id=1, source_target_pairs={{0,4},{1,5},{2,6},{3,7},{4,0},{5,1},{6,2},{7,3},{8,12},{9,13},{10,... | collective-permute-start | bytes 811016 | tf_op jit(solution)/shard_map/ppermute | solution.py:774
  24.9 12.8 %collective-permute-start.5 = (bf16[528,256]{1,0:T(8,128)(2,1)S(1)}, bf16[528,256]{1,0:T(8,128)(2,1)S(1)}, u32[]{:S(2)}, u32[]{:S(2)}) collective-permute-start(bf16[528,256]{1,0:T(8,128)(2,1)S(1)} %get-tuple-element.67), channel_id=1, source_target_pairs={{0,6},{1,7},{2,4},{3,5},{4,2},{5,3},{6,0},{7,1},{8,14},{9,15},{10,... | collective-permute-start | bytes 811016 | tf_op jit(solution)/shard_map/ppermute | solution.py:774
  38.9 11.9 %collective-permute-start.6 = (bf16[528,256]{1,0:T(8,128)(2,1)S(1)}, bf16[528,256]{1,0:T(8,128)(2,1)S(1)}, u32[]{:S(2)}, u32[]{:S(2)}) collective-permute-start(bf16[528,256]{1,0:T(8,128)(2,1)S(1)} %get-tuple-element.69.plane_ref), channel_id=1, source_target_pairs={{16,24},{17,25},{18,26},{19,27},{20,28},{21,29},{22,30},{23,31}} | collective-permute-start | bytes 811016 | tf_op jit(solution)/shard_map/ppermute | solution.py:681
  40.2 0.7 %collective-permute-start.7 = (bf16[512,128]{1,0:T(8,128)(2,1)S(1)}, bf16[512,128]{1,0:T(8,128)(2,1)S(1)}, u32[]{:S(2)}, u32[]{:S(2)}) collective-permute-start(bf16[512,128]{1,0:T(8,128)(2,1)S(1)} %get-tuple-element.70), channel_id=1, source_target_pairs={{0,8},{1,9},{2,10},{3,11},{4,12},{5,13},{6,14},{7,15}} | collective-permute-start | bytes 393224 | tf_op jit(solution)/shard_map/ppermute | solution.py:681
  41.1 2.0 %collective-permute-start.9 = (bf16[512,128]{1,0:T(8,128)(2,1)S(1)}, bf16[512,128]{1,0:T(8,128)(2,1)S(1)}, u32[]{:S(2)}, u32[]{:S(2)}) collective-permute-start(bf16[512,128]{1,0:T(8,128)(2,1)S(1)} %hop.1), channel_id=1, source_target_pairs={{8,16},{9,17},{10,18},{11,19},{12,20},{13,21},{14,22},{15,23}} | collective-permute-start | bytes 393224 | tf_op jit(solution)/shard_map/ppermute | solution.py:681
  41.7 9.0 %collective-permute-start.8 = (bf16[512,128]{1,0:T(8,128)(2,1)S(1)}, bf16[512,128]{1,0:T(8,128)(2,1)S(1)}, u32[]{:S(2)}, u32[]{:S(2)}) collective-permute-start(bf16[512,128]{1,0:T(8,128)(2,1)S(1)} %hop.1), channel_id=1, source_target_pairs={{8,24},{9,25},{10,26},{11,27},{12,28},{13,29},{14,30},{15,31}} | collective-permute-start | bytes 393224 | tf_op jit(solution)/shard_map/ppermute | solution.py:681
  52.2 6.9 %collective-permute-start.11 = (bf16[512,128]{1,0:T(8,128)(2,1)S(1)}, bf16[512,128]{1,0:T(8,128)(2,1)S(1)}, u32[]{:S(2)}, u32[]{:S(2)}) collective-permute-start(bf16[512,128]{1,0:T(8,128)(2,1)S(1)} %get-tuple-element.74), channel_id=1, source_target_pairs={{0,2},{1,3},{2,0},{3,1},{4,6},{5,7},{6,4},{7,5},{8,10},{9,11},{10,... | collective-permute-start | bytes 393224 | tf_op jit(solution)/shard_map/ppermute | solution.py:774
  52.4 8.1 %collective-permute-start.13 = (bf16[512,128]{1,0:T(8,128)(2,1)S(1)}, bf16[512,128]{1,0:T(8,128)(2,1)S(1)}, u32[]{:S(2)}, u32[]{:S(2)}) collective-permute-start(bf16[512,128]{1,0:T(8,128)(2,1)S(1)} %get-tuple-element.75), channel_id=1, source_target_pairs={{0,4},{1,5},{2,6},{3,7},{4,0},{5,1},{6,2},{7,3},{8,12},{9,13},{10,... | collective-permute-start | bytes 393224 | tf_op jit(solution)/shard_map/ppermute | solution.py:774
  53.5 8.5 %collective-permute-start.15 = (bf16[512,128]{1,0:T(8,128)(2,1)S(1)}, bf16[512,128]{1,0:T(8,128)(2,1)S(1)}, u32[]{:S(2)}, u32[]{:S(2)}) collective-permute-start(bf16[512,128]{1,0:T(8,128)(2,1)S(1)} %get-tuple-element.76), channel_id=1, source_target_pairs={{0,6},{1,7},{2,4},{3,5},{4,2},{5,3},{6,0},{7,1},{8,14},{9,15},{10,... | collective-permute-start | bytes 393224 | tf_op jit(solution)/shard_map/ppermute | solution.py:774
  54.9 8.7 %collective-permute-start.10 = (bf16[512,128]{1,0:T(8,128)(2,1)S(1)}, bf16[512,128]{1,0:T(8,128)(2,1)S(1)}, u32[]{:S(2)}, u32[]{:S(2)}) collective-permute-start(bf16[512,128]{1,0:T(8,128)(2,1)S(1)} %get-tuple-element.71.e_k), channel_id=1, source_target_pairs={{0,1},{1,0},{2,3},{3,2},{4,5},{5,4},{6,7},{7,6},{8,9},{9,8},{10,11... | collective-permute-start | bytes 393224 | tf_op jit(solution)/shard_map/ppermute | solution.py:774
  59.1 5.3 %collective-permute-start.12 = (bf16[512,128]{1,0:T(8,128)(2,1)S(1)}, bf16[512,128]{1,0:T(8,128)(2,1)S(1)}, u32[]{:S(2)}, u32[]{:S(2)}) collective-permute-start(bf16[512,128]{1,0:T(8,128)(2,1)S(1)} %collective-permute-done.11.e_k), channel_id=1, source_target_pairs={{0,1},{1,0},{2,3},{3,2},{4,5},{5,4},{6,7},{7,6},{8,9},{9,8},{10,11... | collective-permute-start | bytes 393224 | tf_op jit(solution)/shard_map/ppermute | solution.py:774
  60.5 4.6 %collective-permute-start.14 = (bf16[512,128]{1,0:T(8,128)(2,1)S(1)}, bf16[512,128]{1,0:T(8,128)(2,1)S(1)}, u32[]{:S(2)}, u32[]{:S(2)}) collective-permute-start(bf16[512,128]{1,0:T(8,128)(2,1)S(1)} %collective-permute-done.13.e_k), channel_id=1, source_target_pairs={{0,1},{1,0},{2,3},{3,2},{4,5},{5,4},{6,7},{7,6},{8,9},{9,8},{10,11... | collective-permute-start | bytes 393224 | tf_op jit(solution)/shard_map/ppermute | solution.py:774
  62.0 3.9 %collective-permute-start.16 = (bf16[512,128]{1,0:T(8,128)(2,1)S(1)}, bf16[512,128]{1,0:T(8,128)(2,1)S(1)}, u32[]{:S(2)}, u32[]{:S(2)}) collective-permute-start(bf16[512,128]{1,0:T(8,128)(2,1)S(1)} %collective-permute-done.15.e_k), channel_id=1, source_target_pairs={{0,1},{1,0},{2,3},{3,2},{4,5},{5,4},{6,7},{7,6},{8,9},{9,8},{10,11... | collective-permute-start | bytes 393224 | tf_op jit(solution)/shard_map/ppermute | solution.py:774

commit v3 on v2

--- a/solution.py
+++ b/solution.py
@@ -696,69 +696,70 @@
     return jnp.zeros_like(plane_map), jnp.zeros_like(leaving), states
 
 
-def read_group(g, parts, out):
-    for n, (r_ref, d_ref, e_ref) in enumerate(parts):
+def read_out(meta, r_ref, d_ref, e_refs, rows):
+    for m, e_ref in enumerate(e_refs):
+        g = meta[3] ^ m
         for h in range(GROUP):
             here = slice(h * TOK, (h + 1) * TOK)
             total = dot(r_ref[g, here, :], e_ref[here, :]) + d_ref[g, here, :]
-            out[n, :, h * DV : (h + 1) * DV] = total.astype(BF16)
-
-
-def group_kernel(m, meta, r_k, d_k, e_k, r_s, d_s, e_s, out):
-    read_group(meta[3] ^ m, ((r_k, d_k, e_k), (r_s, d_s, e_s)), out)
-
-
-def group_cost():
-    return pl.CostEstimate(flops=8 * 2 * 128**3, bytes_accessed=2**20, transcendentals=0)
-
-
-def read_out(m, meta, *parts):
-    return pl.pallas_call(
-        functools.partial(group_kernel, m),
+            rows[g, :, h * DV : (h + 1) * DV] = total.astype(BF16)
+        yield m, g
+
+
+def half_kernel(meta, r_ref, d_ref, e0, e1, e2, e3, rows):
+    for _ in read_out(meta, r_ref, d_ref, (e0, e1, e2, e3), rows):
+        pass
+
+
+def read_half(meta, reads, direct, states):
+    return pl.pallas_call(
+        half_kernel,
         in_specs=[smem_spec()] + [whole_spec()] * 6,
         out_specs=whole_spec(),
-        out_shape=jax.ShapeDtypeStruct((2, TOK, GROUP * DV), BF16),
-        compiler_params=params(),
-        cost_estimate=group_cost(),
-        name="group",
-    )(meta, *parts)
-
-
-def emit_kernel(meta, g0, g1, g2, r_k, d_k, e_k, r_s, d_s, e_s, out_ref, rows, sems):
+        out_shape=jax.ShapeDtypeStruct((4, TOK, GROUP * DV), BF16),
+        compiler_params=params(),
+        cost_estimate=pl.CostEstimate(
+            flops=16 * 2 * 128**3, bytes_accessed=3 * 2**20, transcendentals=0
+        ),
+        name="half",
+    )(meta, reads, direct, *states)
+
+
+def emit_kernel(meta, kept, r_ref, d_ref, e0, e1, e2, e3, out_ref, rows, sems):
     copies = []
 
-    def put(source, m):
-        g = meta[3] ^ m
-        for n in range(2):
-            start = pl.multiple_of((meta[1 - n] + g) * (GROUP * DV), GROUP * DV)
-            copy = pltpu.make_async_copy(
-                source.at[n], out_ref.at[:, pl.ds(start, GROUP * DV)], sems.at[2 * m + n]
-            )
-            copy.start()
-            copies.append(copy)
-
-    for m, group in enumerate((g0, g1, g2)):
-        put(group, m)
-    read_group(meta[3] ^ 3, ((r_k, d_k, e_k), (r_s, d_s, e_s)), rows)
-    put(rows, 3)
+    def put(source, n, slot, g):
+        start = pl.multiple_of((meta[slot] + g) * (GROUP * DV), GROUP * DV)
+        copy = pltpu.make_async_copy(
+            source.at[g], out_ref.at[:, pl.ds(start, GROUP * DV)], sems.at[n]
+        )
+        copy.start()
+        copies.append(copy)
+
+    for g in range(4):
+        put(kept, g, 1, g)
+    for m, g in read_out(meta, r_ref, d_ref, (e0, e1, e2, e3), rows):
+        put(rows, 4 + m, 0, g)
     for copy in copies:
         copy.wait()
 
 
-def emit(meta, *parts):
+def emit(meta, kept, reads, direct, states):
     return pl.pallas_call(
         emit_kernel,
-        in_specs=[smem_spec()] + [whole_spec()] * 9,
+        in_specs=[smem_spec()] + [whole_spec()] * 7,
         out_specs=pl.BlockSpec(memory_space=pl.ANY),
         out_shape=jax.ShapeDtypeStruct((TOK, HV * DV), BF16),
         scratch_shapes=[
-            pltpu.VMEM((2, TOK, GROUP * DV), BF16),
+            pltpu.VMEM((4, TOK, GROUP * DV), BF16),
             pltpu.SemaphoreType.DMA((8,)),
         ],
         compiler_params=params(),
-        cost_estimate=group_cost(),
+        cost_estimate=pl.CostEstimate(
+            flops=16 * 2 * 128**3, bytes_accessed=3 * 2**20, transcendentals=0
+        ),
         name="emit",
-    )(meta, *parts)
+    )(meta, kept, reads, direct, *states)
 
 
 def shards(projected, conv_weight, decay_log, write_strength, starts):
@@ -794,14 +795,11 @@
     prefix, plane_map, leaving = plane_maps(meta, (x0, x1, x2, x3))
     before, far, arrived = entering_states(plane_map, leaving, count // 8)
     e0, e1, e2, e3 = spread(meta, prefix, before, far, arrived)
-    states = [e0, e1, e2, e3]
-    for m in range(1, 4):
-        states[m] = exchange(states[m], 2 * m)
+    e3, e1, e2 = exchange(e3, 6), exchange(e1, 2), exchange(e2, 4)
+    states = (e0, e1, e2, e3)
     partner = [exchange(e, 1) for e in states]
-    groups = []
-    for m in range(3):
-        groups.append(read_out(m, meta, r_k, d_k, states[m], r_s, d_s, partner[m]))
-    return emit(meta, *groups, r_k, d_k, states[3], r_s, d_s, partner[3])
+    kept = read_half(meta, r_k, d_k, states)
+    return emit(meta, kept, r_s, d_s, partner)
 
 
 def solution(mesh):

time: 68 us -> 66.7 us (0.981)
  Pallas kernels: 32.8 us -> 31.4 us
    pallas_call x4 -> x2, Pallas kernels: 3.9 us -> 2.57 us  [the longest x1 1.73 us: emit(): pl.pallas_call(emit_kernel, in_specs=[smem_spec()] + [whole_spec()] * 7,...]
  transfers between devices with their start and end apart: 17 -> 17, of which waited for: 2 -> 3; matrix products, arithmetic and copies ran while one was open for 0% -> 0% of each run, Pallas kernels for 27% -> 26%
where the time goes in v3:
time: 66.7 us; the launch traced here: 66.4 us
  Pallas kernels  31.4 us (47%)
  starting transfers between devices  24.5 us (37%)
  waiting for transfers between devices  10.1 us (15%)
    ppermute x12, starting transfers between devices, exchange(): return lax.ppermute(block, 'seq', [(i, i ^ bits) for i in range(count)])  16.9 us
    pallas_call x2, Pallas kernels, make_reads(): pl.pallas_call(read_kernel, grid_spec=pltpu.PrefetchScalarGridSpec(num_sc...  8.45 us
    ppermute x4, waiting for transfers between devices, ahead(): return lax.ppermute(block, 'seq', [(i, i + 8 * distance) for i in members])  7.68 us
    pallas_call x1, Pallas kernels, send_maps(): pl.pallas_call(send_kernel, in_specs=[smem_spec()] + [whole_spec()] * len...  7.52 us
    pallas_call x1, Pallas kernels, keep_maps(): pl.pallas_call(keep_kernel, in_specs=[smem_spec()] + [whole_spec()] * len...  5.96 us
    ppermute x4, starting transfers between devices, ahead(): return lax.ppermute(block, 'seq', [(i, i + 8 * distance) for i in members])  3.92 us
    ppermute x1, starting transfers between devices, shards(): lax.ppermute(tail_rows, 'seq', [(i, i + 1) for i in range(count - 1)])  3.68 us
    ppermute x12, waiting for transfers between devices, exchange(): return lax.ppermute(block, 'seq', [(i, i ^ bits) for i in range(count)])  2.45 us
  transfers between devices with their start and end apart: 17, of which 3 were waited for; matrix products, arithmetic and copies ran while one was open for 0% of the time, Pallas kernels for 26%

profile of v3, /device:TPU:25, one launch (start us, length us, event | category | flops | bytes accessed | tf_op | source)
XLA Modules:
  0.0 66.4 jit_solution(1053180531096430259)
XLA Ops:
  0.0 1.1 %tail.1 = bf16[3,8192]{1,0:T(4,128)(2,1)S(1)} custom-call(s32[1,128]{1,0:T(1,128)} %bitcast.1, bf16[128,8192]{1,0:T(8,128)(2,1)} %x_ref.1), custom_call_target="tpu_custom_call" | custom-call | flops 100000 | bytes 1000000 | tf_op jit(solution)/shard_map/tail/pallas_call | solution.py:59
  1.1 3.7 %collective-permute-start = (bf16[3,8192]{1,0:T(4,128)(2,1)S(1)}, bf16[3,8192]{1,0:T(4,128)(2,1)S(1)}, u32[]{:S(2)}, u32[]{:S(2)}) collective-permute-start(bf16[3,8192]{1,0:T(4,128)(2,1)S(1)} %tail.1), channel_id=1, source_target_pairs={{0,1},{1,2},{2,3},{3,4},{4,5},{5,6},{6,7},{7,8},{8,9},{9,10},{10,1... | collective-permute-start | bytes 147464 | tf_op jit(solution)/shard_map/ppermute | solution.py:779
  4.9 1.7 %stage.1 = (bf16[128,8192]{1,0:T(8,128)(2,1)S(1)}, bf16[4,8192]{1,0:T(4,128)(2,1)S(1)}, f32[8,16,128]{2,1,0:T(8,128)S(1)}, bf16[8,128,128]{2,1,0:T(8,128)(2,1)S(1)}, f32[6,128,128]{2,1,0:T(8,128)S(1)}) custom-call(f32[32,128]{1,0:T(8,128)} %decay_hbm.1, f32[32,128]{1,0:T(8,128)} %beta_hbm.1, s32[1,128]{1,0:T(1,128)} %bitcast.2, bf16[128,8192]{1,0:T(8,128)(2,1)} %x_ref.1, ...), custom_call_target="tpu_custom_call" | custom-call | flops 10000000 | bytes 4194304 | tf_op jit(solution)/shard_map/stage/pallas_call | solution.py:184
  6.6 0.0 collective-permute-done.halo_ref.hq_ref
  6.6 7.5 %send_maps.1 = (bf16[4,528,256]{2,1,0:T(8,128)(2,1)S(1)}, bf16[4,256,128]{2,1,0:T(8,128)(2,1)S(1)}, bf16[4,512,256]{2,1,0:T(8,128)(2,1)S(1)}, bf16[8,128,128]{2,...) custom-call(s32[8]{0:T(128)S(1)} %compare_select_fusion.4.meta, ...), custom_call_target="tpu_custom_call" | custom-call | flops 1342177280 | bytes 5242880 | tf_op jit(solution)/shard_map/send_maps/pallas_call | solution.py:414
  14.1 2.7 %collective-permute-start.1 = (bf16[4,528,256]{2,1,0:T(8,128)(2,1)S(1)}, bf16[4,528,256]{2,1,0:T(8,128)(2,1)S(1)}, u32[]{:S(2)}, u32[]{:S(2)}) collective-permute-start(bf16[4,528,256]{2,1,0:T(8,128)(2,1)S(1)} %get-tuple-element.50), channel_id=1, source_target_pairs={{0,1},{1,0},{2,3},{3,2},{4,5},{5,4},{6,7},{7,6},{8,9},{9,8},{10,11... | collective-permute-start | bytes 3244040 | tf_op jit(solution)/shard_map/ppermute | solution.py:775
  16.8 6.0 %keep_maps.1 = (bf16[4,528,256]{2,1,0:T(8,128)(2,1)S(1)}, bf16[4,256,128]{2,1,0:T(8,128)(2,1)S(1)}, bf16[4,512,256]{2,1,0:T(8,128)(2,1)S(1)}) custom-call(s32[8]{0:T(128)S(1)} %compare_select_fusion.4.meta, bf16[128,8192]{1,0:T(8,128)(2,1)S(1)} %get-tuple-element.41.x_ref.xq_ref, bf16[3,8192]{1,0:T(4,128)(2,1)S(1)} %collective-permute-done.halo_ref.hq_ref, ...), custom_call_target="tpu_custom_call" | custom-call | flops 1342177280 | bytes 5242880 | tf_op jit(solution)/shard_map/keep_maps/pallas_call | solution.py:432
  22.8 0.0 collective-permute-done.1.other_ref.left_ref
  22.8 1.4 %pair.1 = (bf16[528,256]{1,0:T(8,128)(2,1)S(1)}, bf16[528,256]{1,0:T(8,128)(2,1)S(1)}, bf16[528,256]{1,0:T(8,128)(2,1)S(1)}, bf16[528,256]{1,0:T(8,128)(2,1)S(1)}) custom-call(s32[8]{0:T(128)S(1)} %compare_select_fusion.4.meta, bf16[4,528,256]{2,1,0:T(8,128)(2,1)S(1)} %get-tuple-element.59.mine_ref, ...), custom_call_target="tpu_custom_call" | custom-call | flops 134217728 | bytes 3145728 | tf_op jit(solution)/shard_map/pair/pallas_call | solution.py:557
  24.2 0.1 collective-permute-start.2
  24.2 0.1 collective-permute-start.3
  24.3 0.6 collective-permute-start.4
  25.0 2.0 %collective-permute-start.5 = (bf16[528,256]{1,0:T(8,128)(2,1)S(1)}, bf16[528,256]{1,0:T(8,128)(2,1)S(1)}, u32[]{:S(2)}, u32[]{:S(2)}) collective-permute-start(bf16[528,256]{1,0:T(8,128)(2,1)S(1)} %get-tuple-element.67), channel_id=1, source_target_pairs={{0,6},{1,7},{2,4},{3,5},{4,2},{5,3},{6,0},{7,1},{8,14},{9,15},{10,... | collective-permute-start | bytes 811016 | tf_op jit(solution)/shard_map/ppermute | solution.py:775
  26.9 4.2 %reads.2 = (bf16[4,512,128]{2,1,0:T(8,128)(2,1)S(1)}, f32[4,512,128]{2,1,0:T(8,128)S(1)}) custom-call(s32[8]{0:T(128)S(1)} %compare_select_fusion.4.meta, bf16[128,8192]{1,0:T(8,128)(2,1)S(1)} %get-tuple-element.41.x_ref.xq_ref, bf16[3,8192]{1,0:T(4,128)(2,1)S(1)} %collective-permute-done.halo_ref.hq_ref, ...), custom_call_target="tpu_custom_call" | custom-call | flops 402653184 | bytes 5242880 | tf_op jit(solution)/shard_map/reads/pallas_call | solution.py:483
  31.2 0.0 collective-permute-done.2.left_ref
  31.2 4.2 %reads.3 = (bf16[4,512,128]{2,1,0:T(8,128)(2,1)S(1)}, f32[4,512,128]{2,1,0:T(8,128)S(1)}) custom-call(s32[8]{0:T(128)S(1)} %compare_select_fusion.4.meta, bf16[128,8192]{1,0:T(8,128)(2,1)S(1)} %get-tuple-element.41.x_ref.xq_ref, bf16[3,8192]{1,0:T(4,128)(2,1)S(1)} %collective-permute-done.halo_ref.hq_ref, ...), custom_call_target="tpu_custom_call" | custom-call | flops 402653184 | bytes 5242880 | tf_op jit(solution)/shard_map/reads/pallas_call | solution.py:483
  35.4 0.0 collective-permute-done.3.x1
  35.4 0.0 collective-permute-done.4.x2
  35.4 2.3 %collective-permute-done.5.x3 = bf16[528,256]{1,0:T(8,128)(2,1)S(1)} collective-permute-done((bf16[528,256]{1,0:T(8,128)(2,1)S(1)}, bf16[528,256]{1,0:T(8,128)(2,1)S(1)}, u32[]{:S(2)}, u32[]{:S(2)}) %collective-permute-start.5) | collective-permute-done | bytes 270368 | tf_op jit(solution)/shard_map/ppermute | solution.py:775
  37.8 1.1 %plane.1 = (bf16[4,528,256]{2,1,0:T(8,128)(2,1)S(1)}, bf16[528,256]{1,0:T(8,128)(2,1)S(1)}, bf16[512,128]{1,0:T(8,128)(2,1)S(1)}) custom-call(s32[8]{0:T(128)S(1)} %compare_select_fusion.4.meta, bf16[528,256]{1,0:T(8,128)(2,1)S(1)} %get-tuple-element.64.x0, bf16[528,256]{1,0:T(8,128)(2,1)S(1)} %collective-permute-done.3.x1, ...), custom_call_target="tpu_custom_call" | custom-call | flops 100663296 | bytes 2097152 | tf_op jit(solution)/shard_map/plane/pallas_call | solution.py:604
  38.9 1.3 %collective-permute-start.6 = (bf16[528,256]{1,0:T(8,128)(2,1)S(1)}, bf16[528,256]{1,0:T(8,128)(2,1)S(1)}, u32[]{:S(2)}, u32[]{:S(2)}) collective-permute-start(bf16[528,256]{1,0:T(8,128)(2,1)S(1)} %get-tuple-element.69.plane_ref), channel_id=1, source_target_pairs={{16,24},{17,25},{18,26},{19,27},{20,28},{21,29},{22,30},{23,31}} | collective-permute-start | bytes 811016 | tf_op jit(solution)/shard_map/ppermute | solution.py:681
  40.2 0.7 %collective-permute-start.7 = (bf16[512,128]{1,0:T(8,128)(2,1)S(1)}, bf16[512,128]{1,0:T(8,128)(2,1)S(1)}, u32[]{:S(2)}, u32[]{:S(2)}) collective-permute-start(bf16[512,128]{1,0:T(8,128)(2,1)S(1)} %get-tuple-element.70), channel_id=1, source_target_pairs={{0,8},{1,9},{2,10},{3,11},{4,12},{5,13},{6,14},{7,15}} | collective-permute-start | bytes 393224 | tf_op jit(solution)/shard_map/ppermute | solution.py:681
  40.9 0.0 collective-permute-done.7.state_ref.refs_0_
  40.9 0.2 hop.1
  41.1 0.7 %collective-permute-start.9 = (bf16[512,128]{1,0:T(8,128)(2,1)S(1)}, bf16[512,128]{1,0:T(8,128)(2,1)S(1)}, u32[]{:S(2)}, u32[]{:S(2)}) collective-permute-start(bf16[512,128]{1,0:T(8,128)(2,1)S(1)} %hop.1), channel_id=1, source_target_pairs={{8,16},{9,17},{10,18},{11,19},{12,20},{13,21},{14,22},{15,23}} | collective-permute-start | bytes 393224 | tf_op jit(solution)/shard_map/ppermute | solution.py:681
  41.8 1.3 %collective-permute-start.8 = (bf16[512,128]{1,0:T(8,128)(2,1)S(1)}, bf16[512,128]{1,0:T(8,128)(2,1)S(1)}, u32[]{:S(2)}, u32[]{:S(2)}) collective-permute-start(bf16[512,128]{1,0:T(8,128)(2,1)S(1)} %hop.1), channel_id=1, source_target_pairs={{8,24},{9,25},{10,26},{11,27},{12,28},{13,29},{14,30},{15,31}} | collective-permute-start | bytes 393224 | tf_op jit(solution)/shard_map/ppermute | solution.py:681
  43.1 0.0 collective-permute-done.9.refs_1_
  43.1 7.7 %collective-permute-done.8.far_ref = bf16[512,128]{1,0:T(8,128)(2,1)S(1)} collective-permute-done((bf16[512,128]{1,0:T(8,128)(2,1)S(1)}, bf16[512,128]{1,0:T(8,128)(2,1)S(1)}, u32[]{:S(2)}, u32[]{:S(2)}) %collective-permute-start.8) | collective-permute-done | bytes 131104 | tf_op jit(solution)/shard_map/ppermute | solution.py:681
  50.8 0.0 collective-permute-done.6.before_ref
  50.8 1.4 %spread.1 = (bf16[512,128]{1,0:T(8,128)(2,1)S(1)}, bf16[512,128]{1,0:T(8,128)(2,1)S(1)}, bf16[512,128]{1,0:T(8,128)(2,1)S(1)}, bf16[512,128]{1,0:T(8,128)(2,1)S(1)}) custom-call(s32[8]{0:T(128)S(1)} %compare_select_fusion.4.meta, bf16[4,528,256]{2,1,0:T(8,128)(2,1)S(1)} %get-tuple-element.68.prefix_ref, ...), custom_call_target="tpu_custom_call" | custom-call | flops 83886080 | bytes 2097152 | tf_op jit(solution)/shard_map/spread/pallas_call | solution.py:665
  52.2 0.2 collective-permute-start.10
  52.4 1.1 %collective-permute-start.11 = (bf16[512,128]{1,0:T(8,128)(2,1)S(1)}, bf16[512,128]{1,0:T(8,128)(2,1)S(1)}, u32[]{:S(2)}, u32[]{:S(2)}) collective-permute-start(bf16[512,128]{1,0:T(8,128)(2,1)S(1)} %get-tuple-element.73), channel_id=1, source_target_pairs={{0,4},{1,5},{2,6},{3,7},{4,0},{5,1},{6,2},{7,3},{8,12},{9,13},{10,... | collective-permute-start | bytes 393224 | tf_op jit(solution)/shard_map/ppermute | solution.py:775
  53.5 1.4 %collective-permute-start.12 = (bf16[512,128]{1,0:T(8,128)(2,1)S(1)}, bf16[512,128]{1,0:T(8,128)(2,1)S(1)}, u32[]{:S(2)}, u32[]{:S(2)}) collective-permute-start(bf16[512,128]{1,0:T(8,128)(2,1)S(1)} %get-tuple-element.74), channel_id=1, source_target_pairs={{0,6},{1,7},{2,4},{3,5},{4,2},{5,3},{6,0},{7,1},{8,14},{9,15},{10,... | collective-permute-start | bytes 393224 | tf_op jit(solution)/shard_map/ppermute | solution.py:775
  54.9 4.2 %collective-permute-start.13 = (bf16[512,128]{1,0:T(8,128)(2,1)S(1)}, bf16[512,128]{1,0:T(8,128)(2,1)S(1)}, u32[]{:S(2)}, u32[]{:S(2)}) collective-permute-start(bf16[512,128]{1,0:T(8,128)(2,1)S(1)} %get-tuple-element.71.e0), channel_id=1, source_target_pairs={{0,1},{1,0},{2,3},{3,2},{4,5},{5,4},{6,7},{7,6},{8,9},{9,8},{10,11... | collective-permute-start | bytes 393224 | tf_op jit(solution)/shard_map/ppermute | solution.py:775
  59.1 0.0 collective-permute-done.10.e1
  59.1 1.5 %collective-permute-start.14 = (bf16[512,128]{1,0:T(8,128)(2,1)S(1)}, bf16[512,128]{1,0:T(8,128)(2,1)S(1)}, u32[]{:S(2)}, u32[]{:S(2)}) collective-permute-start(bf16[512,128]{1,0:T(8,128)(2,1)S(1)} %collective-permute-done.10.e1), channel_id=1, source_target_pairs={{0,1},{1,0},{2,3},{3,2},{4,5},{5,4},{6,7},{7,6},{8,9},{9,8},{10,11... | collective-permute-start | bytes 393224 | tf_op jit(solution)/shard_map/ppermute | solution.py:775
  60.5 0.0 collective-permute-done.11.e2
  60.5 1.5 %collective-permute-start.15 = (bf16[512,128]{1,0:T(8,128)(2,1)S(1)}, bf16[512,128]{1,0:T(8,128)(2,1)S(1)}, u32[]{:S(2)}, u32[]{:S(2)}) collective-permute-start(bf16[512,128]{1,0:T(8,128)(2,1)S(1)} %collective-permute-done.11.e2), channel_id=1, source_target_pairs={{0,1},{1,0},{2,3},{3,2},{4,5},{5,4},{6,7},{7,6},{8,9},{9,8},{10,11... | collective-permute-start | bytes 393224 | tf_op jit(solution)/shard_map/ppermute | solution.py:775
  62.0 0.0 collective-permute-done.12.e3
  62.0 1.5 %collective-permute-start.16 = (bf16[512,128]{1,0:T(8,128)(2,1)S(1)}, bf16[512,128]{1,0:T(8,128)(2,1)S(1)}, u32[]{:S(2)}, u32[]{:S(2)}) collective-permute-start(bf16[512,128]{1,0:T(8,128)(2,1)S(1)} %collective-permute-done.12.e3), channel_id=1, source_target_pairs={{0,1},{1,0},{2,3},{3,2},{4,5},{5,4},{6,7},{7,6},{8,9},{9,8},{10,11... | collective-permute-start | bytes 393224 | tf_op jit(solution)/shard_map/ppermute | solution.py:775
  63.6 0.8 %half.1.kept = bf16[4,128,512]{2,1,0:T(8,128)(2,1)S(1)} custom-call(s32[8]{0:T(128)S(1)} %compare_select_fusion.4.meta, bf16[4,512,128]{2,1,0:T(8,128)(2,1)S(1)} %get-tuple-element.62.r_ref, f32[4,512,128]{2,1,0:T(8,128)S(1)} %get-tuple-element.63.d_ref, bf16[512,128]{1,0:T(8,128)(2,1)S(1)} %get-tuple-element.71.e0, ...), custom_call_target="tpu_custom_call" | custom-call | flops 67108864 | bytes 3145728 | tf_op jit(solution)/shard_map/half/pallas_call | solution.py:715
  64.4 0.0 collective-permute-done.13.e0
  64.4 0.0 collective-permute-done.14.e1
  64.4 0.0 collective-permute-done.15.e2
  64.4 0.1 collective-permute-done.16.e3
  64.5 1.7 %emit.1 = bf16[128,4096]{1,0:T(8,128)(2,1)} custom-call(s32[8]{0:T(128)S(1)} %compare_select_fusion.4.meta, bf16[4,128,512]{2,1,0:T(8,128)(2,1)S(1)} %half.1.kept, bf16[4,512,128]{2,1,0:T(8,128)(2,1)S(1)} %get-tuple-element.75.r_ref, f32[4,512,128]{2,1,0:T(8,128)S(1)} %get-tuple-element.76.d_ref, bf16[512,128]{1,0:T(8,128)(2,1)S(1)} %collective-permute-done.13.e0, ...), custom_call_target="tpu_custom_call" | custom-call | flops 67108864 | bytes 3145728 | tf_op jit(solution)/shard_map/emit/pallas_call | solution.py:748
  (1 shorter events, 0.0 us)
Async XLA Ops:
  1.1 5.4 %collective-permute-start = (bf16[3,8192]{1,0:T(4,128)(2,1)S(1)}, bf16[3,8192]{1,0:T(4,128)(2,1)S(1)}, u32[]{:S(2)}, u32[]{:S(2)}) collective-permute-start(bf16[3,8192]{1,0:T(4,128)(2,1)S(1)} %tail.1), channel_id=1, source_target_pairs={{0,1},{1,2},{2,3},{3,4},{4,5},{5,6},{6,7},{7,8},{8,9},{9,10},{10,1... | collective-permute-start | bytes 147464 | tf_op jit(solution)/shard_map/ppermute | solution.py:779
  14.1 8.7 %collective-permute-start.1 = (bf16[4,528,256]{2,1,0:T(8,128)(2,1)S(1)}, bf16[4,528,256]{2,1,0:T(8,128)(2,1)S(1)}, u32[]{:S(2)}, u32[]{:S(2)}) collective-permute-start(bf16[4,528,256]{2,1,0:T(8,128)(2,1)S(1)} %get-tuple-element.50), channel_id=1, source_target_pairs={{0,1},{1,0},{2,3},{3,2},{4,5},{5,4},{6,7},{7,6},{8,9},{9,8},{10,11... | collective-permute-start | bytes 3244040 | tf_op jit(solution)/shard_map/ppermute | solution.py:775
  24.2 7.0 %collective-permute-start.2 = (bf16[4,528,256]{2,1,0:T(8,128)(2,1)S(1)}, bf16[4,528,256]{2,1,0:T(8,128)(2,1)S(1)}, u32[]{:S(2)}, u32[]{:S(2)}) collective-permute-start(bf16[4,528,256]{2,1,0:T(8,128)(2,1)S(1)} %get-tuple-element.59.mine_ref), channel_id=1, source_target_pairs={{0,1},{1,0},{2,3},{3,2},{4,5},{5,4},{6,7},{7,6},{8,9},{9,8},{10,11... | collective-permute-start | bytes 3244040 | tf_op jit(solution)/shard_map/ppermute | solution.py:775
  24.2 11.2 %collective-permute-start.3 = (bf16[528,256]{1,0:T(8,128)(2,1)S(1)}, bf16[528,256]{1,0:T(8,128)(2,1)S(1)}, u32[]{:S(2)}, u32[]{:S(2)}) collective-permute-start(bf16[528,256]{1,0:T(8,128)(2,1)S(1)} %get-tuple-element.65), channel_id=1, source_target_pairs={{0,2},{1,3},{2,0},{3,1},{4,6},{5,7},{6,4},{7,5},{8,10},{9,11},{10,... | collective-permute-start | bytes 811016 | tf_op jit(solution)/shard_map/ppermute | solution.py:775
  24.3 11.1 %collective-permute-start.4 = (bf16[528,256]{1,0:T(8,128)(2,1)S(1)}, bf16[528,256]{1,0:T(8,128)(2,1)S(1)}, u32[]{:S(2)}, u32[]{:S(2)}) collective-permute-start(bf16[528,256]{1,0:T(8,128)(2,1)S(1)} %get-tuple-element.66), channel_id=1, source_target_pairs={{0,4},{1,5},{2,6},{3,7},{4,0},{5,1},{6,2},{7,3},{8,12},{9,13},{10,... | collective-permute-start | bytes 811016 | tf_op jit(solution)/shard_map/ppermute | solution.py:775
  25.0 12.8 %collective-permute-start.5 = (bf16[528,256]{1,0:T(8,128)(2,1)S(1)}, bf16[528,256]{1,0:T(8,128)(2,1)S(1)}, u32[]{:S(2)}, u32[]{:S(2)}) collective-permute-start(bf16[528,256]{1,0:T(8,128)(2,1)S(1)} %get-tuple-element.67), channel_id=1, source_target_pairs={{0,6},{1,7},{2,4},{3,5},{4,2},{5,3},{6,0},{7,1},{8,14},{9,15},{10,... | collective-permute-start | bytes 811016 | tf_op jit(solution)/shard_map/ppermute | solution.py:775
  38.9 11.8 %collective-permute-start.6 = (bf16[528,256]{1,0:T(8,128)(2,1)S(1)}, bf16[528,256]{1,0:T(8,128)(2,1)S(1)}, u32[]{:S(2)}, u32[]{:S(2)}) collective-permute-start(bf16[528,256]{1,0:T(8,128)(2,1)S(1)} %get-tuple-element.69.plane_ref), channel_id=1, source_target_pairs={{16,24},{17,25},{18,26},{19,27},{20,28},{21,29},{22,30},{23,31}} | collective-permute-start | bytes 811016 | tf_op jit(solution)/shard_map/ppermute | solution.py:681
  40.2 0.7 %collective-permute-start.7 = (bf16[512,128]{1,0:T(8,128)(2,1)S(1)}, bf16[512,128]{1,0:T(8,128)(2,1)S(1)}, u32[]{:S(2)}, u32[]{:S(2)}) collective-permute-start(bf16[512,128]{1,0:T(8,128)(2,1)S(1)} %get-tuple-element.70), channel_id=1, source_target_pairs={{0,8},{1,9},{2,10},{3,11},{4,12},{5,13},{6,14},{7,15}} | collective-permute-start | bytes 393224 | tf_op jit(solution)/shard_map/ppermute | solution.py:681
  41.1 2.0 %collective-permute-start.9 = (bf16[512,128]{1,0:T(8,128)(2,1)S(1)}, bf16[512,128]{1,0:T(8,128)(2,1)S(1)}, u32[]{:S(2)}, u32[]{:S(2)}) collective-permute-start(bf16[512,128]{1,0:T(8,128)(2,1)S(1)} %hop.1), channel_id=1, source_target_pairs={{8,16},{9,17},{10,18},{11,19},{12,20},{13,21},{14,22},{15,23}} | collective-permute-start | bytes 393224 | tf_op jit(solution)/shard_map/ppermute | solution.py:681
  41.8 9.0 %collective-permute-start.8 = (bf16[512,128]{1,0:T(8,128)(2,1)S(1)}, bf16[512,128]{1,0:T(8,128)(2,1)S(1)}, u32[]{:S(2)}, u32[]{:S(2)}) collective-permute-start(bf16[512,128]{1,0:T(8,128)(2,1)S(1)} %hop.1), channel_id=1, source_target_pairs={{8,24},{9,25},{10,26},{11,27},{12,28},{13,29},{14,30},{15,31}} | collective-permute-start | bytes 393224 | tf_op jit(solution)/shard_map/ppermute | solution.py:681
  52.2 6.9 %collective-permute-start.10 = (bf16[512,128]{1,0:T(8,128)(2,1)S(1)}, bf16[512,128]{1,0:T(8,128)(2,1)S(1)}, u32[]{:S(2)}, u32[]{:S(2)}) collective-permute-start(bf16[512,128]{1,0:T(8,128)(2,1)S(1)} %get-tuple-element.72), channel_id=1, source_target_pairs={{0,2},{1,3},{2,0},{3,1},{4,6},{5,7},{6,4},{7,5},{8,10},{9,11},{10,... | collective-permute-start | bytes 393224 | tf_op jit(solution)/shard_map/ppermute | solution.py:775
  52.4 8.1 %collective-permute-start.11 = (bf16[512,128]{1,0:T(8,128)(2,1)S(1)}, bf16[512,128]{1,0:T(8,128)(2,1)S(1)}, u32[]{:S(2)}, u32[]{:S(2)}) collective-permute-start(bf16[512,128]{1,0:T(8,128)(2,1)S(1)} %get-tuple-element.73), channel_id=1, source_target_pairs={{0,4},{1,5},{2,6},{3,7},{4,0},{5,1},{6,2},{7,3},{8,12},{9,13},{10,... | collective-permute-start | bytes 393224 | tf_op jit(solution)/shard_map/ppermute | solution.py:775
  53.5 8.5 %collective-permute-start.12 = (bf16[512,128]{1,0:T(8,128)(2,1)S(1)}, bf16[512,128]{1,0:T(8,128)(2,1)S(1)}, u32[]{:S(2)}, u32[]{:S(2)}) collective-permute-start(bf16[512,128]{1,0:T(8,128)(2,1)S(1)} %get-tuple-element.74), channel_id=1, source_target_pairs={{0,6},{1,7},{2,4},{3,5},{4,2},{5,3},{6,0},{7,1},{8,14},{9,15},{10,... | collective-permute-start | bytes 393224 | tf_op jit(solution)/shard_map/ppermute | solution.py:775
  54.9 9.5 %collective-permute-start.13 = (bf16[512,128]{1,0:T(8,128)(2,1)S(1)}, bf16[512,128]{1,0:T(8,128)(2,1)S(1)}, u32[]{:S(2)}, u32[]{:S(2)}) collective-permute-start(bf16[512,128]{1,0:T(8,128)(2,1)S(1)} %get-tuple-element.71.e0), channel_id=1, source_target_pairs={{0,1},{1,0},{2,3},{3,2},{4,5},{5,4},{6,7},{7,6},{8,9},{9,8},{10,11... | collective-permute-start | bytes 393224 | tf_op jit(solution)/shard_map/ppermute | solution.py:775
  59.1 5.4 %collective-permute-start.14 = (bf16[512,128]{1,0:T(8,128)(2,1)S(1)}, bf16[512,128]{1,0:T(8,128)(2,1)S(1)}, u32[]{:S(2)}, u32[]{:S(2)}) collective-permute-start(bf16[512,128]{1,0:T(8,128)(2,1)S(1)} %collective-permute-done.10.e1), channel_id=1, source_target_pairs={{0,1},{1,0},{2,3},{3,2},{4,5},{5,4},{6,7},{7,6},{8,9},{9,8},{10,11... | collective-permute-start | bytes 393224 | tf_op jit(solution)/shard_map/ppermute | solution.py:775
  60.5 3.9 %collective-permute-start.15 = (bf16[512,128]{1,0:T(8,128)(2,1)S(1)}, bf16[512,128]{1,0:T(8,128)(2,1)S(1)}, u32[]{:S(2)}, u32[]{:S(2)}) collective-permute-start(bf16[512,128]{1,0:T(8,128)(2,1)S(1)} %collective-permute-done.11.e2), channel_id=1, source_target_pairs={{0,1},{1,0},{2,3},{3,2},{4,5},{5,4},{6,7},{7,6},{8,9},{9,8},{10,11... | collective-permute-start | bytes 393224 | tf_op jit(solution)/shard_map/ppermute | solution.py:775
  62.0 2.5 %collective-permute-start.16 = (bf16[512,128]{1,0:T(8,128)(2,1)S(1)}, bf16[512,128]{1,0:T(8,128)(2,1)S(1)}, u32[]{:S(2)}, u32[]{:S(2)}) collective-permute-start(bf16[512,128]{1,0:T(8,128)(2,1)S(1)} %collective-permute-done.12.e3), channel_id=1, source_target_pairs={{0,1},{1,0},{2,3},{3,2},{4,5},{5,4},{6,7},{7,6},{8,9},{9,8},{10,11... | collective-permute-start | bytes 393224 | tf_op jit(solution)/shard_map/ppermute | solution.py:775

commit v4 on v3

--- a/solution.py
+++ b/solution.py
@@ -534,9 +534,9 @@
     return c[:, :DK] * state.astype(F32) + each[:, DK:].astype(F32) - product
 
 
-def pair_kernel(meta, mine_ref, other_ref, *out_refs):
+def pair_kernel(places, meta, mine_ref, other_ref, *out_refs):
     def combine(left_ref, right_ref):
-        for m, out_ref in enumerate(out_refs):
+        for m, out_ref in zip(places, out_refs):
             g = meta[3] ^ m
             left_tail = left_ref[g, GROUP * DK : ROWS, :]
             right_tail = right_ref[g, GROUP * DK : ROWS, :]
@@ -553,15 +553,15 @@
     pl.when(meta[2] != 0)(lambda: combine(other_ref, mine_ref))
 
 
-def pair_maps(meta, mine, other):
-    return pl.pallas_call(
-        pair_kernel,
+def pair_maps(meta, places, mine, other):
+    return pl.pallas_call(
+        functools.partial(pair_kernel, places),
         in_specs=[smem_spec(), whole_spec(), whole_spec()],
-        out_specs=[whole_spec()] * 4,
-        out_shape=[jax.ShapeDtypeStruct((ROWS, 256), BF16)] * 4,
+        out_specs=[whole_spec()] * len(places),
+        out_shape=[jax.ShapeDtypeStruct((ROWS, 256), BF16)] * len(places),
         compiler_params=params(),
         cost_estimate=pl.CostEstimate(
-            flops=16 * 2 * 2 * 128**3, bytes_accessed=3 * 2**20, transcendentals=0
+            flops=len(places) * 4 * 2 * 2 * 128**3, bytes_accessed=2**21, transcendentals=0
         ),
         name="pair",
     )(meta, mine, other)
@@ -785,8 +785,11 @@
     pay_s, kt_s, ef_s, *ready = send_maps(meta, *ins)
     other = exchange(pay_s, 1)
     mine, kt_k, ef_k = keep_maps(meta, *ins, *ready)
-    x0, x1, x2, x3 = pair_maps(meta, mine, other)
-    x3, x1, x2 = exchange(x3, 6), exchange(x1, 2), exchange(x2, 4)
+    x1, x2 = pair_maps(meta, (1, 2), mine, other)
+    x1 = exchange(x1, 2)
+    x2 = exchange(x2, 4)
+    x0, x3 = pair_maps(meta, (0, 3), mine, other)
+    x3 = exchange(x3, 6)
     x0, own = lax.optimization_barrier((x0, mine))
     left = exchange(own, 1)
     r_k, d_k = make_reads(meta, 1, projected, halo, conv_weight, tables, kt_k, ef_k, other)

time: 66.7 us -> 67.3 us (level)
    pallas_call x1 -> x2, Pallas kernels: 1.38 us -> 1.96 us  [pair_maps(): pl.pallas_call(functools.partial(pair_kernel, places), in_specs=[smem_spe...]
  transfers between devices with their start and end apart: 17 -> 17, of which waited for: 3 -> 3; matrix products, arithmetic and copies ran while one was open for 0% -> 0% of each run, Pallas kernels for 26% -> 27%
where the time goes in v4:
time: 67.3 us; the launch traced here: 67 us
  Pallas kernels  32 us (48%)
  starting transfers between devices  24.6 us (37%)
  waiting for transfers between devices  10 us (15%)
    ppermute x12, starting transfers between devices, exchange(): return lax.ppermute(block, 'seq', [(i, i ^ bits) for i in range(count)])  17 us
    pallas_call x2, Pallas kernels, make_reads(): pl.pallas_call(read_kernel, grid_spec=pltpu.PrefetchScalarGridSpec(num_sc...  8.45 us
    ppermute x4, waiting for transfers between devices, ahead(): return lax.ppermute(block, 'seq', [(i, i + 8 * distance) for i in members])  7.62 us
    pallas_call x1, Pallas kernels, send_maps(): pl.pallas_call(send_kernel, in_specs=[smem_spec()] + [whole_spec()] * len...  7.52 us
    pallas_call x1, Pallas kernels, keep_maps(): pl.pallas_call(keep_kernel, in_specs=[smem_spec()] + [whole_spec()] * len...  5.96 us
    ppermute x4, starting transfers between devices, ahead(): return lax.ppermute(block, 'seq', [(i, i + 8 * distance) for i in members])  3.92 us
    ppermute x1, starting transfers between devices, shards(): lax.ppermute(tail_rows, 'seq', [(i, i + 1) for i in range(count - 1)])  3.68 us
    ppermute x12, waiting for transfers between devices, exchange(): return lax.ppermute(block, 'seq', [(i, i ^ bits) for i in range(count)])  2.38 us
  transfers between devices with their start and end apart: 17, of which 3 were waited for; matrix products, arithmetic and copies ran while one was open for 0% of the time, Pallas kernels for 27%

profile of v4, /device:TPU:25, one launch (start us, length us, event | category | flops | bytes accessed | tf_op | source)
XLA Modules:
  0.0 67.0 jit_solution(9741690521594021881)
XLA Ops:
  0.0 1.1 %tail.1 = bf16[3,8192]{1,0:T(4,128)(2,1)S(1)} custom-call(s32[1,128]{1,0:T(1,128)} %bitcast.1, bf16[128,8192]{1,0:T(8,128)(2,1)} %x_ref.1), custom_call_target="tpu_custom_call" | custom-call | flops 100000 | bytes 1000000 | tf_op jit(solution)/shard_map/tail/pallas_call | solution.py:59
  1.1 3.7 %collective-permute-start = (bf16[3,8192]{1,0:T(4,128)(2,1)S(1)}, bf16[3,8192]{1,0:T(4,128)(2,1)S(1)}, u32[]{:S(2)}, u32[]{:S(2)}) collective-permute-start(bf16[3,8192]{1,0:T(4,128)(2,1)S(1)} %tail.1), channel_id=1, source_target_pairs={{0,1},{1,2},{2,3},{3,4},{4,5},{5,6},{6,7},{7,8},{8,9},{9,10},{10,1... | collective-permute-start | bytes 147464 | tf_op jit(solution)/shard_map/ppermute | solution.py:779
  4.9 1.7 %stage.1 = (bf16[128,8192]{1,0:T(8,128)(2,1)S(1)}, bf16[4,8192]{1,0:T(4,128)(2,1)S(1)}, f32[8,16,128]{2,1,0:T(8,128)S(1)}, bf16[8,128,128]{2,1,0:T(8,128)(2,1)S(1)}, f32[6,128,128]{2,1,0:T(8,128)S(1)}) custom-call(f32[32,128]{1,0:T(8,128)} %decay_hbm.1, f32[32,128]{1,0:T(8,128)} %beta_hbm.1, s32[1,128]{1,0:T(1,128)} %bitcast.2, bf16[128,8192]{1,0:T(8,128)(2,1)} %x_ref.1, ...), custom_call_target="tpu_custom_call" | custom-call | flops 10000000 | bytes 4194304 | tf_op jit(solution)/shard_map/stage/pallas_call | solution.py:184
  6.6 0.0 collective-permute-done.halo_ref.hq_ref
  6.6 7.5 %send_maps.1 = (bf16[4,528,256]{2,1,0:T(8,128)(2,1)S(1)}, bf16[4,256,128]{2,1,0:T(8,128)(2,1)S(1)}, bf16[4,512,256]{2,1,0:T(8,128)(2,1)S(1)}, bf16[8,128,128]{2,...) custom-call(s32[8]{0:T(128)S(1)} %compare_select_fusion.4.meta, ...), custom_call_target="tpu_custom_call" | custom-call | flops 1342177280 | bytes 5242880 | tf_op jit(solution)/shard_map/send_maps/pallas_call | solution.py:414
  14.1 2.7 %collective-permute-start.1 = (bf16[4,528,256]{2,1,0:T(8,128)(2,1)S(1)}, bf16[4,528,256]{2,1,0:T(8,128)(2,1)S(1)}, u32[]{:S(2)}, u32[]{:S(2)}) collective-permute-start(bf16[4,528,256]{2,1,0:T(8,128)(2,1)S(1)} %get-tuple-element.50), channel_id=1, source_target_pairs={{0,1},{1,0},{2,3},{3,2},{4,5},{5,4},{6,7},{7,6},{8,9},{9,8},{10,11... | collective-permute-start | bytes 3244040 | tf_op jit(solution)/shard_map/ppermute | solution.py:775
  16.8 6.0 %keep_maps.1 = (bf16[4,528,256]{2,1,0:T(8,128)(2,1)S(1)}, bf16[4,256,128]{2,1,0:T(8,128)(2,1)S(1)}, bf16[4,512,256]{2,1,0:T(8,128)(2,1)S(1)}) custom-call(s32[8]{0:T(128)S(1)} %compare_select_fusion.4.meta, bf16[128,8192]{1,0:T(8,128)(2,1)S(1)} %get-tuple-element.41.x_ref.xq_ref, bf16[3,8192]{1,0:T(4,128)(2,1)S(1)} %collective-permute-done.halo_ref.hq_ref, ...), custom_call_target="tpu_custom_call" | custom-call | flops 1342177280 | bytes 5242880 | tf_op jit(solution)/shard_map/keep_maps/pallas_call | solution.py:432
  22.8 0.0 collective-permute-done.1.other_ref.left_ref
  22.8 1.1 %pair.2 = (bf16[528,256]{1,0:T(8,128)(2,1)S(1)}, bf16[528,256]{1,0:T(8,128)(2,1)S(1)}) custom-call(s32[8]{0:T(128)S(1)} %compare_select_fusion.4.meta, bf16[4,528,256]{2,1,0:T(8,128)(2,1)S(1)} %get-tuple-element.59.mine_ref, bf16[4,528,256]{2,1,0:T(8,128)(2,1)S(1)} %collective-permute-done.1.other_ref.left_ref), custom_call_target="tpu_custom_call" | custom-call | flops 67108864 | bytes 2097152 | tf_op jit(solution)/shard_map/pair/pallas_call | solution.py:557
  23.9 0.1 collective-permute-start.2
  23.9 0.9 %pair.3 = (bf16[528,256]{1,0:T(8,128)(2,1)S(1)}, bf16[528,256]{1,0:T(8,128)(2,1)S(1)}) custom-call(s32[8]{0:T(128)S(1)} %compare_select_fusion.4.meta, bf16[4,528,256]{2,1,0:T(8,128)(2,1)S(1)} %get-tuple-element.59.mine_ref, bf16[4,528,256]{2,1,0:T(8,128)(2,1)S(1)} %collective-permute-done.1.other_ref.left_ref), custom_call_target="tpu_custom_call" | custom-call | flops 67108864 | bytes 2097152 | tf_op jit(solution)/shard_map/pair/pallas_call | solution.py:557
  24.8 0.1 collective-permute-start.3
  24.9 0.6 collective-permute-start.4
  25.5 2.0 %collective-permute-start.5 = (bf16[528,256]{1,0:T(8,128)(2,1)S(1)}, bf16[528,256]{1,0:T(8,128)(2,1)S(1)}, u32[]{:S(2)}, u32[]{:S(2)}) collective-permute-start(bf16[528,256]{1,0:T(8,128)(2,1)S(1)} %get-tuple-element.67), channel_id=1, source_target_pairs={{0,6},{1,7},{2,4},{3,5},{4,2},{5,3},{6,0},{7,1},{8,14},{9,15},{10,... | collective-permute-start | bytes 811016 | tf_op jit(solution)/shard_map/ppermute | solution.py:775
  27.5 4.2 %reads.2 = (bf16[4,512,128]{2,1,0:T(8,128)(2,1)S(1)}, f32[4,512,128]{2,1,0:T(8,128)S(1)}) custom-call(s32[8]{0:T(128)S(1)} %compare_select_fusion.4.meta, bf16[128,8192]{1,0:T(8,128)(2,1)S(1)} %get-tuple-element.41.x_ref.xq_ref, bf16[3,8192]{1,0:T(4,128)(2,1)S(1)} %collective-permute-done.halo_ref.hq_ref, ...), custom_call_target="tpu_custom_call" | custom-call | flops 402653184 | bytes 5242880 | tf_op jit(solution)/shard_map/reads/pallas_call | solution.py:483
  31.8 0.0 collective-permute-done.2.left_ref
  31.8 4.2 %reads.3 = (bf16[4,512,128]{2,1,0:T(8,128)(2,1)S(1)}, f32[4,512,128]{2,1,0:T(8,128)S(1)}) custom-call(s32[8]{0:T(128)S(1)} %compare_select_fusion.4.meta, bf16[128,8192]{1,0:T(8,128)(2,1)S(1)} %get-tuple-element.41.x_ref.xq_ref, bf16[3,8192]{1,0:T(4,128)(2,1)S(1)} %collective-permute-done.halo_ref.hq_ref, ...), custom_call_target="tpu_custom_call" | custom-call | flops 402653184 | bytes 5242880 | tf_op jit(solution)/shard_map/reads/pallas_call | solution.py:483
  36.0 0.0 collective-permute-done.3.x1
  36.0 0.0 collective-permute-done.4.x2
  36.0 2.2 %collective-permute-done.5.x3 = bf16[528,256]{1,0:T(8,128)(2,1)S(1)} collective-permute-done((bf16[528,256]{1,0:T(8,128)(2,1)S(1)}, bf16[528,256]{1,0:T(8,128)(2,1)S(1)}, u32[]{:S(2)}, u32[]{:S(2)}) %collective-permute-start.5) | collective-permute-done | bytes 270368 | tf_op jit(solution)/shard_map/ppermute | solution.py:775
  38.3 1.1 %plane.1 = (bf16[4,528,256]{2,1,0:T(8,128)(2,1)S(1)}, bf16[528,256]{1,0:T(8,128)(2,1)S(1)}, bf16[512,128]{1,0:T(8,128)(2,1)S(1)}) custom-call(s32[8]{0:T(128)S(1)} %compare_select_fusion.4.meta, bf16[528,256]{1,0:T(8,128)(2,1)S(1)} %get-tuple-element.64.x0, bf16[528,256]{1,0:T(8,128)(2,1)S(1)} %collective-permute-done.3.x1, ...), custom_call_target="tpu_custom_call" | custom-call | flops 100663296 | bytes 2097152 | tf_op jit(solution)/shard_map/plane/pallas_call | solution.py:604
  39.5 1.3 %collective-permute-start.6 = (bf16[528,256]{1,0:T(8,128)(2,1)S(1)}, bf16[528,256]{1,0:T(8,128)(2,1)S(1)}, u32[]{:S(2)}, u32[]{:S(2)}) collective-permute-start(bf16[528,256]{1,0:T(8,128)(2,1)S(1)} %get-tuple-element.69.plane_ref), channel_id=1, source_target_pairs={{16,24},{17,25},{18,26},{19,27},{20,28},{21,29},{22,30},{23,31}} | collective-permute-start | bytes 811016 | tf_op jit(solution)/shard_map/ppermute | solution.py:681
  40.8 0.7 collective-permute-start.7
  41.4 0.0 collective-permute-done.7.state_ref.refs_0_
  41.4 0.2 hop.1
  41.6 0.7 collective-permute-start.9
  42.3 1.3 %collective-permute-start.8 = (bf16[512,128]{1,0:T(8,128)(2,1)S(1)}, bf16[512,128]{1,0:T(8,128)(2,1)S(1)}, u32[]{:S(2)}, u32[]{:S(2)}) collective-permute-start(bf16[512,128]{1,0:T(8,128)(2,1)S(1)} %hop.1), channel_id=1, source_target_pairs={{8,24},{9,25},{10,26},{11,27},{12,28},{13,29},{14,30},{15,31}} | collective-permute-start | bytes 393224 | tf_op jit(solution)/shard_map/ppermute | solution.py:681
  43.6 0.0 collective-permute-done.9.refs_1_
  43.6 7.6 %collective-permute-done.8.far_ref = bf16[512,128]{1,0:T(8,128)(2,1)S(1)} collective-permute-done((bf16[512,128]{1,0:T(8,128)(2,1)S(1)}, bf16[512,128]{1,0:T(8,128)(2,1)S(1)}, u32[]{:S(2)}, u32[]{:S(2)}) %collective-permute-start.8) | collective-permute-done | bytes 131104 | tf_op jit(solution)/shard_map/ppermute | solution.py:681
  51.2 0.0 collective-permute-done.6.before_ref
  51.2 1.4 %spread.1 = (bf16[512,128]{1,0:T(8,128)(2,1)S(1)}, bf16[512,128]{1,0:T(8,128)(2,1)S(1)}, bf16[512,128]{1,0:T(8,128)(2,1)S(1)}, bf16[512,128]{1,0:T(8,128)(2,1)S(1)}) custom-call(s32[8]{0:T(128)S(1)} %compare_select_fusion.4.meta, bf16[4,528,256]{2,1,0:T(8,128)(2,1)S(1)} %get-tuple-element.68.prefix_ref, ...), custom_call_target="tpu_custom_call" | custom-call | flops 83886080 | bytes 2097152 | tf_op jit(solution)/shard_map/spread/pallas_call | solution.py:665
  52.6 0.3 collective-permute-start.10
  53.0 1.1 %collective-permute-start.11 = (bf16[512,128]{1,0:T(8,128)(2,1)S(1)}, bf16[512,128]{1,0:T(8,128)(2,1)S(1)}, u32[]{:S(2)}, u32[]{:S(2)}) collective-permute-start(bf16[512,128]{1,0:T(8,128)(2,1)S(1)} %get-tuple-element.73), channel_id=1, source_target_pairs={{0,4},{1,5},{2,6},{3,7},{4,0},{5,1},{6,2},{7,3},{8,12},{9,13},{10,... | collective-permute-start | bytes 393224 | tf_op jit(solution)/shard_map/ppermute | solution.py:775
  54.1 1.3 %collective-permute-start.12 = (bf16[512,128]{1,0:T(8,128)(2,1)S(1)}, bf16[512,128]{1,0:T(8,128)(2,1)S(1)}, u32[]{:S(2)}, u32[]{:S(2)}) collective-permute-start(bf16[512,128]{1,0:T(8,128)(2,1)S(1)} %get-tuple-element.74), channel_id=1, source_target_pairs={{0,6},{1,7},{2,4},{3,5},{4,2},{5,3},{6,0},{7,1},{8,14},{9,15},{10,... | collective-permute-start | bytes 393224 | tf_op jit(solution)/shard_map/ppermute | solution.py:775
  55.4 4.2 %collective-permute-start.13 = (bf16[512,128]{1,0:T(8,128)(2,1)S(1)}, bf16[512,128]{1,0:T(8,128)(2,1)S(1)}, u32[]{:S(2)}, u32[]{:S(2)}) collective-permute-start(bf16[512,128]{1,0:T(8,128)(2,1)S(1)} %get-tuple-element.71.e0), channel_id=1, source_target_pairs={{0,1},{1,0},{2,3},{3,2},{4,5},{5,4},{6,7},{7,6},{8,9},{9,8},{10,11... | collective-permute-start | bytes 393224 | tf_op jit(solution)/shard_map/ppermute | solution.py:775
  59.6 0.0 collective-permute-done.10.e1
  59.6 1.5 %collective-permute-start.14 = (bf16[512,128]{1,0:T(8,128)(2,1)S(1)}, bf16[512,128]{1,0:T(8,128)(2,1)S(1)}, u32[]{:S(2)}, u32[]{:S(2)}) collective-permute-start(bf16[512,128]{1,0:T(8,128)(2,1)S(1)} %collective-permute-done.10.e1), channel_id=1, source_target_pairs={{0,1},{1,0},{2,3},{3,2},{4,5},{5,4},{6,7},{7,6},{8,9},{9,8},{10,11... | collective-permute-start | bytes 393224 | tf_op jit(solution)/shard_map/ppermute | solution.py:775
  61.1 0.0 collective-permute-done.11.e2
  61.1 1.6 %collective-permute-start.15 = (bf16[512,128]{1,0:T(8,128)(2,1)S(1)}, bf16[512,128]{1,0:T(8,128)(2,1)S(1)}, u32[]{:S(2)}, u32[]{:S(2)}) collective-permute-start(bf16[512,128]{1,0:T(8,128)(2,1)S(1)} %collective-permute-done.11.e2), channel_id=1, source_target_pairs={{0,1},{1,0},{2,3},{3,2},{4,5},{5,4},{6,7},{7,6},{8,9},{9,8},{10,11... | collective-permute-start | bytes 393224 | tf_op jit(solution)/shard_map/ppermute | solution.py:775
  62.6 0.0 collective-permute-done.12.e3
  62.6 1.5 %collective-permute-start.16 = (bf16[512,128]{1,0:T(8,128)(2,1)S(1)}, bf16[512,128]{1,0:T(8,128)(2,1)S(1)}, u32[]{:S(2)}, u32[]{:S(2)}) collective-permute-start(bf16[512,128]{1,0:T(8,128)(2,1)S(1)} %collective-permute-done.12.e3), channel_id=1, source_target_pairs={{0,1},{1,0},{2,3},{3,2},{4,5},{5,4},{6,7},{7,6},{8,9},{9,8},{10,11... | collective-permute-start | bytes 393224 | tf_op jit(solution)/shard_map/ppermute | solution.py:775
  64.2 0.8 %half.1.kept = bf16[4,128,512]{2,1,0:T(8,128)(2,1)S(1)} custom-call(s32[8]{0:T(128)S(1)} %compare_select_fusion.4.meta, bf16[4,512,128]{2,1,0:T(8,128)(2,1)S(1)} %get-tuple-element.62.r_ref, f32[4,512,128]{2,1,0:T(8,128)S(1)} %get-tuple-element.63.d_ref, bf16[512,128]{1,0:T(8,128)(2,1)S(1)} %get-tuple-element.71.e0, ...), custom_call_target="tpu_custom_call" | custom-call | flops 67108864 | bytes 3145728 | tf_op jit(solution)/shard_map/half/pallas_call | solution.py:715
  65.0 0.0 collective-permute-done.13.e0
  65.0 0.0 collective-permute-done.14.e1
  65.0 0.0 collective-permute-done.15.e2
  65.0 0.1 collective-permute-done.16.e3
  65.1 1.7 %emit.1 = bf16[128,4096]{1,0:T(8,128)(2,1)} custom-call(s32[8]{0:T(128)S(1)} %compare_select_fusion.4.meta, bf16[4,128,512]{2,1,0:T(8,128)(2,1)S(1)} %half.1.kept, bf16[4,512,128]{2,1,0:T(8,128)(2,1)S(1)} %get-tuple-element.75.r_ref, f32[4,512,128]{2,1,0:T(8,128)S(1)} %get-tuple-element.76.d_ref, bf16[512,128]{1,0:T(8,128)(2,1)S(1)} %collective-permute-done.13.e0, ...), custom_call_target="tpu_custom_call" | custom-call | flops 67108864 | bytes 3145728 | tf_op jit(solution)/shard_map/emit/pallas_call | solution.py:748
  (1 shorter events, 0.0 us)
Async XLA Ops:
  1.1 5.4 %collective-permute-start = (bf16[3,8192]{1,0:T(4,128)(2,1)S(1)}, bf16[3,8192]{1,0:T(4,128)(2,1)S(1)}, u32[]{:S(2)}, u32[]{:S(2)}) collective-permute-start(bf16[3,8192]{1,0:T(4,128)(2,1)S(1)} %tail.1), channel_id=1, source_target_pairs={{0,1},{1,2},{2,3},{3,4},{4,5},{5,6},{6,7},{7,8},{8,9},{9,10},{10,1... | collective-permute-start | bytes 147464 | tf_op jit(solution)/shard_map/ppermute | solution.py:779
  14.1 8.7 %collective-permute-start.1 = (bf16[4,528,256]{2,1,0:T(8,128)(2,1)S(1)}, bf16[4,528,256]{2,1,0:T(8,128)(2,1)S(1)}, u32[]{:S(2)}, u32[]{:S(2)}) collective-permute-start(bf16[4,528,256]{2,1,0:T(8,128)(2,1)S(1)} %get-tuple-element.50), channel_id=1, source_target_pairs={{0,1},{1,0},{2,3},{3,2},{4,5},{5,4},{6,7},{7,6},{8,9},{9,8},{10,11... | collective-permute-start | bytes 3244040 | tf_op jit(solution)/shard_map/ppermute | solution.py:775
  23.9 7.9 %collective-permute-start.2 = (bf16[4,528,256]{2,1,0:T(8,128)(2,1)S(1)}, bf16[4,528,256]{2,1,0:T(8,128)(2,1)S(1)}, u32[]{:S(2)}, u32[]{:S(2)}) collective-permute-start(bf16[4,528,256]{2,1,0:T(8,128)(2,1)S(1)} %get-tuple-element.59.mine_ref), channel_id=1, source_target_pairs={{0,1},{1,0},{2,3},{3,2},{4,5},{5,4},{6,7},{7,6},{8,9},{9,8},{10,11... | collective-permute-start | bytes 3244040 | tf_op jit(solution)/shard_map/ppermute | solution.py:775
  24.8 11.2 %collective-permute-start.3 = (bf16[528,256]{1,0:T(8,128)(2,1)S(1)}, bf16[528,256]{1,0:T(8,128)(2,1)S(1)}, u32[]{:S(2)}, u32[]{:S(2)}) collective-permute-start(bf16[528,256]{1,0:T(8,128)(2,1)S(1)} %get-tuple-element.65), channel_id=1, source_target_pairs={{0,2},{1,3},{2,0},{3,1},{4,6},{5,7},{6,4},{7,5},{8,10},{9,11},{10,... | collective-permute-start | bytes 811016 | tf_op jit(solution)/shard_map/ppermute | solution.py:775
  24.9 11.1 %collective-permute-start.4 = (bf16[528,256]{1,0:T(8,128)(2,1)S(1)}, bf16[528,256]{1,0:T(8,128)(2,1)S(1)}, u32[]{:S(2)}, u32[]{:S(2)}) collective-permute-start(bf16[528,256]{1,0:T(8,128)(2,1)S(1)} %get-tuple-element.66), channel_id=1, source_target_pairs={{0,4},{1,5},{2,6},{3,7},{4,0},{5,1},{6,2},{7,3},{8,12},{9,13},{10,... | collective-permute-start | bytes 811016 | tf_op jit(solution)/shard_map/ppermute | solution.py:775
  25.5 12.7 %collective-permute-start.5 = (bf16[528,256]{1,0:T(8,128)(2,1)S(1)}, bf16[528,256]{1,0:T(8,128)(2,1)S(1)}, u32[]{:S(2)}, u32[]{:S(2)}) collective-permute-start(bf16[528,256]{1,0:T(8,128)(2,1)S(1)} %get-tuple-element.67), channel_id=1, source_target_pairs={{0,6},{1,7},{2,4},{3,5},{4,2},{5,3},{6,0},{7,1},{8,14},{9,15},{10,... | collective-permute-start | bytes 811016 | tf_op jit(solution)/shard_map/ppermute | solution.py:775
  39.5 11.8 %collective-permute-start.6 = (bf16[528,256]{1,0:T(8,128)(2,1)S(1)}, bf16[528,256]{1,0:T(8,128)(2,1)S(1)}, u32[]{:S(2)}, u32[]{:S(2)}) collective-permute-start(bf16[528,256]{1,0:T(8,128)(2,1)S(1)} %get-tuple-element.69.plane_ref), channel_id=1, source_target_pairs={{16,24},{17,25},{18,26},{19,27},{20,28},{21,29},{22,30},{23,31}} | collective-permute-start | bytes 811016 | tf_op jit(solution)/shard_map/ppermute | solution.py:681
  40.8 0.7 %collective-permute-start.7 = (bf16[512,128]{1,0:T(8,128)(2,1)S(1)}, bf16[512,128]{1,0:T(8,128)(2,1)S(1)}, u32[]{:S(2)}, u32[]{:S(2)}) collective-permute-start(bf16[512,128]{1,0:T(8,128)(2,1)S(1)} %get-tuple-element.70), channel_id=1, source_target_pairs={{0,8},{1,9},{2,10},{3,11},{4,12},{5,13},{6,14},{7,15}} | collective-permute-start | bytes 393224 | tf_op jit(solution)/shard_map/ppermute | solution.py:681
  41.6 2.0 %collective-permute-start.9 = (bf16[512,128]{1,0:T(8,128)(2,1)S(1)}, bf16[512,128]{1,0:T(8,128)(2,1)S(1)}, u32[]{:S(2)}, u32[]{:S(2)}) collective-permute-start(bf16[512,128]{1,0:T(8,128)(2,1)S(1)} %hop.1), channel_id=1, source_target_pairs={{8,16},{9,17},{10,18},{11,19},{12,20},{13,21},{14,22},{15,23}} | collective-permute-start | bytes 393224 | tf_op jit(solution)/shard_map/ppermute | solution.py:681
  42.3 8.9 %collective-permute-start.8 = (bf16[512,128]{1,0:T(8,128)(2,1)S(1)}, bf16[512,128]{1,0:T(8,128)(2,1)S(1)}, u32[]{:S(2)}, u32[]{:S(2)}) collective-permute-start(bf16[512,128]{1,0:T(8,128)(2,1)S(1)} %hop.1), channel_id=1, source_target_pairs={{8,24},{9,25},{10,26},{11,27},{12,28},{13,29},{14,30},{15,31}} | collective-permute-start | bytes 393224 | tf_op jit(solution)/shard_map/ppermute | solution.py:681
  52.6 7.0 %collective-permute-start.10 = (bf16[512,128]{1,0:T(8,128)(2,1)S(1)}, bf16[512,128]{1,0:T(8,128)(2,1)S(1)}, u32[]{:S(2)}, u32[]{:S(2)}) collective-permute-start(bf16[512,128]{1,0:T(8,128)(2,1)S(1)} %get-tuple-element.72), channel_id=1, source_target_pairs={{0,2},{1,3},{2,0},{3,1},{4,6},{5,7},{6,4},{7,5},{8,10},{9,11},{10,... | collective-permute-start | bytes 393224 | tf_op jit(solution)/shard_map/ppermute | solution.py:775
  53.0 8.1 %collective-permute-start.11 = (bf16[512,128]{1,0:T(8,128)(2,1)S(1)}, bf16[512,128]{1,0:T(8,128)(2,1)S(1)}, u32[]{:S(2)}, u32[]{:S(2)}) collective-permute-start(bf16[512,128]{1,0:T(8,128)(2,1)S(1)} %get-tuple-element.73), channel_id=1, source_target_pairs={{0,4},{1,5},{2,6},{3,7},{4,0},{5,1},{6,2},{7,3},{8,12},{9,13},{10,... | collective-permute-start | bytes 393224 | tf_op jit(solution)/shard_map/ppermute | solution.py:775
  54.1 8.6 %collective-permute-start.12 = (bf16[512,128]{1,0:T(8,128)(2,1)S(1)}, bf16[512,128]{1,0:T(8,128)(2,1)S(1)}, u32[]{:S(2)}, u32[]{:S(2)}) collective-permute-start(bf16[512,128]{1,0:T(8,128)(2,1)S(1)} %get-tuple-element.74), channel_id=1, source_target_pairs={{0,6},{1,7},{2,4},{3,5},{4,2},{5,3},{6,0},{7,1},{8,14},{9,15},{10,... | collective-permute-start | bytes 393224 | tf_op jit(solution)/shard_map/ppermute | solution.py:775
  55.4 9.7 %collective-permute-start.13 = (bf16[512,128]{1,0:T(8,128)(2,1)S(1)}, bf16[512,128]{1,0:T(8,128)(2,1)S(1)}, u32[]{:S(2)}, u32[]{:S(2)}) collective-permute-start(bf16[512,128]{1,0:T(8,128)(2,1)S(1)} %get-tuple-element.71.e0), channel_id=1, source_target_pairs={{0,1},{1,0},{2,3},{3,2},{4,5},{5,4},{6,7},{7,6},{8,9},{9,8},{10,11... | collective-permute-start | bytes 393224 | tf_op jit(solution)/shard_map/ppermute | solution.py:775
  59.6 5.4 %collective-permute-start.14 = (bf16[512,128]{1,0:T(8,128)(2,1)S(1)}, bf16[512,128]{1,0:T(8,128)(2,1)S(1)}, u32[]{:S(2)}, u32[]{:S(2)}) collective-permute-start(bf16[512,128]{1,0:T(8,128)(2,1)S(1)} %collective-permute-done.10.e1), channel_id=1, source_target_pairs={{0,1},{1,0},{2,3},{3,2},{4,5},{5,4},{6,7},{7,6},{8,9},{9,8},{10,11... | collective-permute-start | bytes 393224 | tf_op jit(solution)/shard_map/ppermute | solution.py:775
  61.1 3.9 %collective-permute-start.15 = (bf16[512,128]{1,0:T(8,128)(2,1)S(1)}, bf16[512,128]{1,0:T(8,128)(2,1)S(1)}, u32[]{:S(2)}, u32[]{:S(2)}) collective-permute-start(bf16[512,128]{1,0:T(8,128)(2,1)S(1)} %collective-permute-done.11.e2), channel_id=1, source_target_pairs={{0,1},{1,0},{2,3},{3,2},{4,5},{5,4},{6,7},{7,6},{8,9},{9,8},{10,11... | collective-permute-start | bytes 393224 | tf_op jit(solution)/shard_map/ppermute | solution.py:775
  62.6 2.5 %collective-permute-start.16 = (bf16[512,128]{1,0:T(8,128)(2,1)S(1)}, bf16[512,128]{1,0:T(8,128)(2,1)S(1)}, u32[]{:S(2)}, u32[]{:S(2)}) collective-permute-start(bf16[512,128]{1,0:T(8,128)(2,1)S(1)} %collective-permute-done.12.e3), channel_id=1, source_target_pairs={{0,1},{1,0},{2,3},{3,2},{4,5},{5,4},{6,7},{7,6},{8,9},{9,8},{10,11... | collective-permute-start | bytes 393224 | tf_op jit(solution)/shard_map/ppermute | solution.py:775
